TPU v7x, 32 devices: a whole 2x2x4 slice. The times are simulated.
32 devices in a mesh: seq: 8 (over z, y), tensor: 4 (over x, core).
Axes of the slice: x: 2, y: 2, z: 4, core: 2. Of those that a mesh axis runs over, the one named last changes fastest.
Arguments:
- stream: bfloat16 [8192, 768], P('seq'), may hold values from -6 to 6
- cotangent: bfloat16 [8192, 768], P('seq'), may hold values from -6 to 6
- boundary: int32 [8192], P('seq'), may hold values from 0 to 1, as said below
- counts: int32 [2, 4], replicated, may hold values from 0 to 256, as said below
- attend_gain: float32 [768], replicated, may hold values from 0.25 to 1.75
- attend_input: bfloat16 [768, 3, 768], P(None, None, 'tensor'), may hold values from -0.21875 to 0.21875
- attend_output: bfloat16 [768, 768], P('tensor'), may hold values from -3.5 to 3.5
- byte_gain: float32 [768], replicated, may hold values from 0.25 to 1.75
- byte_up: bfloat16 [768, 3072], P(None, 'tensor'), may hold values from -0.21875 to 0.21875
- byte_down: bfloat16 [3072, 768], P('tensor'), may hold values from -0.109375 to 0.109375
- patch_gain: float32 [1536], replicated, may hold values from 0.25 to 1.75
- patch_input: bfloat16 [1536, 3, 1536], P(None, None, 'tensor'), may hold values from -0.15625 to 0.15625
- patch_output: bfloat16 [1536, 1536], P('tensor'), may hold values from -1.75 to 1.75
- dense_gain: float32 [1536], replicated, may hold values from 0.25 to 1.75
- dense_up: bfloat16 [1536, 6144], P(None, 'tensor'), may hold values from -0.15625 to 0.15625
- dense_down: bfloat16 [6144, 768], P('tensor'), may hold values from -0.078125 to 0.078125
Outputs:
- result: bfloat16 [8192, 768], P('seq')
- inflow: bfloat16 [8192, 768], P('seq')
- attendgain_grad: float32 [768], replicated
- attendinput_grad: float32 [768, 3, 768], P(None, None, 'tensor')
- attendoutput_grad: float32 [768, 768], P('tensor')
- bytegain_grad: float32 [768], replicated
- byteup_grad: float32 [768, 3072], P(None, 'tensor')
- bytedown_grad: float32 [3072, 768], P('tensor')
- patchgain_grad: float32 [1536], replicated
- patchinput_grad: float32 [1536, 3, 1536], P(None, None, 'tensor')
- patchoutput_grad: float32 [1536, 1536], P('tensor')
- densegain_grad: float32 [1536], replicated
- denseup_grad: float32 [1536, 6144], P(None, 'tensor')
- densedown_grad: float32 [6144, 768], P('tensor')
Inputs may be any that keep to these rules, and one draw needn't show every extreme that they name: `boundary`: the ones on the 1024 bytes of one device number at most 256, a number reached on some device in every draw. counts[i, j] is the number of ones of boundary on bytes (i * 4 + j) * 1024 to (i * 4 + j + 1) * 1024 - 1; all counts together sum to exactly 1024.
All inputs are finite; a program needn't handle non-finite values.
Results may differ from a plain program's by a relative error of at most 0.024.
Values may be sent and summed in bfloat16 or wider, within the bound.
A program may use at most 320 MiB of HBM per device.

v0:
```python
import jax
import jax.numpy as jnp
from jax import lax
from jax.sharding import PartitionSpec as P

HD = 64
WIN = 1536
DEV_ITEM = 4


EPSILON = 1e-06
NEGATIVE = -1e30
WIDE_TYPE = jnp.float32
NARROW_TYPE = jnp.bfloat16


def from_behind(value, axis, steps):
    count = lax.axis_size(axis)
    initial, last = (max(0, -steps), min(count, count - steps))
    return lax.ppermute(value, axis, [(source, source + steps) for source in range(initial, last)])


def rms_scale(values, scaling):
    return values * lax.rsqrt(jnp.mean(values * values, axis=-1, keepdims=True) + EPSILON) * scaling


def gelu_tanh(values):
    return jax.nn.gelu(values, approximate=True)


def norm_back(values, scaling, upstream):
    unused, pullback = jax.vjp(rms_scale, values, scaling)
    return pullback(upstream)


def gelu_back(values, upstream):
    unused, pullback = jax.vjp(gelu_tanh, values)
    return pullback(upstream)[0]


def product(left_side, right_side):
    return jnp.dot(left_side, right_side, preferred_element_type=WIDE_TYPE)


def times_transposed(left_side, right_side):
    return lax.dot_general(
        left_side, right_side, (((1,), (1,)), ((), ())), preferred_element_type=WIDE_TYPE
    )


def transposed_times(left_side, right_side):
    return lax.dot_general(
        left_side, right_side, (((0,), (0,)), ((), ())), preferred_element_type=WIDE_TYPE
    )


def byte_sum(pieces):
    return lax.psum(pieces, "tensor")


def patch_sum(pieces):
    return lax.psum(pieces.astype(jnp.bfloat16), "tensor").astype(jnp.float32)


def softmax_parts(scores):
    row_top = jnp.max(scores, axis=-1, keepdims=True)
    raised = jnp.exp(scores - row_top)
    row_total = jnp.sum(raised, axis=-1, keepdims=True)
    return (raised / row_total, (row_top + jnp.log(row_total))[..., 0])


def patch_scores(query_slab, key_slab, allowed, score_scale):
    scores = (
        jnp.einsum("iqhe,ikhe->ihqk", query_slab, key_slab, preferred_element_type=WIDE_TYPE)
        * score_scale
    )
    return jnp.where(allowed[:, None], scores, NEGATIVE)


def patch_back(query_slab, key_slab, value_slab, out_grad, log_total, allowed, score_scale):
    scores = patch_scores(query_slab, key_slab, allowed, score_scale)
    soft_weights = jnp.exp(scores - log_total[..., None])
    weight_grad = jnp.einsum(
        "iqhe,ikhe->ihqk", out_grad, value_slab, preferred_element_type=WIDE_TYPE
    )
    row_term = jnp.sum(soft_weights * weight_grad, axis=-1)
    score_grad = (soft_weights * (weight_grad - row_term[..., None])).astype(NARROW_TYPE)
    query_grad = (
        jnp.einsum("ihqk,ikhe->iqhe", score_grad, key_slab, preferred_element_type=WIDE_TYPE)
        * score_scale
    )
    key_grad = (
        jnp.einsum("ihqk,iqhe->ikhe", score_grad, query_slab, preferred_element_type=WIDE_TYPE)
        * score_scale
    )
    value_grad = jnp.einsum(
        "ihqk,iqhe->ikhe",
        soft_weights.astype(NARROW_TYPE),
        out_grad,
        preferred_element_type=WIDE_TYPE,
    )
    return (query_grad, key_grad, value_grad, row_term)


def on_device(
    stream,
    cotangent,
    boundary,
    counts,
    attend_gain,
    attend_input,
    attend_output,
    byte_gain,
    byte_up,
    byte_down,
    patch_gain,
    patch_input,
    patch_output,
    dense_gain,
    dense_up,
    dense_down,
):
    tok_rows = stream.shape[0]
    width = stream.shape[1]
    head_cols = attend_input.shape[2]
    local_heads = head_cols // HD
    big_width = patch_input.shape[0]
    patch_cols = patch_input.shape[2]
    patch_heads = patch_cols // HD
    item_count = counts.shape[0]
    seq_devices = lax.axis_size("seq")
    device = lax.axis_index("seq")
    score_scale = HD ** (-0.5)
    margin = WIN - 1
    capacity = tok_rows // 4
    owned_rows = capacity // 2
    slot_rows = -(-capacity // seq_devices)
    send_rows = seq_devices * slot_rows
    item_cap = DEV_ITEM * capacity
    total_rows = owned_rows * seq_devices
    query_slots = item_cap // seq_devices + 1
    block_rows = min(512, tok_rows)
    block_count = tok_rows // block_rows
    span_rows = block_rows + margin
    stream_value = stream.astype(WIDE_TYPE)
    normed = rms_scale(stream_value, attend_gain).astype(NARROW_TYPE)
    in_matrix = attend_input.reshape(width, 3 * head_cols)
    projected = product(normed, in_matrix).astype(NARROW_TYPE)
    queries = projected[:, :head_cols]
    key_value = projected[:, head_cols:]
    need_list = []
    for reach_step in range(1, -(-margin // tok_rows) + 1):
        need_list.append(min(tok_rows, margin - (reach_step - 1) * tok_rows))
    arrived_list = []
    for reach_step in range(1, len(need_list) + 1):
        need_rows = need_list[reach_step - 1]
        arrived_list.append(from_behind(key_value[tok_rows - need_rows :], "seq", reach_step))
    extended = jnp.concatenate(arrived_list[::-1] + [key_value], axis=0)

    def window_block(block_start):
        query_rows = lax.dynamic_slice_in_dim(queries, block_start, block_rows, 0).reshape(
            block_rows, local_heads, HD
        )
        pair_rows = lax.dynamic_slice_in_dim(extended, block_start, span_rows, 0)
        key_rows = pair_rows[:, :head_cols].reshape(span_rows, local_heads, HD)
        value_rows = pair_rows[:, head_cols:].reshape(span_rows, local_heads, HD)
        query_pos = device * tok_rows + block_start + jnp.arange(block_rows, dtype=jnp.int32)
        key_pos = device * tok_rows + block_start - margin + jnp.arange(span_rows, dtype=jnp.int32)
        distance = query_pos[:, None] - key_pos[None, :]
        allowed = (distance >= 0) & (distance < WIN) & (key_pos[None, :] >= 0)
        scores = (
            jnp.einsum("qhe,khe->hqk", query_rows, key_rows, preferred_element_type=WIDE_TYPE)
            * score_scale
        )
        return (query_rows, key_rows, value_rows, jnp.where(allowed[None], scores, NEGATIVE))

    def window_forward(block_start):
        query_rows, key_rows, value_rows, scores = window_block(block_start)
        soft_weights, log_total = softmax_parts(scores)
        mixed_rows = jnp.einsum(
            "hqk,khe->qhe",
            soft_weights.astype(NARROW_TYPE),
            value_rows,
            preferred_element_type=WIDE_TYPE,
        )
        return (mixed_rows.astype(NARROW_TYPE).reshape(block_rows, head_cols), log_total)

    starts = jnp.arange(block_count, dtype=jnp.int32) * block_rows
    mixed_blocks, log_blocks = lax.map(window_forward, starts)
    mixed_heads = mixed_blocks.reshape(tok_rows, head_cols)
    after_attend = stream_value + byte_sum(product(mixed_heads, attend_output))
    normed_two = rms_scale(after_attend, byte_gain).astype(NARROW_TYPE)
    gate_pre = product(normed_two, byte_up)
    activated = gelu_tanh(gate_pre).astype(NARROW_TYPE)
    after_feed = after_attend + byte_sum(product(activated, byte_down))
    feed_low = after_feed.astype(NARROW_TYPE)
    per_device = counts.reshape(-1)
    offsets = jnp.cumsum(per_device) - per_device
    item_begin = offsets.reshape(item_count, DEV_ITEM)[:, 0]
    item_end = item_begin + jnp.sum(counts, axis=1)
    rank_local = jnp.cumsum(boundary) - 1
    global_rank = offsets[device] + rank_local
    target = jnp.where(
        boundary == 1, global_rank % seq_devices * slot_rows + rank_local // seq_devices, -1
    )
    send_map = (jnp.arange(send_rows)[:, None] == target[None, :]).astype(NARROW_TYPE)
    first_rank = (device - offsets) % seq_devices
    within = first_rank[:, None] + jnp.arange(slot_rows)[None, :] * seq_devices
    compact = jnp.where(
        within < per_device[:, None], (offsets[:, None] + within) // seq_devices, -1
    ).reshape(-1)
    take_map = (jnp.arange(owned_rows)[:, None] == compact[None, :]).astype(NARROW_TYPE)
    rows_sent = (
        product(send_map, feed_low).astype(NARROW_TYPE).reshape(seq_devices, slot_rows, width)
    )
    sent_cotangent = (
        product(send_map, cotangent).astype(NARROW_TYPE).reshape(seq_devices, slot_rows, width)
    )
    rows_arrived, arrived_cotangent = (
        lax.all_to_all(rows_sent, "seq", split_axis=0, concat_axis=0, tiled=True),
        lax.all_to_all(sent_cotangent, "seq", split_axis=0, concat_axis=0, tiled=True),
    )
    rows_arrived = rows_arrived.reshape(send_rows, width)
    arrived_cotangent = arrived_cotangent.reshape(send_rows, width)
    patch_rows = jnp.concatenate(
        [product(take_map, rows_arrived), jnp.zeros((owned_rows, big_width - width), WIDE_TYPE)],
        axis=1,
    )
    normed_three = rms_scale(patch_rows, patch_gain).astype(NARROW_TYPE)
    patch_matrix = patch_input.reshape(big_width, 3 * patch_cols)
    patch_projected = product(normed_three, patch_matrix).astype(NARROW_TYPE)
    patch_queries = patch_projected[:, :patch_cols]
    patch_pairs = patch_projected[:, patch_cols:]
    key_table = lax.all_gather(patch_pairs[:, None, :], "seq", axis=1, tiled=True).reshape(
        total_rows, 2 * patch_cols
    )
    slot_low = (item_begin - device + seq_devices - 1) // seq_devices
    slot_high = (item_end - device + seq_devices - 1) // seq_devices
    query_slot = slot_low[:, None] + jnp.arange(query_slots)[None, :]
    query_ok = query_slot < slot_high[:, None]
    query_index = jnp.minimum(query_slot, owned_rows - 1)
    query_global = query_slot * seq_devices + device
    key_global = item_begin[:, None] + jnp.arange(item_cap)[None, :]
    key_ok = key_global < item_end[:, None]
    key_index = jnp.minimum(key_global, total_rows - 1)
    allowed_slab = key_ok[:, None, :] & (key_global[:, None, :] <= query_global[:, :, None])
    own_place = jnp.where(query_ok, query_slot, owned_rows).reshape(-1)
    query_slab = jnp.take(patch_queries, query_index, axis=0).reshape(
        item_count, query_slots, patch_heads, HD
    )
    pair_slab = jnp.take(key_table, key_index, axis=0)
    key_slab = pair_slab[..., :patch_cols].reshape(item_count, item_cap, patch_heads, HD)
    value_slab = pair_slab[..., patch_cols:].reshape(item_count, item_cap, patch_heads, HD)
    soft_slab, log_slab = softmax_parts(
        patch_scores(query_slab, key_slab, allowed_slab, score_scale)
    )
    mixed_slab = jnp.einsum(
        "ihqk,ikhe->iqhe",
        soft_slab.astype(NARROW_TYPE),
        value_slab,
        preferred_element_type=WIDE_TYPE,
    )
    mixed_slab = mixed_slab.astype(NARROW_TYPE).reshape(-1, patch_cols)
    mixed_patch = (
        jnp.zeros((owned_rows + 1, patch_cols), NARROW_TYPE)
        .at[own_place]
        .set(mixed_slab)[:owned_rows]
    )
    patch_branch = patch_sum(product(mixed_patch, patch_output))
    after_patch = patch_rows + patch_branch
    normed_four = rms_scale(after_patch, dense_gain).astype(NARROW_TYPE)
    dense_pre = product(normed_four, dense_up)
    dense_act = gelu_tanh(dense_pre).astype(NARROW_TYPE)
    dense_out = patch_sum(product(dense_act, dense_down))
    delta_rows = (patch_branch[:, :width] + dense_out).astype(NARROW_TYPE)
    back_rows = (
        transposed_times(take_map, delta_rows)
        .astype(NARROW_TYPE)
        .reshape(seq_devices, slot_rows, width)
    )
    returned_rows = lax.all_to_all(
        back_rows, "seq", split_axis=0, concat_axis=0, tiled=True
    ).reshape(send_rows, width)
    result = (after_feed + transposed_times(send_map, returned_rows)).astype(NARROW_TYPE)
    delta_grad = product(take_map, arrived_cotangent).astype(NARROW_TYPE)
    dense_act_grad = times_transposed(delta_grad, dense_down)
    dense_pre_grad = gelu_back(dense_pre, dense_act_grad).astype(NARROW_TYPE)
    densedown_grad = transposed_times(dense_act, delta_grad)
    denseup_grad = transposed_times(normed_four, dense_pre_grad)
    normed_four_grad = patch_sum(times_transposed(dense_pre_grad, dense_up))
    after_patch_grad, densegain_grad = norm_back(after_patch, dense_gain, normed_four_grad)
    padded_delta = jnp.pad(delta_grad.astype(WIDE_TYPE), ((0, 0), (0, big_width - width)))
    branch_grad = (after_patch_grad + padded_delta).astype(NARROW_TYPE)
    patchoutput_grad = transposed_times(mixed_patch, branch_grad)
    mixed_patch_grad = times_transposed(branch_grad, patch_output).astype(NARROW_TYPE)
    out_slab = jnp.take(mixed_patch_grad, query_index, axis=0).reshape(
        item_count, query_slots, patch_heads, HD
    )
    out_slab = jnp.where(query_ok[:, :, None, None], out_slab, 0)
    query_grad, key_grad, value_grad, row_term = patch_back(
        query_slab, key_slab, value_slab, out_slab, log_slab, allowed_slab, score_scale
    )
    query_grad_own = (
        jnp.zeros((owned_rows + 1, patch_cols), WIDE_TYPE)
        .at[own_place]
        .set(query_grad.reshape(-1, patch_cols))[:owned_rows]
    )
    pair_grad = jnp.concatenate(
        [
            key_grad.reshape(item_count, item_cap, patch_cols),
            value_grad.reshape(item_count, item_cap, patch_cols),
        ],
        axis=-1,
    )
    key_place = jnp.where(key_ok, key_global, total_rows).reshape(-1)
    table_grad = (
        jnp.zeros((total_rows + 1, 2 * patch_cols), WIDE_TYPE)
        .at[key_place]
        .add(pair_grad.reshape(-1, 2 * patch_cols))[:total_rows]
    )
    pair_grad_own = lax.psum_scatter(
        table_grad.reshape(owned_rows, seq_devices, 2 * patch_cols),
        "seq",
        scatter_dimension=1,
        tiled=True,
    ).reshape(owned_rows, 2 * patch_cols)
    projected_patch_grad = jnp.concatenate(
        [query_grad_own.astype(NARROW_TYPE), pair_grad_own.astype(NARROW_TYPE)], axis=1
    )
    patchinput_grad = transposed_times(normed_three, projected_patch_grad).reshape(
        big_width, 3, patch_cols
    )
    normed_three_grad = patch_sum(times_transposed(projected_patch_grad, patch_matrix))
    patch_norm_grad, patchgain_grad = norm_back(patch_rows, patch_gain, normed_three_grad)
    rows_grad = (after_patch_grad + patch_norm_grad)[:, :width].astype(NARROW_TYPE)
    back_grads = (
        transposed_times(take_map, rows_grad)
        .astype(NARROW_TYPE)
        .reshape(seq_devices, slot_rows, width)
    )
    returned_grads = lax.all_to_all(
        back_grads, "seq", split_axis=0, concat_axis=0, tiled=True
    ).reshape(send_rows, width)
    after_feed_grad = cotangent.astype(WIDE_TYPE) + transposed_times(send_map, returned_grads)
    feed_grad = after_feed_grad.astype(NARROW_TYPE)
    activated_grad = times_transposed(feed_grad, byte_down)
    gate_grad = gelu_back(gate_pre, activated_grad).astype(NARROW_TYPE)
    bytedown_grad = transposed_times(activated, feed_grad)
    byteup_grad = transposed_times(normed_two, gate_grad)
    normed_two_grad = byte_sum(times_transposed(gate_grad, byte_up))
    feed_norm_grad, bytegain_grad = norm_back(after_attend, byte_gain, normed_two_grad)
    after_attend_grad = after_feed_grad + feed_norm_grad
    attend_branch_grad = after_attend_grad.astype(NARROW_TYPE)
    attendoutput_grad = transposed_times(mixed_heads, attend_branch_grad)
    mixed_heads_grad = times_transposed(attend_branch_grad, attend_output).astype(NARROW_TYPE)

    def window_back(ext_grad, inputs):
        block_start, log_total = inputs
        query_rows, key_rows, value_rows, scores = window_block(block_start)
        out_rows = lax.dynamic_slice_in_dim(mixed_heads_grad, block_start, block_rows, 0).reshape(
            block_rows, local_heads, HD
        )
        soft_weights = jnp.exp(scores - log_total[..., None])
        weight_grad = jnp.einsum(
            "qhe,khe->hqk", out_rows, value_rows, preferred_element_type=WIDE_TYPE
        )
        row_sum = jnp.sum(soft_weights * weight_grad, axis=-1, keepdims=True)
        score_grad = (soft_weights * (weight_grad - row_sum)).astype(NARROW_TYPE)
        query_part = (
            jnp.einsum("hqk,khe->qhe", score_grad, key_rows, preferred_element_type=WIDE_TYPE)
            * score_scale
        )
        key_part = (
            jnp.einsum("hqk,qhe->khe", score_grad, query_rows, preferred_element_type=WIDE_TYPE)
            * score_scale
        )
        value_part = jnp.einsum(
            "hqk,qhe->khe",
            soft_weights.astype(NARROW_TYPE),
            out_rows,
            preferred_element_type=WIDE_TYPE,
        )
        pair_part = jnp.concatenate(
            [key_part.reshape(span_rows, head_cols), value_part.reshape(span_rows, head_cols)],
            axis=1,
        )
        current = lax.dynamic_slice_in_dim(ext_grad, block_start, span_rows, 0)
        ext_grad = lax.dynamic_update_slice_in_dim(ext_grad, current + pair_part, block_start, 0)
        return (ext_grad, query_part.reshape(block_rows, head_cols))

    ext_grad, query_blocks = lax.scan(
        window_back, jnp.zeros((tok_rows + margin, 2 * head_cols), WIDE_TYPE), (starts, log_blocks)
    )
    own_grad = ext_grad[margin:]
    begin_row = margin
    for reach_step in range(1, len(need_list) + 1):
        need_rows = need_list[reach_step - 1]
        begin_row = begin_row - need_rows
        returned_halo = from_behind(
            ext_grad[begin_row : begin_row + need_rows].astype(jnp.bfloat16), "seq", -reach_step
        ).astype(jnp.float32)
        own_grad = own_grad.at[tok_rows - need_rows :].add(returned_halo)
    projected_grad = jnp.concatenate(
        [
            query_blocks.reshape(tok_rows, head_cols).astype(NARROW_TYPE),
            own_grad.astype(NARROW_TYPE),
        ],
        axis=1,
    )
    attendinput_grad = transposed_times(normed, projected_grad).reshape(width, 3, head_cols)
    normed_grad = byte_sum(times_transposed(projected_grad, in_matrix))
    stream_norm_grad, attendgain_grad = norm_back(stream_value, attend_gain, normed_grad)
    inflow = (after_attend_grad + stream_norm_grad).astype(NARROW_TYPE)
    summed = (
        lax.psum_scatter(attendgain_grad, "seq", scatter_dimension=0, tiled=True),
        lax.psum_scatter(attendinput_grad, "seq", scatter_dimension=0, tiled=True),
        lax.psum_scatter(attendoutput_grad, "seq", scatter_dimension=0, tiled=True),
        lax.psum_scatter(bytegain_grad, "seq", scatter_dimension=0, tiled=True),
        lax.psum_scatter(byteup_grad, "seq", scatter_dimension=0, tiled=True),
        lax.psum_scatter(bytedown_grad, "seq", scatter_dimension=0, tiled=True),
        lax.psum_scatter(patchgain_grad, "seq", scatter_dimension=0, tiled=True),
        lax.psum_scatter(patchinput_grad, "seq", scatter_dimension=0, tiled=True),
        lax.psum_scatter(patchoutput_grad, "seq", scatter_dimension=0, tiled=True),
        lax.psum_scatter(densegain_grad, "seq", scatter_dimension=0, tiled=True),
        lax.psum_scatter(denseup_grad, "seq", scatter_dimension=0, tiled=True),
        lax.psum_scatter(densedown_grad, "seq", scatter_dimension=0, tiled=True),
    )
    complete = (
        lax.all_gather(summed[0].astype(jnp.bfloat16), "seq", axis=0, tiled=True).astype(
            jnp.float32
        ),
        lax.all_gather(summed[1].astype(jnp.bfloat16), "seq", axis=0, tiled=True).astype(
            jnp.float32
        ),
        lax.all_gather(summed[2].astype(jnp.bfloat16), "seq", axis=0, tiled=True).astype(
            jnp.float32
        ),
        lax.all_gather(summed[3].astype(jnp.bfloat16), "seq", axis=0, tiled=True).astype(
            jnp.float32
        ),
        lax.all_gather(summed[4].astype(jnp.bfloat16), "seq", axis=0, tiled=True).astype(
            jnp.float32
        ),
        lax.all_gather(summed[5].astype(jnp.bfloat16), "seq", axis=0, tiled=True).astype(
            jnp.float32
        ),
        lax.all_gather(summed[6].astype(jnp.bfloat16), "seq", axis=0, tiled=True).astype(
            jnp.float32
        ),
        lax.all_gather(summed[7].astype(jnp.bfloat16), "seq", axis=0, tiled=True).astype(
            jnp.float32
        ),
        lax.all_gather(summed[8].astype(jnp.bfloat16), "seq", axis=0, tiled=True).astype(
            jnp.float32
        ),
        lax.all_gather(summed[9].astype(jnp.bfloat16), "seq", axis=0, tiled=True).astype(
            jnp.float32
        ),
        lax.all_gather(summed[10].astype(jnp.bfloat16), "seq", axis=0, tiled=True).astype(
            jnp.float32
        ),
        lax.all_gather(summed[11].astype(jnp.bfloat16), "seq", axis=0, tiled=True).astype(
            jnp.float32
        ),
    )
    return (result, inflow) + tuple(complete)


def solution(mesh):
    in_specs = (
        P("seq", None),
        P("seq", None),
        P("seq"),
        P(),
        P(),
        P(None, None, "tensor"),
        P("tensor", None),
        P(),
        P(None, "tensor"),
        P("tensor", None),
        P(),
        P(None, None, "tensor"),
        P("tensor", None),
        P(),
        P(None, "tensor"),
        P("tensor", None),
    )
    out_specs = (
        P("seq", None),
        P("seq", None),
        P(),
        P(None, None, "tensor"),
        P("tensor", None),
        P(),
        P(None, "tensor"),
        P("tensor", None),
        P(),
        P(None, None, "tensor"),
        P("tensor", None),
        P(),
        P(None, "tensor"),
        P("tensor", None),
    )
    return jax.shard_map(
        on_device, mesh=mesh, in_specs=in_specs, out_specs=out_specs, check_vma=False
    )
```

profile of v0, /device:TPU:0, one launch (start us, length us, event | category | flops | bytes accessed | tf_op | source)
XLA Modules:
  0.0 1887.0 jit_solution(9041444131595190952)
XLA Ops:
  38.6 58.2 %while.31 = (s32[]{:T(128)}, bf16[2,512,192]{1,2,0:T(8,128)(2,1)S(1)}, f32[2,3,512]{2,1,0:T(4,128)S(1)}, s32[2]{0:T(128)}, bf16[2559,384]{0,1:T(8,128)(2,1)}, /*...) while((s32[]{:T(128)}, ...), condition=%wide.region_4.5_spmd, body=%wide.region_1.4_spmd.sunk | while | flops 847987200 | bytes 47898628 | solution.py:189
  100.6 78.7 %all-reduce.21.cloned.1.call-done = f32[1024,768]{1,0:T(8,128)} async-done(((f32[1024,768]{1,0:T(8,128)}), f32[1024,768]{1,0:T(8,128)}) %all-reduce.21.cloned.1.call-update) | async-done | bytes 3145744 | tf_op jit(solution)/shard_map/psum | solution.py:58
  193.6 64.4 %all-reduce.23.cloned.1.call-done = f32[1024,768]{1,0:T(8,128)} async-done(((f32[1024,768]{1,0:T(8,128)}), f32[1024,768]{1,0:T(8,128)}) %all-reduce.23.cloned.1.call-update) | async-done | bytes 3145744 | tf_op jit(solution)/shard_map/psum | solution.py:58
  304.5 31.2 %all-gather.21.cloned.1.call-done = bf16[128,6144]{1,0:T(8,128)(2,1)} async-done(((bf16[128,768]{1,0:T(8,128)(2,1)}), bf16[128,6144]{1,0:T(8,128)(2,1)}) %all-gather.21.cloned.1.call-update) | async-done | bytes 1572880 | tf_op jit(solution)/shard_map/all_gather | solution.py:234
  339.3 11.7 gather_fusion
  373.4 29.8 %all-reduce.25.cloned.1.call-done = bf16[128,1536]{1,0:T(8,128)(2,1)} async-done(((bf16[128,1536]{1,0:T(8,128)(2,1)}), bf16[128,1536]{1,0:T(8,128)(2,1)}) %all-reduce.25.cloned.1.call-update) | async-done | bytes 393232 | tf_op jit(solution)/shard_map/psum | solution.py:62
  414.9 32.7 %all-reduce.27.cloned.1.call-done = bf16[128,1536]{1,0:T(8,128)(2,1)} async-done(((bf16[128,1536]{1,0:T(8,128)(2,1)}), bf16[128,1536]{1,0:T(8,128)(2,1)}) %all-reduce.27.cloned.1.call-update) | async-done | bytes 393232 | tf_op jit(solution)/shard_map/psum | solution.py:62
  490.4 16.8 scatter_custom_fusion.2
  519.9 66.5 %reduce-scatter.12.cloned.1.call-done = f32[128,1,768]{2,0,1:T(8,128)} async-done(((f32[128,8,768]{2,0,1:T(8,128)}), f32[128,1,768]{2,0,1:T(8,128)}) %reduce-scatter.12.cloned.1.call-update) | async-done | bytes 393232 | tf_op jit(solution)/shard_map/reduce_scatter | solution.py:321
  593.0 31.0 %all-reduce.33.cloned.1.call-done = (bf16[128,1536]{1,0:T(8,128)(2,1)}, bf16[128,768]{1,0:T(8,128)(2,1)}) async-done(((bf16[128,1536]{1,0:T(8,128)(2,1)}, bf16[128,768]{1,0:T(8,128)(2,1)}), (bf16[128,1536]{1,0:T(8,128)(2,1)}, bf16[128,768]{1,0:T(8,128)(2,1)})) %all-reduce.33.cloned.1.call-update) | async-done | bytes 589840 | tf_op jit(solution)/shard_map/psum | solution.py:62
  626.3 24.0 %all_to_all.20 = bf16[8,32,768]{2,1,0:T(8,128)(2,1)S(1)} all-to-all(bf16[8,32,768]{2,1,0:T(8,128)(2,1)S(1)} %bitcast.267), channel_id=1, replica_groups=mesh['seq'=8,'tensor'=4] {'seq'}, dimensions={0} | all-to-all | bytes 786432 | tf_op jit(solution)/shard_map/all_to_all | solution.py:341
  702.0 68.3 %all-reduce.29.cloned.1.call-done = f32[1024,768]{1,0:T(8,128)} async-done(((f32[1024,768]{1,0:T(8,128)}), f32[1024,768]{1,0:T(8,128)}) %all-reduce.29.cloned.1.call-update) | async-done | bytes 3145744 | tf_op jit(solution)/shard_map/psum | solution.py:58
  780.7 97.0 %while.32 = (s32[]{:T(128)}, f32[2559,384]{0,1:T(8,128)}, bf16[2,512,192]{1,2,0:T(8,128)(2,1)}, s32[2]{0:T(128)}, bf16[1024,192]{0,1:T(8,128)(2,1)}, /*index=5*/...) while((s32[]{:T(128)}, f32[2559,384]{0,1:T(8,128)}, ...), condition=%wide.region_31.33_spmd, body=%wide.region_29.32_spmd.sunk | while | flops 2066852864 | bytes 160753520 | solution.py:391
  815.0 14.5 dynamic_update_slice.37
  863.6 14.0 dynamic_update_slice.37
  888.7 18.3 collective-permute-done.2
  909.2 19.2 %collective-permute-done.3 = bf16[511,384]{0,1:T(8,128)(2,1)S(1)} collective-permute-done((bf16[511,384]{0,1:T(8,128)(2,1)S(1)}, bf16[511,384]{0,1:T(8,128)(2,1)S(1)}, u32[]{:S(2)}, u32[]{:S(2)}) %collective-permute-start.3) | collective-permute-done | bytes 392480 | tf_op jit(solution)/shard_map/ppermute | solution.py:20
  956.8 71.1 %reduce-scatter.16.cloned.1.call-done = f32[96,768]{1,0:T(8,128)} async-done(((f32[768,768]{1,0:T(8,128)}), f32[96,768]{1,0:T(8,128)}) %reduce-scatter.16.cloned.1.call-update) | async-done | bytes 294928 | tf_op jit(solution)/shard_map/reduce_scatter | solution.py:419
  1029.6 130.3 %reduce-scatter.20.cloned.1.call-done = f32[192,3,384]{2,0,1:T(8,128)} async-done(((f32[1536,3,384]{2,0,1:T(8,128)}), f32[192,3,384]{2,0,1:T(8,128)}) %reduce-scatter.20.cloned.1.call-update) | async-done | bytes 884752 | tf_op jit(solution)/shard_map/reduce_scatter | solution.py:422
  1162.0 163.2 %reduce-scatter.24.cloned.1.call-done = f32[192,1536]{1,0:T(8,128)} async-done(((f32[1536,1536]{1,0:T(8,128)}), f32[192,1536]{1,0:T(8,128)}) %reduce-scatter.24.cloned.1.call-update) | async-done | bytes 1179664 | tf_op jit(solution)/shard_map/reduce_scatter | solution.py:425
  1337.1 33.1 %all-gather.15.cloned.1.call-done = bf16[384,1536]{1,0:T(8,128)(2,1)} async-done(((bf16[48,1536]{1,0:T(8,128)(2,1)}), bf16[384,1536]{1,0:T(8,128)(2,1)}) %all-gather.15.cloned.1.call-update) | async-done | bytes 1179664 | tf_op jit(solution)/shard_map/all_gather | solution.py:453
  1377.0 58.4 %reduce-scatter.14.cloned.1.call-done = f32[24,768]{1,0:T(8,128)} async-done(((f32[192,768]{1,0:T(8,128)}), f32[24,768]{1,0:T(8,128)}) %reduce-scatter.14.cloned.1.call-update) | async-done | bytes 73744 | tf_op jit(solution)/shard_map/reduce_scatter | solution.py:417
  1436.3 31.0 %all_gather.42 = bf16[192,768]{1,0:T(8,128)(2,1)S(1)} all-gather(bf16[24,768]{1,0:T(8,128)(2,1)S(1)} %convert_element_type.298), channel_id=1, replica_groups=mesh['seq'=8,'tensor'=4] {'seq'}, dimensions={0}, use_global_device_ids=true | all-gather | bytes 331776 | tf_op jit(solution)/shard_map/all_gather | solution.py:435
  1468.1 37.6 %all-reduce.31.cloned.1.call-done = f32[1024,768]{1,0:T(8,128)} async-done(((f32[1024,768]{1,0:T(8,128)}), f32[1024,768]{1,0:T(8,128)}) %all-reduce.31.cloned.1.call-update) | async-done | bytes 3145744 | tf_op jit(solution)/shard_map/psum | solution.py:58
  1509.2 37.3 %all-reduce.10 = (bf16[768]{0:T(1024)(128)(2,1)S(1)}, bf16[768]{0:T(1024)(128)(2,1)S(1)}, bf16[1536]{0:T(1024)(128)(2,1)S(1)}, bf16[1536]{0:T(1024)(128)(2,1)S(1)}) all-reduce(f32[768]{0:T(1024)S(1)} %get-tuple-element.275, f32[768]{0:T(1024)S(1)} %copy-done.72, ...), channel_id=4, replica_groups=mesh['seq'=8,'tensor'=4] {'seq'}, use_global_device_ids=true, to_apply=%region_35.37.clone | all-reduce | flops 4608 | bytes 27648
  1547.7 33.1 %all-reduce.11 = (bf16[768]{0:T(1024)(128)(2,1)S(1)}, bf16[768]{0:T(1024)(128)(2,1)S(1)}, bf16[1536]{0:T(1024)(128)(2,1)S(1)}, bf16[1536]{0:T(1024)(128)(2,1)S(1)}) all-reduce(bf16[768]{0:T(1024)(128)(2,1)S(1)} %dynamic-update-slice.5, bf16[768]{0:T(1024)(128)(2,1)S(1)} %dynamic-update-slice.6, ...), channel_id=1, replica_groups=mesh['seq'=8,'tensor'=4] {'seq'}, use_global_device_ids=true, to_apply=%add.2 | all-reduce | flops 4608 | bytes 18432
  1588.8 38.2 %all_gather.41 = bf16[768,3,192]{2,1,0:T(4,128)(2,1)S(1)} all-gather(bf16[96,3,192]{2,1,0:T(4,128)(2,1)S(1)} %copy.82), channel_id=1, replica_groups=mesh['seq'=8,'tensor'=4] {'seq'}, dimensions={0}, use_global_device_ids=true | all-gather | bytes 995328 | tf_op jit(solution)/shard_map/all_gather | solution.py:432
  1629.2 12.0 all-gather.19.cloned.1.call-done
  1645.4 38.9 %all-gather.11.cloned.1.call-done = bf16[768,768]{1,0:T(8,128)(2,1)} async-done(((bf16[96,768]{1,0:T(8,128)(2,1)}), bf16[768,768]{1,0:T(8,128)(2,1)}) %all-gather.11.cloned.1.call-update) | async-done | bytes 1179664 | tf_op jit(solution)/shard_map/all_gather | solution.py:444
  1687.2 39.2 %all-gather.9.cloned.1.call-done = bf16[768,768]{1,0:T(8,128)(2,1)} async-done(((bf16[96,768]{1,0:T(8,128)(2,1)}), bf16[768,768]{1,0:T(8,128)(2,1)}) %all-gather.9.cloned.1.call-update) | async-done | bytes 1179664 | tf_op jit(solution)/shard_map/all_gather | solution.py:441
  1729.2 62.7 %all-gather.13.cloned.1.call-done = bf16[1536,3,384]{2,0,1:T(8,128)(2,1)} async-done(((bf16[192,3,384]{2,0,1:T(8,128)(2,1)}), bf16[1536,3,384]{2,0,1:T(8,128)(2,1)}) %all-gather.13.cloned.1.call-update) | async-done | bytes 3538960 | tf_op jit(solution)/shard_map/all_gather | solution.py:450
  1797.3 75.4 %all-gather.17.cloned.1.call-done = bf16[1536,1536]{1,0:T(8,128)(2,1)} async-done(((bf16[192,1536]{1,0:T(8,128)(2,1)}), bf16[1536,1536]{1,0:T(8,128)(2,1)}) %all-gather.17.cloned.1.call-update) | async-done | bytes 4718608 | tf_op jit(solution)/shard_map/all_gather | solution.py:459
  (500 shorter events, 469.8 us)
Async XLA Ops:
  7.2 172.1 %all-reduce.21.cloned.1.call-start = ((), (), s32[]{:S(2)}) async-start(), calls=%async_computation.13 | async-start | bytes 6291456 | tf_op jit(solution)/shard_map/psum | solution.py:58
  12.7 21.7 %collective-permute-start.1 = (bf16[1024,384]{0,1:T(8,128)(2,1)S(1)}, bf16[1024,384]{0,1:T(8,128)(2,1)}, u32[]{:S(2)}, u32[]{:S(2)}) collective-permute-start(bf16[1024,384]{0,1:T(8,128)(2,1)S(1)} %slice.146), channel_id=1, source_target_pairs={{0,4},{4,8},{8,12},{12,16},{16,20},{20,24},{24,28},{1,5},{5,9},{9,... | collective-permute-start | bytes 2359304 | tf_op jit(solution)/shard_map/ppermute | solution.py:20
  19.5 11.0 collective-permute-start
  100.0 157.9 %all-reduce.23.cloned.1.call-start = ((), (), s32[]{:S(2)}) async-start(), calls=%async_computation.14 | async-start | bytes 6291456 | tf_op jit(solution)/shard_map/psum | solution.py:58
  264.2 17.0 all-to-all-start
  281.2 16.0 all-to-all-start.2
  285.5 50.2 %all-gather.21.cloned.1.call-start = ((), (), s32[]{:S(2)}) async-start(), calls=%async_computation.33 | async-start | bytes 1769472 | tf_op jit(solution)/shard_map/all_gather | solution.py:234
  290.4 112.7 %all-reduce.25.cloned.1.call-start = ((), (), s32[]{:S(2)}) async-start(), calls=%async_computation.15 | async-start | bytes 786432 | tf_op jit(solution)/shard_map/psum | solution.py:62
  371.6 76.0 %all-reduce.27.cloned.1.call-start = ((), (), s32[]{:S(2)}) async-start(), calls=%async_computation.16 | async-start | bytes 786432 | tf_op jit(solution)/shard_map/psum | solution.py:62
  414.6 171.8 %reduce-scatter.12.cloned.1.call-start = ((), (), s32[]{:S(2)}) async-start(), calls=%async_computation.17 | async-start | bytes 3538944 | tf_op jit(solution)/shard_map/reduce_scatter | solution.py:321
  512.0 112.0 %all-reduce.33.cloned.1.call-start = ((), (), s32[]{:S(2)}) async-start(), calls=%async_computation.35 | async-start | bytes 1179648 | tf_op jit(solution)/shard_map/psum | solution.py:62
  591.0 109.3 %reduce-scatter.22.cloned.1.call-start = ((), (), s32[]{:S(2)}) async-start(), calls=%async_computation.27 | async-start | bytes 2654208 | tf_op jit(solution)/shard_map/reduce_scatter | solution.py:423
  593.0 177.4 %all-reduce.29.cloned.1.call-start = ((), (), s32[]{:S(2)}) async-start(), calls=%async_computation.18 | async-start | bytes 6291456 | tf_op jit(solution)/shard_map/psum | solution.py:58
  658.4 287.8 %reduce-scatter.26.cloned.1.call-start = ((), (), s32[]{:S(2)}) async-start(), calls=%async_computation.31 | async-start | bytes 5308416 | tf_op jit(solution)/shard_map/reduce_scatter | solution.py:426
  662.6 292.5 %reduce-scatter.18.cloned.1.call-start = ((), (), s32[]{:S(2)}) async-start(), calls=%async_computation.23 | async-start | bytes 2654208 | tf_op jit(solution)/shard_map/reduce_scatter | solution.py:420
  669.6 358.3 %reduce-scatter.16.cloned.1.call-start = ((), (), s32[]{:S(2)}) async-start(), calls=%async_computation.21 | async-start | bytes 2654208 | tf_op jit(solution)/shard_map/reduce_scatter | solution.py:419
  674.1 485.8 %reduce-scatter.20.cloned.1.call-start = ((), (), s32[]{:S(2)}) async-start(), calls=%async_computation.25 | async-start | bytes 7962624 | tf_op jit(solution)/shard_map/reduce_scatter | solution.py:422
  687.4 637.8 %reduce-scatter.24.cloned.1.call-start = ((), (), s32[]{:S(2)}) async-start(), calls=%async_computation.29 | async-start | bytes 10616832 | tf_op jit(solution)/shard_map/reduce_scatter | solution.py:425
  694.4 675.8 %all-gather.15.cloned.1.call-start = ((), (), s32[]{:S(2)}) async-start(), calls=%async_computation.28 | async-start | bytes 1327104 | tf_op jit(solution)/shard_map/all_gather | solution.py:453
  702.0 733.4 %reduce-scatter.14.cloned.1.call-start = ((), (), s32[]{:S(2)}) async-start(), calls=%async_computation.20 | async-start | bytes 663552 | tf_op jit(solution)/shard_map/reduce_scatter | solution.py:417
  882.7 24.2 %collective-permute-start.2 = (bf16[1024,384]{0,1:T(8,128)(2,1)}, bf16[1024,384]{0,1:T(8,128)(2,1)}, u32[]{:S(2)}, u32[]{:S(2)}) collective-permute-start(bf16[1024,384]{0,1:T(8,128)(2,1)} %slice.159), channel_id=1, source_target_pairs={{4,0},{8,4},{12,8},{16,12},{20,16},{24,20},{28,24},{5,1},{9,5},{13... | collective-permute-start | bytes 2359304 | tf_op jit(solution)/shard_map/ppermute | solution.py:20
  885.5 620.2 %all-reduce.31.cloned.1.call-start = ((), (), s32[]{:S(2)}) async-start(), calls=%async_computation.19 | async-start | bytes 6291456 | tf_op jit(solution)/shard_map/psum | solution.py:58
  886.6 41.9 %collective-permute-start.3 = (bf16[511,384]{0,1:T(8,128)(2,1)S(1)}, bf16[511,384]{0,1:T(8,128)(2,1)S(1)}, u32[]{:S(2)}, u32[]{:S(2)}) collective-permute-start(bf16[511,384]{0,1:T(8,128)(2,1)S(1)} %slice.161), channel_id=1, source_target_pairs={{8,0},{12,4},{16,8},{20,12},{24,16},{28,20},{9,1},{13,5},{17,9},{2... | collective-permute-start | bytes 1177352 | tf_op jit(solution)/shard_map/ppermute | solution.py:20
  940.9 646.6 %reduce-scatter.28.cloned.1.call-start = ((), (), s32[]{:S(2)}) async-start(), calls=%async_computation.34 | async-start | bytes 2211840
  946.1 381.3 %copy-start.20 = (bf16[128,1536]{1,0:T(8,128)(2,1)S(1)}, bf16[128,1536]{1,0:T(8,128)(2,1)}, u32[]{:S(2)}) copy-start(bf16[128,1536]{1,0:T(8,128)(2,1)} %all-reduce.25.cloned.1.call-done) | copy-start | bytes 1179652
  946.1 695.1 %all-gather.19.cloned.1.call-start = ((), (), s32[]{:S(2)}) async-start(), calls=%async_computation.32 | async-start | bytes 2654208 | tf_op jit(solution)/shard_map/all_gather | solution.py:462
  948.1 379.4 %copy-start.68 = (s32[256]{0:T(256)S(1)}, s32[256]{0:T(256)}, u32[]{:S(2)}) copy-start(s32[256]{0:T(256)} %copy-done.66) | copy-start | bytes 3076
  948.1 736.3 %all-gather.11.cloned.1.call-start = ((), (), s32[]{:S(2)}) async-start(), calls=%async_computation.24 | async-start | bytes 1327104 | tf_op jit(solution)/shard_map/all_gather | solution.py:444
  956.7 769.7 %all-gather.9.cloned.1.call-start = ((), (), s32[]{:S(2)}) async-start(), calls=%async_computation.22 | async-start | bytes 1327104 | tf_op jit(solution)/shard_map/all_gather | solution.py:441
  1029.5 762.4 %all-gather.13.cloned.1.call-start = ((), (), s32[]{:S(2)}) async-start(), calls=%async_computation.26 | async-start | bytes 3981312 | tf_op jit(solution)/shard_map/all_gather | solution.py:450
  1161.9 710.8 %all-gather.17.cloned.1.call-start = ((), (), s32[]{:S(2)}) async-start(), calls=%async_computation.30 | async-start | bytes 5308416 | tf_op jit(solution)/shard_map/all_gather | solution.py:459
  1329.5 43.7 %all-to-all-start.1 = ((bf16[8,32,768]{2,1,0:T(8,128)(2,1)}), bf16[8,32,768]{2,1,0:T(8,128)(2,1)S(1)}, u32[]{:S(2)}, u32[]{:S(2)}) async-start(bf16[8,32,768]{2,1,0:T(8,128)(2,1)} %bitcast.265), calls=%async_computation.1 | async-start | bytes 786432 | tf_op jit(solution)/shard_map/all_to_all | solution.py:281
  (95 other events, 2504.2 us)
Sparse Core Ops, SparseCore 0:
  100.1 79.1 all-reduce.20
  189.4 68.5 all-reduce.22
  290.5 45.1 all-gather.20
  371.7 31.4 all-reduce.24
  414.7 32.8 all-reduce.26
  512.1 74.2 reduce-scatter.11
  591.1 32.8 all-reduce.32
  628.1 72.1 reduce-scatter.21
  702.7 67.6 all-reduce.28
  774.4 95.7 reduce-scatter.25
  874.3 80.7 reduce-scatter.17
  959.0 68.8 reduce-scatter.15
  1031.5 128.3 reduce-scatter.19
  1163.9 161.2 reduce-scatter.23
  1327.2 42.9 all-gather.14
  1373.9 61.4 reduce-scatter.13
  1438.2 67.4 all-reduce.30
  1509.6 68.1 reduce-scatter.27
  1580.6 60.6 all-gather.18
  1643.8 40.4 all-gather.10
  1686.6 39.7 all-gather.8
  1728.6 63.2 all-gather.12
  1794.7 78.0 all-gather.16
where the time goes:
time: 1900 us; the launch traced here: 1890 us
  waiting for transfers between devices  1190 us (63%)
  local copies, waits for them, and re-layouts  166 us (9%)
  matrix products  164 us (9%)
  blocking collectives  164 us (9%)
  other arithmetic  146 us (8%)
  starting transfers between devices  27.4 us (1%)
    psum x4, waiting for transfers between devices, byte_sum(): return lax.psum(pieces, 'tensor')  249 us
    reduce_scatter x1, waiting for transfers between devices, on_device(): lax.psum_scatter(denseup_grad, 'seq', scatter_dimension=0, tiled=True)  163 us
    reduce_scatter x1, waiting for transfers between devices, on_device(): lax.psum_scatter(patchinput_grad, 'seq', scatter_dimension=0, tiled=True)  130 us
    psum x3, waiting for transfers between devices, patch_sum(): return lax.psum(pieces.astype(jnp.bfloat16), 'tensor').astype(jnp.float32)  93.4 us
    all_gather x1, waiting for transfers between devices, on_device(): lax.all_gather(summed[10].astype(jnp.bfloat16), 'seq', axis=0, tiled=True)  75.4 us
    reduce_scatter x1, waiting for transfers between devices, on_device(): lax.psum_scatter(byteup_grad, 'seq', scatter_dimension=0, tiled=True)  71.1 us
    unnamed x2, blocking collectives  70.4 us
    reduce_scatter x1, waiting for transfers between devices, on_device(): lax.psum_scatter(table_grad.reshape(owned_rows, seq_devices, 2 * patch_co...  66.5 us
  transfers between devices with their start and end apart: 30, of which 26 were waited for; matrix products, arithmetic and copies ran while one was open for 14% of the time, Pallas kernels for 0%

commit v1 on v0

v1 whole, which is shorter than its diff:
```python
import functools

import jax
import jax.numpy as jnp
from jax import lax
from jax.experimental import pallas as pl
from jax.experimental.pallas import tpu as pltpu
from jax.sharding import PartitionSpec as P

HD = 64
WIN = 1536
DEV_ITEM = 4

EPSILON = 1e-06
NEGATIVE = -1e30
SCORE_SCALE = HD ** (-0.5)
WIDE_TYPE = jnp.float32
NARROW_TYPE = jnp.bfloat16
VMEM_BYTES = 48 << 20


def from_behind(value, axis, steps):
    count = lax.axis_size(axis)
    initial, last = (max(0, -steps), min(count, count - steps))
    return lax.ppermute(value, axis, [(source, source + steps) for source in range(initial, last)])


def rms_scale(values, scaling):
    return values * lax.rsqrt(jnp.mean(values * values, axis=-1, keepdims=True) + EPSILON) * scaling


def gelu_tanh(values):
    return jax.nn.gelu(values, approximate=True)


def norm_back(values, scaling, upstream):
    unused, pullback = jax.vjp(rms_scale, values, scaling)
    return pullback(upstream)


def gelu_back(values, upstream):
    unused, pullback = jax.vjp(gelu_tanh, values)
    return pullback(upstream)[0]


def contract(left_side, right_side, left_axis, right_axis):
    return lax.dot_general(
        left_side,
        right_side,
        (((left_axis,), (right_axis,)), ((), ())),
        preferred_element_type=WIDE_TYPE,
    )


def product(left_side, right_side):
    return contract(left_side, right_side, 1, 0)


def times_transposed(left_side, right_side):
    return contract(left_side, right_side, 1, 1)


def transposed_times(left_side, right_side):
    return contract(left_side, right_side, 0, 0)


def wide(values):
    return values.astype(WIDE_TYPE)


def narrow(values):
    return values.astype(NARROW_TYPE)


def tensor_sum(pieces):
    return lax.psum(narrow(pieces), "tensor")


def seq_gather(block):
    gathered = lax.all_gather(block, "seq", axis=0, tiled=True)
    return gathered


def allowed_pairs(low_row, first_key, span, first_query, query_rows):
    key_pos = first_key + lax.broadcasted_iota(jnp.int32, (span, query_rows), 0)
    query_pos = first_query + lax.broadcasted_iota(jnp.int32, (span, query_rows), 1)
    return (key_pos >= low_row) & (key_pos <= query_pos)


def forward_body(heads, query_rows, span, offset, low, queries, keys, values, mixed, log_total):
    block = pl.program_id(1)
    start = jnp.maximum(block * query_rows + query_rows + offset - span, 0)
    start = pl.multiple_of(start, 128)
    allowed = allowed_pairs(low[...], start, span, block * query_rows + offset, query_rows)
    rows = pl.ds(start, span)
    for head in range(heads):
        cols = slice(head * HD, (head + 1) * HD)
        scores = contract(keys[rows, cols], queries[:, cols] * SCORE_SCALE, 1, 1)
        scores = jnp.where(allowed, scores, NEGATIVE)
        top = jnp.max(scores, axis=0, keepdims=True)
        raised = jnp.exp(scores - top)
        total = jnp.sum(raised, axis=0, keepdims=True)
        weights = narrow(raised * (1.0 / total))
        mixed[:, cols] = narrow(contract(values[rows, cols], weights, 0, 0).T)
        log_total[0, head : head + 1, :] = top + jnp.log(total)


def backward_body(
    heads,
    query_rows,
    span,
    offset,
    low,
    log_total,
    queries,
    out_grads,
    keys,
    values,
    query_grads,
    key_grads,
    value_grads,
    key_sum,
    value_sum,
):
    block = pl.program_id(1)

    @pl.when(block == 0)
    def clear():
        key_sum[...] = jnp.zeros_like(key_sum)
        value_sum[...] = jnp.zeros_like(value_sum)

    start = jnp.maximum(block * query_rows + query_rows + offset - span, 0)
    start = pl.multiple_of(start, 128)
    allowed = allowed_pairs(low[...], start, span, block * query_rows + offset, query_rows)
    rows = pl.ds(start, span)
    for head in range(heads):
        cols = slice(head * HD, (head + 1) * HD)
        query = queries[:, cols] * SCORE_SCALE
        out_grad = out_grads[:, cols]
        key = keys[rows, cols]
        scores = contract(key, query, 1, 1)
        weights = jnp.where(allowed, jnp.exp(scores - log_total[0, head : head + 1, :]), 0.0)
        weight_grad = contract(values[rows, cols], out_grad, 1, 1)
        inner = jnp.sum(weights * weight_grad, axis=0, keepdims=True)
        score_grad = narrow(weights * (weight_grad - inner))
        query_grads[:, cols] = narrow(contract(key, score_grad, 0, 0).T * SCORE_SCALE)
        key_sum[rows, cols] += contract(score_grad, query, 1, 0)
        value_sum[rows, cols] += contract(narrow(weights), out_grad, 1, 0)

    @pl.when(block == pl.num_programs(1) - 1)
    def finish():
        key_grads[...] = narrow(key_sum[...])
        value_grads[...] = narrow(value_sum[...])


def attend_sizes(queries, keys, span, query_rows):
    rows, cols = queries.shape
    extent = keys.shape[0]
    group_cols = 128 if cols % 128 == 0 else cols
    groups = cols // group_cols
    heads = group_cols // HD
    low_spec = pl.BlockSpec((1, query_rows), lambda g, b: (0, b))
    row_spec = pl.BlockSpec((query_rows, group_cols), lambda g, b: (b, g))
    all_spec = pl.BlockSpec((extent, group_cols), lambda g, b: (0, g))
    log_spec = pl.BlockSpec((1, heads, query_rows), lambda g, b: (g, 0, b))
    args = (heads, query_rows, span, extent - rows)
    log_shape = jax.ShapeDtypeStruct((groups, heads, rows), WIDE_TYPE)
    grid = (groups, rows // query_rows)
    flops = 2 * rows * span * cols
    return args, grid, low_spec, row_spec, all_spec, log_spec, log_shape, group_cols, flops


def attend_forward(low, queries, keys, values, span, query_rows):
    args, grid, low_spec, row_spec, all_spec, log_spec, log_shape, unused, flops = attend_sizes(
        queries, keys, span, query_rows
    )
    return pl.pallas_call(
        functools.partial(forward_body, *args),
        grid=grid,
        in_specs=[low_spec, row_spec, all_spec, all_spec],
        out_specs=[row_spec, log_spec],
        out_shape=[jax.ShapeDtypeStruct(queries.shape, NARROW_TYPE), log_shape],
        compiler_params=pltpu.CompilerParams(vmem_limit_bytes=VMEM_BYTES),
        cost_estimate=pl.CostEstimate(
            flops=16 * flops, transcendentals=flops // 128, bytes_accessed=1 << 20
        ),
        name="attend_forward",
    )(low, queries, keys, values)


def attend_backward(low, log_total, queries, out_grads, keys, values, span, query_rows):
    args, grid, low_spec, row_spec, all_spec, log_spec, unused, group_cols, flops = attend_sizes(
        queries, keys, span, query_rows
    )
    key_shape = jax.ShapeDtypeStruct(keys.shape, NARROW_TYPE)
    return pl.pallas_call(
        functools.partial(backward_body, *args),
        grid=grid,
        in_specs=[low_spec, log_spec, row_spec, row_spec, all_spec, all_spec],
        out_specs=[row_spec, all_spec, all_spec],
        out_shape=[jax.ShapeDtypeStruct(queries.shape, NARROW_TYPE), key_shape, key_shape],
        scratch_shapes=[pltpu.VMEM((keys.shape[0], group_cols), WIDE_TYPE)] * 2,
        compiler_params=pltpu.CompilerParams(vmem_limit_bytes=VMEM_BYTES),
        cost_estimate=pl.CostEstimate(
            flops=20 * flops, transcendentals=flops // 128, bytes_accessed=1 << 20
        ),
        name="attend_backward",
    )(low, log_total, queries, out_grads, keys, values)


def in_blocks(function, rows, block_rows):
    if rows <= block_rows:
        return function(0)
    starts = jnp.arange(rows // block_rows, dtype=jnp.int32) * block_rows
    return lax.map(function, starts).reshape(rows, -1)


def on_device(
    stream,
    cotangent,
    boundary,
    counts,
    attend_gain,
    attend_input,
    attend_output,
    byte_gain,
    byte_up,
    byte_down,
    patch_gain,
    patch_input,
    patch_output,
    dense_gain,
    dense_up,
    dense_down,
):
    tok_rows, width = stream.shape
    head_cols = attend_input.shape[2]
    big_width = patch_input.shape[0]
    patch_cols = patch_input.shape[2]
    item_count = counts.shape[0]
    seq_devices = lax.axis_size("seq")
    device = lax.axis_index("seq")
    capacity = tok_rows // 4
    total_rows = seq_devices * capacity // 2
    owned_rows = total_rows // seq_devices
    item_cap = DEV_ITEM * capacity
    query_rows = min(256, tok_rows)

    per_device = counts.reshape(-1)
    ends = jnp.cumsum(per_device)
    offsets = ends - per_device
    item_begin = offsets.reshape(item_count, DEV_ITEM)[:, 0]
    my_first = offsets[device]
    rank_local = jnp.cumsum(boundary) - 1
    target = jnp.where(boundary == 1, rank_local, -1)
    send_map = narrow(jnp.arange(capacity)[:, None] == target[None, :])
    rank = jnp.arange(total_rows, dtype=jnp.int32)
    rank_device = jnp.sum(rank[:, None] >= ends[None, :], axis=1)
    rank_start = jnp.sum(
        jnp.where(rank_device[:, None] == jnp.arange(seq_devices)[None, :], offsets[None, :], 0),
        axis=1,
    )
    rank_slot = rank_device * capacity + rank - rank_start
    rank_low = jnp.max(
        jnp.where(rank[:, None] >= item_begin[None, :], item_begin[None, :], 0), axis=1
    )
    rank_low = rank_low[None, :].astype(jnp.int32)
    slot_rows = seq_devices * capacity

    def compact(slots):
        block_rows = min(1024, total_rows)

        def one_block(first_row):
            places = lax.dynamic_slice_in_dim(rank_slot, first_row, block_rows, 0)
            take_map = narrow(places[:, None] == jnp.arange(slot_rows)[None, :])
            return narrow(product(take_map, slots))

        return in_blocks(one_block, total_rows, block_rows)

    def my_slots(table):
        padded = jnp.pad(table, ((0, capacity), (0, 0)))
        return lax.dynamic_slice_in_dim(padded, my_first, capacity, 0)

    def my_block(table):
        return lax.dynamic_slice_in_dim(table, device * owned_rows, owned_rows, 0)

    with jax.named_scope("cotangent_rows"):
        delta_grad = compact(seq_gather(narrow(product(send_map, cotangent))))
        delta_own = my_block(delta_grad)

    with jax.named_scope("byte_attend"):
        stream_value = wide(stream)
        normed = narrow(rms_scale(stream_value, attend_gain))
        in_matrix = attend_input.reshape(width, 3 * head_cols)
        projected = narrow(product(normed, in_matrix))
        queries = projected[:, :head_cols]
        key_value = projected[:, head_cols:]
        need_list = []
        while sum(need_list) < WIN:
            need_list.append(min(tok_rows, WIN - sum(need_list)))
        arrived_list = []
        for step, need_rows in enumerate(need_list):
            arrived_list.append(from_behind(key_value[tok_rows - need_rows :], "seq", step + 1))
        extended = jnp.concatenate(arrived_list[::-1] + [key_value], axis=0)
        keys = extended[:, :head_cols]
        values = extended[:, head_cols:]
        window_low = jnp.maximum(
            jnp.arange(tok_rows, dtype=jnp.int32) + 1, WIN - device * tok_rows
        )[None, :]
        window_span = WIN + query_rows
        mixed_heads, window_log = attend_forward(
            window_low, queries, keys, values, window_span, query_rows
        )
        all_mixed = lax.all_gather(mixed_heads, "tensor", axis=1, tiled=True)
        all_output = lax.all_gather(attend_output, "tensor", axis=0, tiled=True)
        after_attend = stream_value + product(all_mixed, all_output)

    with jax.named_scope("byte_feed"):
        normed_two = narrow(rms_scale(after_attend, byte_gain))
        gate_pre = product(normed_two, byte_up)
        activated = narrow(gelu_tanh(gate_pre))
        feed_part = narrow(product(activated, byte_down))

    with jax.named_scope("patch_rows"):
        attend_high = narrow(after_attend)
        attend_rest = narrow(after_attend - wide(attend_high))
        rows_sum = wide(tensor_sum(product(send_map, feed_part)))
        rows_here = narrow(
            product(send_map, attend_high) + product(send_map, attend_rest) + rows_sum
        )
        byte_rows = compact(seq_gather(rows_here))

    wide_pad = ((0, 0), (0, big_width - width))
    with jax.named_scope("patch_attend"):
        normed_three = narrow(rms_scale(wide(jnp.pad(byte_rows, wide_pad)), patch_gain))
        patch_matrix = patch_input.reshape(big_width, 3 * patch_cols)
        patch_projected = narrow(product(normed_three, patch_matrix))
        patch_queries = patch_projected[:, :patch_cols]
        patch_keys = patch_projected[:, patch_cols : 2 * patch_cols]
        patch_values = patch_projected[:, 2 * patch_cols :]
        patch_query_rows = min(256, total_rows)
        patch_span = min(total_rows, item_cap + patch_query_rows)
        mixed_patch, patch_log = attend_forward(
            rank_low, patch_queries, patch_keys, patch_values, patch_span, patch_query_rows
        )
        branch_own = wide(tensor_sum(product(my_block(mixed_patch), patch_output)))

    with jax.named_scope("patch_dense"):
        own_rows = wide(jnp.pad(my_block(byte_rows), wide_pad))
        after_patch = own_rows + branch_own
        normed_four = narrow(rms_scale(after_patch, dense_gain))
        all_normed = seq_gather(normed_four)
        dense_pre = product(normed_four, dense_up)
        dense_pre_grad = narrow(gelu_back(dense_pre, times_transposed(delta_own, dense_down)))
        normed_four_grad = wide(tensor_sum(times_transposed(dense_pre_grad, dense_up)))
        after_patch_grad, densegain_grad = norm_back(after_patch, dense_gain, normed_four_grad)
        branch_grad_own = narrow(after_patch_grad + wide(jnp.pad(delta_own, wide_pad)))
        branch_grad = seq_gather(branch_grad_own)

    with jax.named_scope("dense_weights"):
        block_rows = min(1024, total_rows)

        def dense_block(first_row):
            some_normed = lax.dynamic_slice_in_dim(all_normed, first_row, block_rows, 0)
            some_delta = lax.dynamic_slice_in_dim(delta_grad, first_row, block_rows, 0)
            some_pre = product(some_normed, dense_up)
            some_act = narrow(gelu_tanh(some_pre))
            some_grad = narrow(gelu_back(some_pre, times_transposed(some_delta, dense_down)))
            return (
                some_act,
                transposed_times(some_act, some_delta),
                transposed_times(some_normed, some_grad),
            )

        if total_rows == block_rows:
            dense_act, densedown_grad, denseup_grad = dense_block(0)
        else:

            def dense_step(sums, first_row):
                some_act, down_part, up_part = dense_block(first_row)
                return (sums[0] + down_part, sums[1] + up_part), some_act

            starts = jnp.arange(total_rows // block_rows, dtype=jnp.int32) * block_rows
            initial = (jnp.zeros(dense_down.shape), jnp.zeros(dense_up.shape))
            (densedown_grad, denseup_grad), dense_act = lax.scan(dense_step, initial, starts)
            dense_act = dense_act.reshape(total_rows, -1)

    with jax.named_scope("result"):
        delta_part = product(my_slots(mixed_patch), patch_output[:, :width])
        delta_part = narrow(delta_part + product(my_slots(dense_act), dense_down))
        result_part = wide(feed_part) + transposed_times(send_map, delta_part)
        result = narrow(after_attend + wide(tensor_sum(result_part)))

    with jax.named_scope("patch_attend_back"):
        patchoutput_grad = transposed_times(mixed_patch, branch_grad)
        mixed_patch_grad = narrow(times_transposed(branch_grad, patch_output))
        patch_projected_grad = jnp.concatenate(
            attend_backward(
                rank_low,
                patch_log,
                patch_queries,
                mixed_patch_grad,
                patch_keys,
                patch_values,
                patch_span,
                patch_query_rows,
            ),
            axis=1,
        )
        patchinput_grad = transposed_times(normed_three, patch_projected_grad)
        patchinput_grad = patchinput_grad.reshape(big_width, 3, patch_cols)
        normed_three_grad = wide(
            tensor_sum(times_transposed(my_slots(patch_projected_grad), patch_matrix))
        )
        patch_norm_grad, patchgain_grad = norm_back(
            wide(jnp.pad(rows_here, wide_pad)), patch_gain, normed_three_grad
        )
        rows_grad = narrow(wide(my_slots(branch_grad[:, :width])) + patch_norm_grad[:, :width])

    with jax.named_scope("byte_feed_back"):
        feed_grad = narrow(
            jnp.where(
                boundary[:, None] == 1,
                transposed_times(send_map, rows_grad),
                wide(cotangent),
            )
        )
        activated_grad = times_transposed(feed_grad, byte_down)
        gate_grad = narrow(gelu_back(gate_pre, activated_grad))
        bytedown_grad = transposed_times(activated, feed_grad)
        byteup_grad = transposed_times(normed_two, gate_grad)
        normed_two_grad = wide(tensor_sum(times_transposed(gate_grad, byte_up)))
        feed_norm_grad, bytegain_grad = norm_back(after_attend, byte_gain, normed_two_grad)
        after_attend_grad = wide(feed_grad) + feed_norm_grad

    with jax.named_scope("byte_attend_back"):
        attend_branch_grad = narrow(after_attend_grad)
        attendoutput_grad = transposed_times(mixed_heads, attend_branch_grad)
        mixed_heads_grad = narrow(times_transposed(attend_branch_grad, attend_output))
        query_grad, key_grad, value_grad = attend_backward(
            window_low, window_log, queries, mixed_heads_grad, keys, values, window_span, query_rows
        )
        pair_grad = jnp.concatenate([key_grad, value_grad], axis=1)
        own_grad = wide(pair_grad[WIN:])
        begin_row = WIN
        for step, need_rows in enumerate(need_list):
            begin_row = begin_row - need_rows
            returned = from_behind(pair_grad[begin_row : begin_row + need_rows], "seq", -step - 1)
            own_grad = own_grad.at[tok_rows - need_rows :].add(wide(returned))
        projected_grad = jnp.concatenate([query_grad, narrow(own_grad)], axis=1)
        attendinput_grad = transposed_times(normed, projected_grad)
        normed_grad = wide(tensor_sum(times_transposed(projected_grad, in_matrix)))
        stream_norm_grad, attendgain_grad = norm_back(stream_value, attend_gain, normed_grad)
        inflow = narrow(after_attend_grad + stream_norm_grad)

    with jax.named_scope("weight_sums"):

        def seq_sum(pieces):
            part = lax.psum_scatter(narrow(pieces), "seq", scatter_dimension=0, tiled=True)
            return wide(lax.all_gather(part, "seq", axis=0, tiled=True))

        feed_sum = seq_sum(jnp.concatenate([byteup_grad, bytedown_grad], axis=1))
        hidden = byte_up.shape[1]
        byteup_grad = feed_sum[:, :hidden]
        bytedown_grad = feed_sum[:, hidden:]
        attend_sum = seq_sum(
            jnp.concatenate([attendinput_grad, attendoutput_grad.reshape(width, -1)], axis=1)
        )
        attendinput_grad = attend_sum[:, : 3 * head_cols].reshape(width, 3, head_cols)
        attendoutput_grad = attend_sum[:, 3 * head_cols :].reshape(head_cols, width)
        gains = jnp.concatenate([attendgain_grad, bytegain_grad, patchgain_grad, densegain_grad])
        gains = lax.psum(gains, "seq")
        attendgain_grad = gains[:width]
        bytegain_grad = gains[width : 2 * width]
        patchgain_grad = gains[2 * width : 2 * width + big_width]
        densegain_grad = gains[2 * width + big_width :]

    return (
        result,
        inflow,
        attendgain_grad,
        attendinput_grad,
        attendoutput_grad,
        bytegain_grad,
        byteup_grad,
        bytedown_grad,
        patchgain_grad,
        patchinput_grad,
        patchoutput_grad,
        densegain_grad,
        denseup_grad,
        densedown_grad,
    )


def solution(mesh):
    in_specs = (
        P("seq", None),
        P("seq", None),
        P("seq"),
        P(),
        P(),
        P(None, None, "tensor"),
        P("tensor", None),
        P(),
        P(None, "tensor"),
        P("tensor", None),
        P(),
        P(None, None, "tensor"),
        P("tensor", None),
        P(),
        P(None, "tensor"),
        P("tensor", None),
    )
    out_specs = (
        P("seq", None),
        P("seq", None),
        P(),
        P(None, None, "tensor"),
        P("tensor", None),
        P(),
        P(None, "tensor"),
        P("tensor", None),
        P(),
        P(None, None, "tensor"),
        P("tensor", None),
        P(),
        P(None, "tensor"),
        P("tensor", None),
    )
    return jax.shard_map(
        on_device, mesh=mesh, in_specs=in_specs, out_specs=out_specs, check_vma=False
    )
```

time: 1900 us -> 871 us (0.46)
  waiting for transfers between devices: 1190 us -> 452 us
  blocking collectives: 164 us -> 36.2 us
  other arithmetic: 146 us -> 42 us
  Pallas kernels: 0 us -> 92.8 us
  local copies, waits for them, and re-layouts: 166 us -> 73.4 us
  matrix products: 164 us -> 133 us
    reduce_scatter x8 -> x2, waiting for transfers between devices: 502 us -> 102 us  [seq_sum(): lax.psum_scatter(narrow(pieces), 'seq', scatter_dimension=0, tiled=True)]
    psum x7 -> x6, waiting for transfers between devices: 342 us -> 160 us  [tensor_sum(): return lax.psum(narrow(pieces), 'tensor')]
    all_gather x7 -> x8, waiting for transfers between devices: 293 us -> 155 us  [the longest x4 126 us: seq_gather(): gathered = lax.all_gather(block, 'seq', axis=0, tiled=True)]
    pallas_call x0 -> x4, Pallas kernels: none -> 92.8 us  [the longest x2 50.6 us: attend_backward(): pl.pallas_call(functools.partial(backward_body, *args), grid=grid, in_spe...]
    unnamed x2 -> x0, blocking collectives: 70.4 us -> none
    all_gather x2 -> x0, blocking collectives: 69.2 us -> none  [the longest x1 38.2 us: on_device(): lax.all_gather(summed[1].astype(jnp.bfloat16), 'seq', axis=0, tiled=True)]
    convert_element_type x25 -> x6, other arithmetic: 59.5 us -> 13.5 us  [the longest x5 12.2 us: narrow(): return values.astype(NARROW_TYPE)]
    psum x0 -> x1, blocking collectives: none -> 36.2 us  [on_device(): gains = lax.psum(gains, 'seq')]
  transfers between devices with their start and end apart: 30 -> 20, of which waited for: 26 -> 15; matrix products, arithmetic and copies ran while one was open for 14% -> 19% of each run, Pallas kernels for 0% -> 5%
where the time goes in v1:
time: 871 us; the launch traced here: 863 us
  waiting for transfers between devices  452 us (52%)
  matrix products  133 us (15%)
  Pallas kernels  92.8 us (11%)
  local copies, waits for them, and re-layouts  73.4 us (8%)
  other arithmetic  42 us (5%)
  blocking collectives  36.2 us (4%)
  between operations  18.8 us (2%)
  starting transfers between devices  14.2 us (2%)
    psum x6, waiting for transfers between devices, tensor_sum(): return lax.psum(narrow(pieces), 'tensor')  160 us
    dot_general x32, matrix products, contract(): lax.dot_general(left_side, right_side, (((left_axis,), (right_axis,)), ((...  133 us
    all_gather x4, waiting for transfers between devices, seq_gather(): gathered = lax.all_gather(block, 'seq', axis=0, tiled=True)  126 us
    reduce_scatter x2, waiting for transfers between devices, seq_sum(): lax.psum_scatter(narrow(pieces), 'seq', scatter_dimension=0, tiled=True)  102 us
    pallas_call x2, Pallas kernels, attend_backward(): pl.pallas_call(functools.partial(backward_body, *args), grid=grid, in_spe...  50.6 us
    unnamed x148, local copies, waits for them, and re-layouts  48.1 us
    pallas_call x2, Pallas kernels, attend_forward(): pl.pallas_call(functools.partial(forward_body, *args), grid=grid, in_spec...  42.2 us
    psum x1, blocking collectives, on_device(): gains = lax.psum(gains, 'seq')  36.2 us
  transfers between devices with their start and end apart: 20, of which 15 were waited for; matrix products, arithmetic and copies ran while one was open for 19% of the time, Pallas kernels for 5%

profile of v1, /device:TPU:0, one launch (start us, length us, event | category | flops | bytes accessed | tf_op | source)
XLA Modules:
  0.0 862.7 jit_solution(16051668813193499740)
XLA Ops:
  17.5 5.8 collective-permute-start.1
  28.1 6.1 collective-permute-done
  34.2 5.3 collective-permute-done.1
  41.9 17.3 %attend_forward.2 = (bf16[1024,192]{1,0:T(8,128)(2,1)S(1)}, f32[1,3,1024]{2,1,0:T(4,128)S(1)}) custom-call(s32[1,1024]{1,0:T(1,128)S(1)} %add_maximum_fusion.low, bf16[1024,192]{1,0:T(8,128)(2,1)S(1)} %slice.136.queries, bf16[2560,192]{1,0:T(8,128)(2,1)S(1)} %get-tuple-element.168.keys, bf16[2560,192]{1,0:T(8,128)(2,1)S(1)} %get-tuple-element.167.values), custom_call_target="tpu_custom_call" | custom-call | flops 11274289152 | bytes 1048576 | tf_op jit(solution)/shard_map/byte_attend/attend_forward/pallas_call | solution.py:177
  61.0 29.5 %all-gather.9.cloned.1.call-done = bf16[1024,768]{0,1:T(8,128)(2,1)} async-done(((bf16[1024,192]{0,1:T(8,128)(2,1)}), bf16[1024,768]{0,1:T(8,128)(2,1)}) %all-gather.9.cloned.1.call-update) | async-done | bytes 1572880 | tf_op jit(solution)/shard_map/byte_attend/all_gather | solution.py:314
  90.6 5.6 multiply_reduce_fusion
  110.3 26.7 %all-reduce.16.cloned.1.call-done = bf16[256,768]{1,0:T(8,128)(2,1)} async-done(((bf16[256,768]{1,0:T(8,128)(2,1)}), bf16[256,768]{1,0:T(8,128)(2,1)}) %all-reduce.16.cloned.1.call-update) | async-done | bytes 393232 | tf_op jit(solution)/shard_map/patch_rows/psum | solution.py:76
  143.8 6.0 copy.127
  150.2 17.0 %all-gather.17.cloned.1.call-done = bf16[2048,768]{1,0:T(8,128)(2,1)} async-done(((bf16[256,768]{1,0:T(8,128)(2,1)}), bf16[2048,768]{1,0:T(8,128)(2,1)}) %all-gather.17.cloned.1.call-update) | async-done | bytes 3145744 | tf_op jit(solution)/shard_map/cotangent_rows/all_gather | solution.py:80
  167.2 6.8 fusion.37
  174.0 53.9 %all-gather.13.cloned.1.call-done = bf16[2048,768]{1,0:T(8,128)(2,1)} async-done(((bf16[256,768]{1,0:T(8,128)(2,1)}), bf16[2048,768]{1,0:T(8,128)(2,1)}) %all-gather.13.cloned.1.call-update) | async-done | bytes 3145744 | tf_op jit(solution)/shard_map/patch_rows/all_gather | solution.py:80
  227.9 5.8 fusion.36
  239.0 24.9 %attend_forward.3 = (bf16[1024,384]{1,0:T(8,128)(2,1)S(1)}, f32[3,2,1024]{2,1,0:T(2,128)S(1)}) custom-call(s32[1,1024]{1,0:T(1,128)S(1)} %bitcast.53, bf16[1024,384]{1,0:T(8,128)(2,1)S(1)} %get-tuple-element.166.queries, bf16[1024,384]{1,0:T(8,128)(2,1)S(1)} %get-tuple-element.165.keys, bf16[1024,384]{1,0:T(8,128)(2,1)S(1)} %get-tuple-element.164.values), custom_call_target="tpu_custom_call" | custom-call | flops 12884901888 | bytes 1048576 | tf_op jit(solution)/shard_map/patch_attend/attend_forward/pallas_call | solution.py:177
  268.8 28.8 %all-reduce.18.cloned.1.call-done = bf16[128,1536]{1,0:T(8,128)(2,1)} async-done(((bf16[128,1536]{1,0:T(8,128)(2,1)}), bf16[128,1536]{1,0:T(8,128)(2,1)}) %all-reduce.18.cloned.1.call-update) | async-done | bytes 393232 | tf_op jit(solution)/shard_map/patch_attend/psum | solution.py:76
  304.9 5.9 convolution_convert_fusion.2
  310.9 32.9 %all-reduce.20.cloned.1.call-done = bf16[128,1536]{1,0:T(8,128)(2,1)} async-done(((bf16[128,1536]{1,0:T(8,128)(2,1)}), bf16[128,1536]{1,0:T(8,128)(2,1)}) %all-reduce.20.cloned.1.call-update) | async-done | bytes 393232 | tf_op jit(solution)/shard_map/patch_dense/psum | solution.py:76
  353.4 54.7 %all-gather.19.cloned.1.call-done = bf16[1024,1536]{1,0:T(8,128)(2,1)} async-done(((bf16[128,1536]{1,0:T(8,128)(2,1)}), bf16[1024,1536]{1,0:T(8,128)(2,1)}) %all-gather.19.cloned.1.call-update) | async-done | bytes 3145744 | tf_op jit(solution)/shard_map/patch_dense/all_gather | solution.py:80
  412.2 28.8 %attend_backward.2 = (bf16[1024,384]{1,0:T(8,128)(2,1)S(1)}, bf16[1024,384]{1,0:T(8,128)(2,1)S(1)}, bf16[1024,384]{1,0:T(8,128)(2,1)S(1)}) custom-call(s32[1,1024]{1,0:T(1,128)S(1)} %bitcast.54, f32[3,2,1024]{2,1,0:T(2,128)S(1)} %get-tuple-element.58.log_total, bf16[1024,384]{1,0:T(8,128)(2,1)S(1)} %copy-done.13, ...), custom_call_target="tpu_custom_call" | custom-call | flops 16106127360 | bytes 1048576 | tf_op jit(solution)/shard_map/patch_attend_back/attend_backward/pallas_call | solution.py:196
  450.1 29.8 %all-reduce.22.cloned.1.call-done = bf16[256,1536]{1,0:T(8,128)(2,1)} async-done(((bf16[256,1536]{1,0:T(8,128)(2,1)}), bf16[256,1536]{1,0:T(8,128)(2,1)}) %all-reduce.22.cloned.1.call-update) | async-done | bytes 786448 | tf_op jit(solution)/shard_map/patch_attend_back/psum | solution.py:76
  493.2 42.0 %all-reduce.24.cloned.1.call-done = bf16[1024,768]{0,1:T(8,128)(2,1)} async-done(((bf16[1024,768]{0,1:T(8,128)(2,1)}), bf16[1024,768]{0,1:T(8,128)(2,1)}) %all-reduce.24.cloned.1.call-update) | async-done | bytes 1572880 | tf_op jit(solution)/shard_map/byte_feed_back/psum | solution.py:76
  548.8 21.9 %attend_backward.3 = (bf16[1024,192]{1,0:T(8,128)(2,1)S(1)}, bf16[2560,192]{1,0:T(8,128)(2,1)S(1)}, bf16[2560,192]{1,0:T(8,128)(2,1)S(1)}) custom-call(s32[1,1024]{1,0:T(1,128)S(1)} %add_maximum_fusion.low, f32[1,3,1024]{2,1,0:T(4,128)S(1)} %get-tuple-element.62.log_total, bf16[1024,192]{1,0:T(8,128)(2,1)S(1)} %copy-done.15, ...), custom_call_target="tpu_custom_call" | custom-call | flops 14092861440 | bytes 1048576 | tf_op jit(solution)/shard_map/byte_attend_back/attend_backward/pallas_call | solution.py:196
  578.0 15.5 %collective-permute-done.2 = bf16[1024,384]{1,0:T(8,128)(2,1)} collective-permute-done((bf16[1024,384]{1,0:T(8,128)(2,1)}, bf16[1024,384]{1,0:T(8,128)(2,1)}, u32[]{:S(2)}, u32[]{:S(2)}) %collective-permute-start.2) | collective-permute-done | bytes 786464 | tf_op jit(solution)/shard_map/byte_attend_back/ppermute | solution.py:25
  595.3 7.5 collective-permute-done.3
  619.2 10.6 %multiply_convert_fusion = (bf16[1024,1536]{1,0:T(8,128)(2,1)S(1)}, f32[1024,1536]{1,0:T(8,128)}) fusion(bf16[1024,1536]{1,0:T(8,128)(2,1)} %all-gather.15.cloned.1.call-done, bf16[1536,1536]{1,0:T(8,128)(2,1)} %param.36), kind=kOutput, calls=%fused_computation.17 | convolution fusion | flops 4845993984 | bytes 17301504 | tf_op jit(solution)/shard_map/dense_weights/dot_general | solution.py:47
  641.5 29.2 %reduce-scatter.7.cloned.1.call-done = bf16[96,768]{1,0:T(8,128)(2,1)} async-done(((bf16[768,768]{1,0:T(8,128)(2,1)}), bf16[96,768]{1,0:T(8,128)(2,1)}) %reduce-scatter.7.cloned.1.call-update) | async-done | bytes 147472 | tf_op jit(solution)/shard_map/weight_sums/reduce_scatter | solution.py:459
  670.9 72.5 %reduce-scatter.9.cloned.1.call-done = bf16[96,1536]{1,0:T(8,128)(2,1)} async-done(((bf16[768,1536]{1,0:T(8,128)(2,1)}), bf16[96,1536]{1,0:T(8,128)(2,1)}) %reduce-scatter.9.cloned.1.call-update) | async-done | bytes 294928 | tf_op jit(solution)/shard_map/weight_sums/reduce_scatter | solution.py:459
  743.5 15.0 %fusion.34 = f32[1536,1536]{1,0:T(8,128)} fusion(bf16[1024,1536]{1,0:T(8,128)(2,1)} %all-gather.15.cloned.1.call-done, f32[1024,1536]{1,0:T(8,128)} %get-tuple-element.177, bf16[1024,768]{1,0:T(8,128)(2,1)} %fusion.37, bf16[1536,768]{1,0:T(8,128)(2,1)S(1)} %copy-done), kind=kOutput, calls=%fused_computation.62 | convolution fusion | flops 7279214592 | bytes 22806528 | tf_op jit(solution)/shard_map/dense_weights/dot_general | solution.py:47
  758.5 7.4 fusion.136
  765.9 6.6 fusion.40
  772.5 8.0 copy.141
  780.5 4.7 fusion.135
  802.3 36.2 %psum.63 = f32[4608]{0:T(1024)S(1)} all-reduce(f32[4608]{0:T(1024)S(1)} %pad_maximum_fusion.7), channel_id=1, replica_groups=mesh['seq'=8,'tensor'=4] {'seq'}, use_global_device_ids=true, to_apply=%region_26.27 | all-reduce | flops 4608 | bytes 36864 | tf_op jit(solution)/shard_map/weight_sums/psum | solution.py:472
  (281 shorter events, 175.2 us)
Async XLA Ops:
  8.0 296.9 %copy-start = (bf16[1536,768]{1,0:T(8,128)(2,1)S(1)}, bf16[1536,768]{1,0:T(8,128)(2,1)}, u32[]{:S(2)}) copy-start(bf16[1536,768]{1,0:T(8,128)(2,1)} %param.37) | copy-start | bytes 7077892
  8.1 53.0 %all-gather.11.cloned.1.call-start = ((), (), s32[]{:S(2)}) async-start(), calls=%async_computation.3 | async-start | bytes 1474560 | tf_op jit(solution)/shard_map/byte_attend/all_gather | solution.py:315
  17.5 22.0 %collective-permute-start.1 = (bf16[1024,384]{1,0:T(8,128)(2,1)}, bf16[1024,384]{1,0:T(8,128)(2,1)}, u32[]{:S(2)}, u32[]{:S(2)}) collective-permute-start(bf16[1024,384]{1,0:T(8,128)(2,1)} %slice.138), channel_id=1, source_target_pairs={{0,4},{4,8},{8,12},{12,16},{16,20},{20,24},{24,28},{1,5},{5,9},{9,... | collective-permute-start | bytes 2359304 | tf_op jit(solution)/shard_map/byte_attend/ppermute | solution.py:25
  23.5 10.7 %collective-permute-start = (bf16[512,384]{1,0:T(8,128)(2,1)S(1)}, bf16[512,384]{1,0:T(8,128)(2,1)}, u32[]{:S(2)}, u32[]{:S(2)}) collective-permute-start(bf16[512,384]{1,0:T(8,128)(2,1)S(1)} %slice.137), channel_id=1, source_target_pairs={{0,8},{4,12},{8,16},{12,20},{16,24},{20,28},{1,9},{5,13},{9,17},{1... | collective-permute-start | bytes 1179656 | tf_op jit(solution)/shard_map/byte_attend/ppermute | solution.py:25
  26.9 63.6 %all-gather.9.cloned.1.call-start = ((), (), s32[]{:S(2)}) async-start(), calls=%async_computation.2 | async-start | bytes 1966080 | tf_op jit(solution)/shard_map/byte_attend/all_gather | solution.py:314
  41.8 18.6 %copy-start.53 = (s32[1024]{0:T(1024)S(1)}, s32[1024]{0:T(1024)}, u32[]{:S(2)}) copy-start(s32[1024]{0:T(1024)} %param.24) | copy-start | bytes 12292
  60.2 76.8 %all-reduce.16.cloned.1.call-start = ((), (), s32[]{:S(2)}) async-start(), calls=%async_computation.4 | async-start | bytes 786432 | tf_op jit(solution)/shard_map/patch_rows/psum | solution.py:76
  61.0 35.1 %copy-start.49 = (f32[768]{0:T(1024)S(1)}, f32[768]{0:T(1024)}, u32[]{:S(2)}) copy-start(f32[768]{0:T(1024)} %param.29) | copy-start | bytes 9220
  104.0 63.2 %all-gather.17.cloned.1.call-start = ((), (), s32[]{:S(2)}) async-start(), calls=%async_computation.8 | async-start | bytes 3538944 | tf_op jit(solution)/shard_map/cotangent_rows/all_gather | solution.py:80
  106.8 121.0 %all-gather.13.cloned.1.call-start = ((), (), s32[]{:S(2)}) async-start(), calls=%async_computation.5 | async-start | bytes 3538944 | tf_op jit(solution)/shard_map/patch_rows/all_gather | solution.py:80
  110.3 31.8 %copy-start.58 = (s32[2,4]{1,0:T(2,128)S(1)}, s32[2,4]{1,0:T(2,128)}, u32[]{:S(2)}) copy-start(s32[2,4]{1,0:T(2,128)} %param.25) | copy-start | bytes 100
  141.7 155.9 %all-reduce.18.cloned.1.call-start = ((), (), s32[]{:S(2)}) async-start(), calls=%async_computation.6 | async-start | bytes 786432 | tf_op jit(solution)/shard_map/patch_attend/psum | solution.py:76
  174.0 60.1 %copy-start.54 = (f32[1536]{0:T(1024)S(1)}, f32[1536]{0:T(1024)}, u32[]{:S(2)}) copy-start(f32[1536]{0:T(1024)} %param.32) | copy-start | bytes 18436
  239.0 24.9 %copy-start.8 = (bf16[1024,384]{1,0:T(8,128)(2,1)}, bf16[1024,384]{1,0:T(8,128)(2,1)S(1)}, u32[]{:S(2)}) copy-start(bf16[1024,384]{1,0:T(8,128)(2,1)S(1)} %get-tuple-element.164.values) | copy-start | bytes 2359300
  239.0 24.9 %copy-start.10 = (bf16[1024,384]{1,0:T(8,128)(2,1)}, bf16[1024,384]{1,0:T(8,128)(2,1)S(1)}, u32[]{:S(2)}) copy-start(bf16[1024,384]{1,0:T(8,128)(2,1)S(1)} %get-tuple-element.165.keys) | copy-start | bytes 2359300
  239.0 24.9 %copy-start.12 = (bf16[1024,384]{1,0:T(8,128)(2,1)}, bf16[1024,384]{1,0:T(8,128)(2,1)S(1)}, u32[]{:S(2)}) copy-start(bf16[1024,384]{1,0:T(8,128)(2,1)S(1)} %get-tuple-element.166.queries) | copy-start | bytes 2359300
  239.0 25.8 %copy-start.36 = (bf16[384,1536]{1,0:T(8,128)(2,1)S(1)}, bf16[384,1536]{1,0:T(8,128)(2,1)}, u32[]{:S(2)}) copy-start(bf16[384,1536]{1,0:T(8,128)(2,1)} %param.34) | copy-start | bytes 3538948
  264.0 34.8 %copy-start.44 = (f32[1536]{0:T(1024)S(1)}, f32[1536]{0:T(1024)}, u32[]{:S(2)}) copy-start(f32[1536]{0:T(1024)} %param.35) | copy-start | bytes 18436
  266.0 77.8 %all-reduce.20.cloned.1.call-start = ((), (), s32[]{:S(2)}) async-start(), calls=%async_computation.9 | async-start | bytes 786432 | tf_op jit(solution)/shard_map/patch_dense/psum | solution.py:76
  268.8 32.0 %copy-start.32 = (bf16[128,768]{1,0:T(8,128)(2,1)}, bf16[128,768]{1,0:T(8,128)(2,1)S(1)}, u32[]{:S(2)}) copy-start(bf16[128,768]{1,0:T(8,128)(2,1)S(1)} %constant_dynamic-slice_fusion.1) | copy-start | bytes 589828
  304.9 38.9 %copy-start.29 = (bf16[128,1536]{1,0:T(8,128)(2,1)S(1)}, bf16[128,1536]{1,0:T(8,128)(2,1)}, u32[]{:S(2)}) copy-start(bf16[128,1536]{1,0:T(8,128)(2,1)} %all-reduce.18.cloned.1.call-done) | copy-start | bytes 1179652
  310.8 97.2 %all-gather.19.cloned.1.call-start = ((), (), s32[]{:S(2)}) async-start(), calls=%async_computation.10 | async-start | bytes 3538944 | tf_op jit(solution)/shard_map/patch_dense/all_gather | solution.py:80
  348.0 131.9 %all-reduce.22.cloned.1.call-start = ((), (), s32[]{:S(2)}) async-start(), calls=%async_computation.11 | async-start | bytes 1572864 | tf_op jit(solution)/shard_map/patch_attend_back/psum | solution.py:76
  446.0 89.2 %all-reduce.24.cloned.1.call-start = ((), (), s32[]{:S(2)}) async-start(), calls=%async_computation.12 | async-start | bytes 3145728 | tf_op jit(solution)/shard_map/byte_feed_back/psum | solution.py:76
  492.2 126.9 %all-gather.15.cloned.1.call-start = ((), (), s32[]{:S(2)}) async-start(), calls=%async_computation.7 | async-start | bytes 3538944 | tf_op jit(solution)/shard_map/patch_dense/all_gather | solution.py:80
  493.0 177.7 %reduce-scatter.7.cloned.1.call-start = ((), (), s32[]{:S(2)}) async-start(), calls=%async_computation.15 | async-start | bytes 1327104 | tf_op jit(solution)/shard_map/weight_sums/reduce_scatter | solution.py:459
  571.9 21.6 %collective-permute-start.2 = (bf16[1024,384]{1,0:T(8,128)(2,1)}, bf16[1024,384]{1,0:T(8,128)(2,1)}, u32[]{:S(2)}, u32[]{:S(2)}) collective-permute-start(bf16[1024,384]{1,0:T(8,128)(2,1)} %fusion.63), channel_id=1, source_target_pairs={{4,0},{8,4},{12,8},{16,12},{20,16},{24,20},{28,24},{5,1},{9,5},{13... | collective-permute-start | bytes 2359304 | tf_op jit(solution)/shard_map/byte_attend_back/ppermute | solution.py:25
  574.4 28.4 %collective-permute-start.3 = (bf16[512,384]{1,0:T(8,128)(2,1)}, bf16[512,384]{1,0:T(8,128)(2,1)}, u32[]{:S(2)}, u32[]{:S(2)}) collective-permute-start(bf16[512,384]{1,0:T(8,128)(2,1)} %pad_maximum_fusion.6), channel_id=1, source_target_pairs={{8,0},{12,4},{16,8},{20,12},{24,16},{28,20},{9,1},{13,5},{17,9},{2... | collective-permute-start | bytes 1179656 | tf_op jit(solution)/shard_map/byte_attend_back/ppermute | solution.py:25
  607.4 136.0 %reduce-scatter.9.cloned.1.call-start = ((), (), s32[]{:S(2)}) async-start(), calls=%async_computation.16 | async-start | bytes 2654208 | tf_op jit(solution)/shard_map/weight_sums/reduce_scatter | solution.py:459
  619.1 166.1 %all-reduce.26.cloned.1.call-start = ((), (), s32[]{:S(2)}) async-start(), calls=%async_computation.17 | async-start | bytes 6291456 | tf_op jit(solution)/shard_map/result/psum | solution.py:76
  641.4 198.3 %all-gather.21.cloned.1.call-start = ((), (), s32[]{:S(2)}) async-start(), calls=%async_computation.13 | async-start | bytes 1327104 | tf_op jit(solution)/shard_map/weight_sums/all_gather | solution.py:460
  670.7 180.2 %all-gather.23.cloned.1.call-start = ((), (), s32[]{:S(2)}) async-start(), calls=%async_computation.14 | async-start | bytes 2654208 | tf_op jit(solution)/shard_map/weight_sums/all_gather | solution.py:460
  (56 other events, 257.9 us)
Sparse Core Ops, SparseCore 0:
  27.0 15.9 all-gather.10
  60.3 30.1 all-gather.8
  104.1 32.8 all-reduce.15
  266.1 31.4 all-reduce.17
  311.0 32.7 all-reduce.19
  446.1 33.6 all-reduce.21
  492.4 42.8 all-reduce.23
  641.6 66.7 all-reduce.25
Sparse Core Ops, SparseCore 1:
  107.3 59.9 all-gather.16
  169.2 58.5 all-gather.12
  348.1 59.9 all-gather.18
  495.2 59.9 all-gather.14
  607.5 63.1 reduce-scatter.6
  674.8 68.6 reduce-scatter.8
  745.5 40.5 all-gather.20
  788.2 50.5 all-gather.22

commit v2 on v1

--- a/solution.py
+++ b/solution.py
@@ -17,6 +17,7 @@
 WIDE_TYPE = jnp.float32
 NARROW_TYPE = jnp.bfloat16
 VMEM_BYTES = 48 << 20
+MESH = pl.DeviceIdType.MESH
 
 
 def from_behind(value, axis, steps):
@@ -72,13 +73,299 @@
     return values.astype(NARROW_TYPE)
 
 
-def tensor_sum(pieces):
-    return lax.psum(narrow(pieces), "tensor")
-
-
-def seq_gather(block):
-    gathered = lax.all_gather(block, "seq", axis=0, tiled=True)
-    return gathered
+def meet(peers):
+    barrier = pltpu.get_barrier_semaphore()
+    for peer in peers:
+        pl.semaphore_signal(barrier, inc=1, device_id=peer, device_id_type=MESH)
+    pl.semaphore_wait(barrier, len(peers))
+
+
+def tensor_peers():
+    place = lax.axis_index("tensor")
+    pair = place + 1 - 2 * (place % 2)
+    across = (place + 2) % 4
+    return place, pair, across
+
+
+def remote(source, target, send_sem, recv_sem, peer):
+    return pltpu.make_async_remote_copy(
+        src_ref=source,
+        dst_ref=target,
+        send_sem=send_sem,
+        recv_sem=recv_sem,
+        device_id=peer,
+        device_id_type=MESH,
+    )
+
+
+def tensor_sum_body(
+    chunks, part, total, pair_got, mine, across_got, pair_send, pair_recv, far_send, far_recv,
+    out_send, out_recv,
+):
+    place, pair, across = tensor_peers()
+    pair_id = {"tensor": pair}
+    across_id = {"tensor": across}
+    meet((pair_id, across_id))
+    rows = part.shape[0] // 4
+    step = rows // chunks
+    pair_across = (pair + 2) % 4
+
+    def piece(quarter, chunk):
+        return pl.ds(pl.multiple_of(quarter * rows + chunk * step, 16), step)
+
+    copies = []
+    for slot, quarter in enumerate((pair_across, pair)):
+        for chunk in range(chunks):
+            copy = remote(
+                part.at[piece(quarter, chunk)],
+                pair_got.at[slot, pl.ds(chunk * step, step)],
+                pair_send.at[slot, chunk],
+                pair_recv.at[slot, chunk],
+                pair_id,
+            )
+            copy.start()
+            copies.append(copy)
+    far = []
+    for chunk in range(chunks):
+        copies[chunk].wait_recv()
+        here = pl.ds(chunk * step, step)
+        mine[here] = (
+            part[piece(across, chunk)].astype(WIDE_TYPE) + pair_got[0, here].astype(WIDE_TYPE)
+        ).astype(NARROW_TYPE)
+        copy = remote(
+            mine.at[here],
+            across_got.at[here],
+            far_send.at[chunk],
+            far_recv.at[chunk],
+            across_id,
+        )
+        copy.start()
+        far.append(copy)
+    out_copies = []
+    for chunk in range(chunks):
+        copies[chunks + chunk].wait_recv()
+        far[chunk].wait_recv()
+        here = pl.ds(chunk * step, step)
+        own = piece(place, chunk)
+        total[own] = (
+            part[own].astype(WIDE_TYPE)
+            + pair_got[1, here].astype(WIDE_TYPE)
+            + across_got[here].astype(WIDE_TYPE)
+        ).astype(NARROW_TYPE)
+        for kind, peer in ((0, across_id), (1, pair_id)):
+            copy = remote(
+                total.at[own],
+                total.at[own],
+                out_send.at[kind, chunk],
+                out_recv.at[kind, chunk],
+                peer,
+            )
+            copy.start()
+            out_copies.append(copy)
+    passed = []
+    for chunk in range(chunks):
+        out_copies[2 * chunk].wait_recv()
+        theirs = piece(across, chunk)
+        copy = remote(
+            total.at[theirs],
+            total.at[theirs],
+            out_send.at[2, chunk],
+            out_recv.at[2, chunk],
+            pair_id,
+        )
+        copy.start()
+        passed.append(copy)
+    for chunk in range(chunks):
+        out_copies[2 * chunk + 1].wait_recv()
+        passed[chunk].wait_recv()
+    for copy in copies + far + out_copies + passed:
+        copy.wait_send()
+
+
+def tensor_sum(part, collective_id, chunks):
+    rows, cols = part.shape
+    quarter = rows // 4
+    dma = pltpu.SemaphoreType.DMA
+    return pl.pallas_call(
+        functools.partial(tensor_sum_body, chunks),
+        in_specs=[pl.BlockSpec(memory_space=pltpu.VMEM)],
+        out_specs=pl.BlockSpec(memory_space=pltpu.VMEM),
+        out_shape=jax.ShapeDtypeStruct((rows, cols), NARROW_TYPE),
+        scratch_shapes=[
+            pltpu.VMEM((2, quarter, cols), NARROW_TYPE),
+            pltpu.VMEM((quarter, cols), NARROW_TYPE),
+            pltpu.VMEM((quarter, cols), NARROW_TYPE),
+            dma((2, chunks)), dma((2, chunks)), dma((chunks,)), dma((chunks,)),
+            dma((3, chunks)), dma((3, chunks)),
+        ],
+        compiler_params=pltpu.CompilerParams(
+            collective_id=collective_id, has_side_effects=True, vmem_limit_bytes=VMEM_BYTES
+        ),
+        name="tensor_sum",
+    )(part)
+
+
+def tensor_gather_body(chunks, block, out, local_sem, send_sem, recv_sem):
+    place, pair, across = tensor_peers()
+    pair_id = {"tensor": pair}
+    across_id = {"tensor": across}
+    meet((pair_id, across_id))
+    rows = block.shape[0]
+    step = rows // chunks
+
+    def piece(owner, chunk):
+        return pl.ds(pl.multiple_of(owner * rows + chunk * step, 16), step)
+
+    copies = []
+    for kind, peer in ((0, across_id), (1, pair_id)):
+        for chunk in range(chunks):
+            copy = remote(
+                block.at[pl.ds(chunk * step, step)],
+                out.at[piece(place, chunk)],
+                send_sem.at[kind, chunk],
+                recv_sem.at[kind, chunk],
+                peer,
+            )
+            copy.start()
+            copies.append(copy)
+    local = pltpu.make_async_copy(block, out.at[pl.ds(pl.multiple_of(place * rows, 16), rows)], local_sem)
+    local.start()
+    passed = []
+    for chunk in range(chunks):
+        copies[chunk].wait_recv()
+        copy = remote(
+            out.at[piece(across, chunk)],
+            out.at[piece(across, chunk)],
+            send_sem.at[2, chunk],
+            recv_sem.at[2, chunk],
+            pair_id,
+        )
+        copy.start()
+        passed.append(copy)
+    local.wait()
+    for chunk in range(chunks):
+        copies[chunks + chunk].wait_recv()
+        passed[chunk].wait_recv()
+    for copy in copies + passed:
+        copy.wait_send()
+
+
+def tensor_gather(block, collective_id, chunks):
+    rows, cols = block.shape
+    dma = pltpu.SemaphoreType.DMA
+    return pl.pallas_call(
+        functools.partial(tensor_gather_body, chunks),
+        in_specs=[pl.BlockSpec(memory_space=pltpu.VMEM)],
+        out_specs=pl.BlockSpec(memory_space=pltpu.VMEM),
+        out_shape=jax.ShapeDtypeStruct((4*rows, cols), NARROW_TYPE),
+        scratch_shapes=[dma(()), dma((3, chunks)), dma((3, chunks))],
+        compiler_params=pltpu.CompilerParams(
+            collective_id=collective_id, has_side_effects=True, vmem_limit_bytes=VMEM_BYTES
+        ),
+        name="tensor_gather",
+    )(block)
+
+
+def ring_at(spot, count):
+    half = spot // (count // 2)
+    return (1 - half) * 2 * spot + half * (2 * (count - 1 - spot) + 1)
+
+
+def ring_spot(device, count):
+    return device // 2 + (device % 2) * (count - 1 - 2 * (device // 2))
+
+
+def seq_gather_body(count, block, out, local_sem, ring_send, ring_recv, pair_send, pair_recv):
+    device = lax.axis_index("seq")
+    place, pair, across = tensor_peers()
+    spot = ring_spot(device, count)
+    ahead = {"seq": ring_at((spot + 1) % count, count)}
+    behind = {"seq": ring_at((spot + count - 1) % count, count)}
+    pair_id = {"tensor": pair}
+    meet((ahead, behind, pair_id))
+    rows = block.shape[0]
+    step = rows // 4
+    core = place % 2
+
+    def piece(owner, sub):
+        return pl.ds(pl.multiple_of(owner * rows + core * 2 * step + sub * step, 16), step)
+
+    hops = count // 2
+    sends = []
+    moves = {}
+
+    def launch(way, hop, sub):
+        distance = hop - 1
+        if way == 0:
+            owner = ring_at((spot + count - distance) % count, count)
+        else:
+            owner = ring_at((spot + distance) % count, count)
+        if hop == 1:
+            source = block.at[pl.ds(pl.multiple_of(core * 2 * step + sub * step, 16), step)]
+        else:
+            source = out.at[piece(owner, sub)]
+        copy = remote(
+            source,
+            out.at[piece(owner, sub)],
+            ring_send.at[way, hop - 1, sub],
+            ring_recv.at[way, hop - 1, sub],
+            (ahead, behind)[way],
+        )
+        copy.start()
+        moves[way, hop, sub] = copy
+        sends.append(copy)
+
+    order = ((0, 0), (1, 1), (0, 1), (1, 0))
+    for way, sub in order:
+        launch(way, 1, sub)
+    local = pltpu.make_async_copy(
+        block, out.at[pl.ds(pl.multiple_of(device * rows, 16), rows)], local_sem
+    )
+    local.start()
+    pairs = []
+    for hop in range(1, hops + 1):
+        for way, sub in order:
+            if hop == hops and way != sub:
+                continue
+            moves[way, hop, sub].wait_recv()
+            if hop + 1 < hops or (hop + 1 == hops and way == sub):
+                launch(way, hop + 1, sub)
+            if way == 0:
+                owner = ring_at((spot + count - hop) % count, count)
+            else:
+                owner = ring_at((spot + hop) % count, count)
+            copy = remote(
+                out.at[piece(owner, sub)],
+                out.at[piece(owner, sub)],
+                pair_send.at[way, hop - 1, sub],
+                pair_recv.at[way, hop - 1, sub],
+                pair_id,
+            )
+            copy.start()
+            pairs.append(copy)
+    local.wait()
+    for copy in pairs:
+        copy.wait_recv()
+    for copy in sends + pairs:
+        copy.wait_send()
+
+
+def seq_gather(block, collective_id):
+    rows, cols = block.shape
+    count = lax.axis_size("seq")
+    dma = pltpu.SemaphoreType.DMA
+    sems = dma((2, count // 2, 2))
+    return pl.pallas_call(
+        functools.partial(seq_gather_body, count),
+        in_specs=[pl.BlockSpec(memory_space=pltpu.VMEM)],
+        out_specs=pl.BlockSpec(memory_space=pltpu.VMEM),
+        out_shape=jax.ShapeDtypeStruct((count*rows, cols), NARROW_TYPE),
+        scratch_shapes=[dma(()), sems, sems, sems, sems],
+        compiler_params=pltpu.CompilerParams(
+            collective_id=collective_id, has_side_effects=True, vmem_limit_bytes=VMEM_BYTES
+        ),
+        name="seq_gather",
+    )(block)
 
 
 def allowed_pairs(low_row, first_key, span, first_query, query_rows):
@@ -87,7 +374,9 @@
     return (key_pos >= low_row) & (key_pos <= query_pos)
 
 
-def forward_body(heads, query_rows, span, offset, low, queries, keys, values, mixed, log_total):
+def forward_body(
+    heads, query_rows, span, offset, upright, low, queries, keys, values, mixed, log_total
+):
     block = pl.program_id(1)
     start = jnp.maximum(block * query_rows + query_rows + offset - span, 0)
     start = pl.multiple_of(start, 128)
@@ -101,7 +390,11 @@
         raised = jnp.exp(scores - top)
         total = jnp.sum(raised, axis=0, keepdims=True)
         weights = narrow(raised * (1.0 / total))
-        mixed[:, cols] = narrow(contract(values[rows, cols], weights, 0, 0).T)
+        mixed_head = contract(values[rows, cols], weights, 0, 0)
+        if upright:
+            mixed[cols, :] = narrow(mixed_head)
+        else:
+            mixed[:, cols] = narrow(mixed_head.T)
         log_total[0, head : head + 1, :] = top + jnp.log(total)
 
 
@@ -170,16 +463,21 @@
     return args, grid, low_spec, row_spec, all_spec, log_spec, log_shape, group_cols, flops
 
 
-def attend_forward(low, queries, keys, values, span, query_rows):
+def attend_forward(low, queries, keys, values, span, query_rows, upright):
     args, grid, low_spec, row_spec, all_spec, log_spec, log_shape, unused, flops = attend_sizes(
         queries, keys, span, query_rows
     )
+    mixed_spec, mixed_shape = row_spec, queries.shape
+    if upright:
+        group_cols = args[0] * HD
+        mixed_spec = pl.BlockSpec((group_cols, query_rows), lambda g, b: (g, b))
+        mixed_shape = queries.shape[::-1]
     return pl.pallas_call(
-        functools.partial(forward_body, *args),
+        functools.partial(forward_body, *args, upright),
         grid=grid,
         in_specs=[low_spec, row_spec, all_spec, all_spec],
-        out_specs=[row_spec, log_spec],
-        out_shape=[jax.ShapeDtypeStruct(queries.shape, NARROW_TYPE), log_shape],
+        out_specs=[mixed_spec, log_spec],
+        out_shape=[jax.ShapeDtypeStruct(mixed_shape, NARROW_TYPE), log_shape],
         compiler_params=pltpu.CompilerParams(vmem_limit_bytes=VMEM_BYTES),
         cost_estimate=pl.CostEstimate(
             flops=16 * flops, transcendentals=flops // 128, bytes_accessed=1 << 20
@@ -284,10 +582,6 @@
     def my_block(table):
         return lax.dynamic_slice_in_dim(table, device * owned_rows, owned_rows, 0)
 
-    with jax.named_scope("cotangent_rows"):
-        delta_grad = compact(seq_gather(narrow(product(send_map, cotangent))))
-        delta_own = my_block(delta_grad)
-
     with jax.named_scope("byte_attend"):
         stream_value = wide(stream)
         normed = narrow(rms_scale(stream_value, attend_gain))
@@ -302,6 +596,8 @@
         for step, need_rows in enumerate(need_list):
             arrived_list.append(from_behind(key_value[tok_rows - need_rows :], "seq", step + 1))
         extended = jnp.concatenate(arrived_list[::-1] + [key_value], axis=0)
+        delta_slots = narrow(product(send_map, cotangent))
+        extended, delta_slots = lax.optimization_barrier((extended, delta_slots))
         keys = extended[:, :head_cols]
         values = extended[:, head_cols:]
         window_low = jnp.maximum(
@@ -309,11 +605,11 @@
         )[None, :]
         window_span = WIN + query_rows
         mixed_heads, window_log = attend_forward(
-            window_low, queries, keys, values, window_span, query_rows
-        )
-        all_mixed = lax.all_gather(mixed_heads, "tensor", axis=1, tiled=True)
+            window_low, queries, keys, values, window_span, query_rows, True
+        )
+        all_mixed = tensor_gather(mixed_heads, 0, 2)
         all_output = lax.all_gather(attend_output, "tensor", axis=0, tiled=True)
-        after_attend = stream_value + product(all_mixed, all_output)
+        after_attend = stream_value + transposed_times(all_mixed, all_output)
 
     with jax.named_scope("byte_feed"):
         normed_two = narrow(rms_scale(after_attend, byte_gain))
@@ -324,11 +620,15 @@
     with jax.named_scope("patch_rows"):
         attend_high = narrow(after_attend)
         attend_rest = narrow(after_attend - wide(attend_high))
-        rows_sum = wide(tensor_sum(product(send_map, feed_part)))
+        rows_sum = wide(tensor_sum(narrow(product(send_map, feed_part)), 1, 2))
         rows_here = narrow(
             product(send_map, attend_high) + product(send_map, attend_rest) + rows_sum
         )
-        byte_rows = compact(seq_gather(rows_here))
+        byte_rows = compact(seq_gather(rows_here, 2))
+
+    with jax.named_scope("cotangent_rows"):
+        delta_grad = compact(lax.all_gather(delta_slots, "seq", axis=0, tiled=True))
+        delta_own = my_block(delta_grad)
 
     wide_pad = ((0, 0), (0, big_width - width))
     with jax.named_scope("patch_attend"):
@@ -341,21 +641,22 @@
         patch_query_rows = min(256, total_rows)
         patch_span = min(total_rows, item_cap + patch_query_rows)
         mixed_patch, patch_log = attend_forward(
-            rank_low, patch_queries, patch_keys, patch_values, patch_span, patch_query_rows
-        )
-        branch_own = wide(tensor_sum(product(my_block(mixed_patch), patch_output)))
+            rank_low, patch_queries, patch_keys, patch_values, patch_span, patch_query_rows, False
+        )
+        branch_own = wide(tensor_sum(narrow(product(my_block(mixed_patch), patch_output)), 3, 2))
 
     with jax.named_scope("patch_dense"):
         own_rows = wide(jnp.pad(my_block(byte_rows), wide_pad))
         after_patch = own_rows + branch_own
         normed_four = narrow(rms_scale(after_patch, dense_gain))
-        all_normed = seq_gather(normed_four)
         dense_pre = product(normed_four, dense_up)
         dense_pre_grad = narrow(gelu_back(dense_pre, times_transposed(delta_own, dense_down)))
-        normed_four_grad = wide(tensor_sum(times_transposed(dense_pre_grad, dense_up)))
+        normed_four_grad = wide(tensor_sum(narrow(times_transposed(dense_pre_grad, dense_up)), 4, 2))
         after_patch_grad, densegain_grad = norm_back(after_patch, dense_gain, normed_four_grad)
         branch_grad_own = narrow(after_patch_grad + wide(jnp.pad(delta_own, wide_pad)))
-        branch_grad = seq_gather(branch_grad_own)
+        branch_grad = seq_gather(branch_grad_own, 5)
+        branch_grad, normed_later = lax.optimization_barrier((branch_grad, normed_four))
+        all_normed = lax.all_gather(normed_later, "seq", axis=0, tiled=True)
 
     with jax.named_scope("dense_weights"):
         block_rows = min(1024, total_rows)
@@ -389,7 +690,7 @@
         delta_part = product(my_slots(mixed_patch), patch_output[:, :width])
         delta_part = narrow(delta_part + product(my_slots(dense_act), dense_down))
         result_part = wide(feed_part) + transposed_times(send_map, delta_part)
-        result = narrow(after_attend + wide(tensor_sum(result_part)))
+        result = narrow(after_attend + wide(lax.psum(narrow(result_part), "tensor")))
 
     with jax.named_scope("patch_attend_back"):
         patchoutput_grad = transposed_times(mixed_patch, branch_grad)
@@ -409,9 +710,8 @@
         )
         patchinput_grad = transposed_times(normed_three, patch_projected_grad)
         patchinput_grad = patchinput_grad.reshape(big_width, 3, patch_cols)
-        normed_three_grad = wide(
-            tensor_sum(times_transposed(my_slots(patch_projected_grad), patch_matrix))
-        )
+        normed_three_grad = times_transposed(my_slots(patch_projected_grad), patch_matrix)
+        normed_three_grad = wide(tensor_sum(narrow(normed_three_grad), 6, 2))
         patch_norm_grad, patchgain_grad = norm_back(
             wide(jnp.pad(rows_here, wide_pad)), patch_gain, normed_three_grad
         )
@@ -429,13 +729,16 @@
         gate_grad = narrow(gelu_back(gate_pre, activated_grad))
         bytedown_grad = transposed_times(activated, feed_grad)
         byteup_grad = transposed_times(normed_two, gate_grad)
-        normed_two_grad = wide(tensor_sum(times_transposed(gate_grad, byte_up)))
+        feed_pack = narrow(jnp.concatenate([byteup_grad, bytedown_grad], axis=1))
+        normed_two_part = narrow(times_transposed(gate_grad, byte_up))
+        feed_pack, normed_two_part = lax.optimization_barrier((feed_pack, normed_two_part))
+        normed_two_grad = wide(tensor_sum(normed_two_part, 7, 2))
         feed_norm_grad, bytegain_grad = norm_back(after_attend, byte_gain, normed_two_grad)
         after_attend_grad = wide(feed_grad) + feed_norm_grad
 
     with jax.named_scope("byte_attend_back"):
         attend_branch_grad = narrow(after_attend_grad)
-        attendoutput_grad = transposed_times(mixed_heads, attend_branch_grad)
+        attendoutput_grad = product(mixed_heads, attend_branch_grad)
         mixed_heads_grad = narrow(times_transposed(attend_branch_grad, attend_output))
         query_grad, key_grad, value_grad = attend_backward(
             window_low, window_log, queries, mixed_heads_grad, keys, values, window_span, query_rows
@@ -449,27 +752,29 @@
             own_grad = own_grad.at[tok_rows - need_rows :].add(wide(returned))
         projected_grad = jnp.concatenate([query_grad, narrow(own_grad)], axis=1)
         attendinput_grad = transposed_times(normed, projected_grad)
-        normed_grad = wide(tensor_sum(times_transposed(projected_grad, in_matrix)))
+        normed_grad = wide(tensor_sum(narrow(times_transposed(projected_grad, in_matrix)), 8, 2))
         stream_norm_grad, attendgain_grad = norm_back(stream_value, attend_gain, normed_grad)
         inflow = narrow(after_attend_grad + stream_norm_grad)
 
     with jax.named_scope("weight_sums"):
 
         def seq_sum(pieces):
-            part = lax.psum_scatter(narrow(pieces), "seq", scatter_dimension=0, tiled=True)
+            part = lax.psum_scatter(pieces, "seq", scatter_dimension=0, tiled=True)
             return wide(lax.all_gather(part, "seq", axis=0, tiled=True))
 
-        feed_sum = seq_sum(jnp.concatenate([byteup_grad, bytedown_grad], axis=1))
+        feed_sum = seq_sum(feed_pack)
         hidden = byte_up.shape[1]
         byteup_grad = feed_sum[:, :hidden]
         bytedown_grad = feed_sum[:, hidden:]
+        gains = jnp.concatenate([attendgain_grad, bytegain_grad, patchgain_grad, densegain_grad])
+        gain_cols = gains.shape[0] // width
+        gains = jnp.pad(gains.reshape(gain_cols, width).T, ((0, 0), (0, 128 - gain_cols)))
         attend_sum = seq_sum(
-            jnp.concatenate([attendinput_grad, attendoutput_grad.reshape(width, -1)], axis=1)
+            narrow(jnp.concatenate([attendinput_grad, attendoutput_grad.T, gains], axis=1))
         )
         attendinput_grad = attend_sum[:, : 3 * head_cols].reshape(width, 3, head_cols)
-        attendoutput_grad = attend_sum[:, 3 * head_cols :].reshape(head_cols, width)
-        gains = jnp.concatenate([attendgain_grad, bytegain_grad, patchgain_grad, densegain_grad])
-        gains = lax.psum(gains, "seq")
+        attendoutput_grad = attend_sum[:, 3 * head_cols : 4 * head_cols].T
+        gains = attend_sum[:, 4 * head_cols : 4 * head_cols + gain_cols].T.reshape(-1)
         attendgain_grad = gains[:width]
         bytegain_grad = gains[width : 2 * width]
         patchgain_grad = gains[2 * width : 2 * width + big_width]

time: 871 us -> 665 us (0.76)
  waiting for transfers between devices: 452 us -> 143 us
  Pallas kernels: 92.8 us -> 269 us
  blocking collectives: 36.2 us -> 0 us
  matrix products: 133 us -> 115 us
  local copies, waits for them, and re-layouts: 73.4 us -> 63.4 us
    pallas_call x2 -> x11, Pallas kernels: 42.2 us -> 218 us  [the longest x6 101 us: tensor_sum(): pl.pallas_call(functools.partial(tensor_sum_body, chunks), in_specs=[pl.B...]
    all_gather x5 -> x2, waiting for transfers between devices: 155 us -> 0.01 us  [the longest x1 0.01 us: on_device(): delta_grad = compact(lax.all_gather(delta_slots, 'seq', axis=0, tiled=True))]
    psum x6 -> x1, waiting for transfers between devices: 160 us -> 7.14 us  [on_device(): lax.psum(narrow(result_part), 'tensor')]
    all_gather x2, waiting for transfers between devices: 0.01 us -> 71.6 us  [seq_sum(): return wide(lax.all_gather(part, 'seq', axis=0, tiled=True))]
    reduce_scatter x2, waiting for transfers between devices: 102 us -> 37.2 us  [seq_sum(): part = lax.psum_scatter(pieces, 'seq', scatter_dimension=0, tiled=True)]
    psum x1 -> x0, blocking collectives: 36.2 us -> none  [on_device(): gains = lax.psum(gains, 'seq')]
    dot_general x32, matrix products: 133 us -> 115 us  [contract(): lax.dot_general(left_side, right_side, (((left_axis,), (right_axis,)), ((...]
    unnamed x148 -> x180, local copies, waits for them, and re-layouts: 48.1 us -> 43.8 us
  transfers between devices with their start and end apart: 20 -> 12, of which waited for: 15 -> 6; matrix products, arithmetic and copies ran while one was open for 19% -> 21% of each run, Pallas kernels for 5% -> 36%
where the time goes in v2:
time: 665 us; the launch traced here: 658 us
  Pallas kernels  269 us (40%)
  waiting for transfers between devices  143 us (22%)
  matrix products  115 us (17%)
  local copies, waits for them, and re-layouts  63.4 us (10%)
  other arithmetic  37.2 us (6%)
  between operations  17.8 us (3%)
  starting transfers between devices  13.1 us (2%)
    dot_general x32, matrix products, contract(): lax.dot_general(left_side, right_side, (((left_axis,), (right_axis,)), ((...  115 us
    pallas_call x6, Pallas kernels, tensor_sum(): pl.pallas_call(functools.partial(tensor_sum_body, chunks), in_specs=[pl.B...  101 us
    all_gather x2, waiting for transfers between devices, seq_sum(): return wide(lax.all_gather(part, 'seq', axis=0, tiled=True))  71.6 us
    pallas_call x2, Pallas kernels, seq_gather(): pl.pallas_call(functools.partial(seq_gather_body, count), in_specs=[pl.Bl...  62.4 us
    pallas_call x2, Pallas kernels, attend_backward(): pl.pallas_call(functools.partial(backward_body, *args), grid=grid, in_spe...  51 us
    unnamed x180, local copies, waits for them, and re-layouts  43.8 us
    pallas_call x2, Pallas kernels, attend_forward(): pl.pallas_call(functools.partial(forward_body, *args, upright), grid=grid...  42 us
    reduce_scatter x2, waiting for transfers between devices, seq_sum(): part = lax.psum_scatter(pieces, 'seq', scatter_dimension=0, tiled=True)  37.2 us
  transfers between devices with their start and end apart: 12, of which 6 were waited for; matrix products, arithmetic and copies ran while one was open for 21% of the time, Pallas kernels for 36%

profile of v2, /device:TPU:0, one launch (start us, length us, event | category | flops | bytes accessed | tf_op | source)
XLA Modules:
  0.0 657.9 jit_solution(13051224147852977100)
XLA Ops:
  14.2 5.8 collective-permute-start.1
  27.8 6.3 copy.76
  41.7 16.9 %attend_forward.2 = (bf16[192,1024]{1,0:T(8,128)(2,1)S(1)}, f32[1,3,1024]{2,1,0:T(4,128)S(1)}) custom-call(s32[1,1024]{1,0:T(1,128)S(1)} %add_maximum_fusion.low, bf16[1024,192]{1,0:T(8,128)(2,1)S(1)} %slice.156.queries, bf16[2560,192]{1,0:T(8,128)(2,1)S(1)} %get-tuple-element.182.keys, bf16[2560,192]{1,0:T(8,128)(2,1)S(1)} %get-tuple-element.181.values), custom_call_target="tpu_custom_call" | custom-call | flops 11274289152 | bytes 1048576 | tf_op jit(solution)/shard_map/byte_attend/attend_forward/pallas_call | solution.py:475
  58.7 12.5 %tensor_gather.1 = bf16[768,1024]{1,0:T(8,128)(2,1)S(1)} custom-call(bf16[192,1024]{1,0:T(8,128)(2,1)S(1)} %get-tuple-element.63.block), custom_call_target="tpu_custom_call" | custom-call | tf_op jit(solution)/shard_map/byte_attend/tensor_gather/pallas_call | solution.py:256
  81.9 10.2 %tensor_sum.6 = bf16[256,768]{1,0:T(8,128)(2,1)S(1)} custom-call(bf16[256,768]{1,0:T(8,128)(2,1)S(1)} %convolution_convert_fusion.12.part), custom_call_target="tpu_custom_call" | custom-call | tf_op jit(solution)/shard_map/patch_rows/tensor_sum/pallas_call | solution.py:189
  93.4 40.0 %seq_gather.2 = bf16[2048,768]{1,0:T(8,128)(2,1)S(1)} custom-call(bf16[256,768]{1,0:T(8,128)(2,1)S(1)} %fusion.47.block), custom_call_target="tpu_custom_call" | custom-call | tf_op jit(solution)/shard_map/patch_rows/seq_gather/pallas_call | solution.py:358
  137.6 4.7 convolution_convert_fusion
  142.5 25.1 %attend_forward.3 = (bf16[1024,384]{1,0:T(8,128)(2,1)S(1)}, f32[3,2,1024]{2,1,0:T(2,128)S(1)}) custom-call(s32[1,1024]{1,0:T(1,128)S(1)} %bitcast.58, bf16[1024,384]{1,0:T(8,128)(2,1)S(1)} %get-tuple-element.180.queries, bf16[1024,384]{1,0:T(8,128)(2,1)S(1)} %get-tuple-element.179.keys, bf16[1024,384]{1,0:T(8,128)(2,1)S(1)} %get-tuple-element.178.values), custom_call_target="tpu_custom_call" | custom-call | flops 12884901888 | bytes 1048576 | tf_op jit(solution)/shard_map/patch_attend/attend_forward/pallas_call | solution.py:475
  168.1 11.1 %tensor_sum.7 = bf16[128,1536]{1,0:T(8,128)(2,1)S(1)} custom-call(bf16[128,1536]{1,0:T(8,128)(2,1)S(1)} %convolution_convert_fusion.3.part), custom_call_target="tpu_custom_call" | custom-call | tf_op jit(solution)/shard_map/patch_attend/tensor_sum/pallas_call | solution.py:189
  181.3 5.6 fusion.38
  196.1 5.9 convolution_convert_fusion.2.part
  203.0 10.1 %tensor_sum.8 = bf16[128,1536]{1,0:T(8,128)(2,1)S(1)} custom-call(bf16[128,1536]{1,0:T(8,128)(2,1)S(1)} %copy-done.20), custom_call_target="tpu_custom_call" | custom-call | tf_op jit(solution)/shard_map/patch_dense/tensor_sum/pallas_call | solution.py:189
  216.9 22.5 %seq_gather.3 = bf16[1024,1536]{1,0:T(8,128)(2,1)S(1)} custom-call(bf16[128,1536]{1,0:T(8,128)(2,1)S(1)} %fusion.62.block), custom_call_target="tpu_custom_call" | custom-call | tf_op jit(solution)/shard_map/patch_dense/seq_gather/pallas_call | solution.py:358
  245.5 29.2 %attend_backward.2 = (bf16[1024,384]{1,0:T(8,128)(2,1)S(1)}, bf16[1024,384]{1,0:T(8,128)(2,1)S(1)}, bf16[1024,384]{1,0:T(8,128)(2,1)S(1)}) custom-call(s32[1,1024]{1,0:T(1,128)S(1)} %bitcast.59, f32[3,2,1024]{2,1,0:T(2,128)S(1)} %copy-done.23, bf16[1024,384]{1,0:T(8,128)(2,1)S(1)} %copy-done.16, bf16[1024,384]{1,0:T(8,128)(2,1)S(1)} %convolution_convert_fusion.11.out_grads, ...), custom_call_target="tpu_custom_call" | custom-call | flops 16106127360 | bytes 1048576 | tf_op jit(solution)/shard_map/patch_attend_back/attend_backward/pallas_call | solution.py:494
  278.9 14.1 %tensor_sum.9 = bf16[256,1536]{1,0:T(8,128)(2,1)S(1)} custom-call(bf16[256,1536]{1,0:T(8,128)(2,1)S(1)} %convolution_convert_fusion.1.part), custom_call_target="tpu_custom_call" | custom-call | tf_op jit(solution)/shard_map/patch_attend_back/tensor_sum/pallas_call | solution.py:189
  308.0 10.7 %multiply_convert_fusion = (bf16[1024,1536]{1,0:T(8,128)(2,1)S(1)}, f32[1024,1536]{1,0:T(8,128)}) fusion(bf16[1024,1536]{1,0:T(8,128)(2,1)} %all-gather.10.cloned.1.call-done, bf16[1536,1536]{1,0:T(8,128)(2,1)} %param.36), kind=kOutput, calls=%fused_computation.17 | convolution fusion | flops 4845993984 | bytes 17301504 | tf_op jit(solution)/shard_map/dense_weights/dot_general | solution.py:48
  329.5 33.7 %tensor_sum.10 = bf16[1024,768]{1,0:T(8,128)(2,1)S(1)} custom-call(bf16[1024,768]{1,0:T(8,128)(2,1)S(1)} %copy-done.4), custom_call_target="tpu_custom_call" | custom-call | tf_op jit(solution)/shard_map/byte_feed_back/tensor_sum/pallas_call | solution.py:189
  373.4 7.1 %all-reduce.11.cloned.1.call-done = bf16[1024,768]{1,0:T(8,128)(2,1)} async-done(((bf16[1024,768]{1,0:T(8,128)(2,1)}), bf16[1024,768]{1,0:T(8,128)(2,1)}) %all-reduce.11.cloned.1.call-update) | async-done | bytes 1572880 | tf_op jit(solution)/shard_map/result/psum | solution.py:693
  380.6 4.8 fusion.29
  394.5 21.9 %attend_backward.3 = (bf16[1024,192]{1,0:T(8,128)(2,1)S(1)}, bf16[2560,192]{1,0:T(8,128)(2,1)S(1)}, bf16[2560,192]{1,0:T(8,128)(2,1)S(1)}) custom-call(s32[1,1024]{1,0:T(1,128)S(1)} %add_maximum_fusion.low, f32[1,3,1024]{2,1,0:T(4,128)S(1)} %copy-done.25, bf16[1024,192]{1,0:T(8,128)(2,1)S(1)} %copy-done.19, bf16[1024,192]{1,0:T(8,128)(2,1)S(1)} %copy-done.17, ...), custom_call_target="tpu_custom_call" | custom-call | flops 14092861440 | bytes 1048576 | tf_op jit(solution)/shard_map/byte_attend_back/attend_backward/pallas_call | solution.py:494
  421.2 20.5 %collective-permute-done.2 = bf16[1024,384]{1,0:T(8,128)(2,1)S(1)} collective-permute-done((bf16[1024,384]{1,0:T(8,128)(2,1)S(1)}, bf16[1024,384]{1,0:T(8,128)(2,1)S(1)}, u32[]{:S(2)}, u32[]{:S(2)}) %collective-permute-start.2) | collective-permute-done | bytes 786464 | tf_op jit(solution)/shard_map/byte_attend_back/ppermute | solution.py:26
  442.0 5.6 collective-permute-done.3
  450.3 21.5 %tensor_sum.11 = bf16[1024,768]{1,0:T(8,128)(2,1)S(1)} custom-call(bf16[1024,768]{1,0:T(8,128)(2,1)S(1)} %convolution_convert_fusion.4.part), custom_call_target="tpu_custom_call" | custom-call | tf_op jit(solution)/shard_map/byte_attend_back/tensor_sum/pallas_call | solution.py:189
  482.5 9.1 %fusion.42 = f32[1536,1152]{0,1:T(8,128)} fusion(bf16[1024,1152]{1,0:T(8,128)(2,1)} %copy-done.36, bf16[1024,768]{1,0:T(8,128)(2,1)} %copy-done.42, f32[1536]{0:T(1024)S(1)} %copy-done.72, f32[1024]{0:T(1024)S(1)} %copy-done.77), kind=kOutput, calls=%fused_computation.94 | convolution fusion | flops 3630170112 | bytes 11020288 | tf_op jit(solution)/shard_map/patch_attend_back/dot_general | solution.py:48
  491.7 8.3 %copy.81 = f32[1536,3,384]{2,0,1:T(8,128)} copy(f32[1536,3,384]{0,2,1:T(8,128)} %bitcast.62) | data formatting | bytes 14155776
  500.0 4.9 fusion.136
  504.9 4.4 fusion.137
  509.3 37.2 %reduce-scatter.7.cloned.1.call-done = bf16[96,896]{1,0:T(8,128)(2,1)} async-done(((bf16[768,896]{1,0:T(8,128)(2,1)}), bf16[96,896]{1,0:T(8,128)(2,1)}) %reduce-scatter.7.cloned.1.call-update) | async-done | bytes 172048 | tf_op jit(solution)/shard_map/weight_sums/reduce_scatter | solution.py:762
  546.5 15.1 %fusion.34 = f32[1536,1536]{1,0:T(8,128)} fusion(bf16[1024,1536]{1,0:T(8,128)(2,1)} %all-gather.10.cloned.1.call-done, f32[1024,1536]{1,0:T(8,128)} %get-tuple-element.189, bf16[1024,768]{1,0:T(8,128)(2,1)} %copy-done.57, bf16[1536,768]{1,0:T(8,128)(2,1)S(1)} %copy-done), kind=kOutput, calls=%fused_computation.62 | convolution fusion | flops 7279214592 | bytes 22806528 | tf_op jit(solution)/shard_map/dense_weights/dot_general | solution.py:48
  561.6 4.9 fusion.31
  566.5 32.9 %all-gather.14.cloned.1.call-done = bf16[768,1536]{1,0:T(8,128)(2,1)} async-done(((bf16[96,1536]{1,0:T(8,128)(2,1)}), bf16[768,1536]{1,0:T(8,128)(2,1)}) %all-gather.14.cloned.1.call-update) | async-done | bytes 2359312 | tf_op jit(solution)/shard_map/weight_sums/all_gather | solution.py:763
  603.6 38.7 %all-gather.12.cloned.1.call-done = bf16[768,896]{1,0:T(8,128)(2,1)} async-done(((bf16[96,896]{1,0:T(8,128)(2,1)}), bf16[768,896]{1,0:T(8,128)(2,1)}) %all-gather.12.cloned.1.call-update) | async-done | bytes 1376272 | tf_op jit(solution)/shard_map/weight_sums/all_gather | solution.py:763
  (297 shorter events, 138.9 us)
Async XLA Ops:
  7.2 188.9 %copy-start = (bf16[1536,768]{1,0:T(8,128)(2,1)S(1)}, bf16[1536,768]{1,0:T(8,128)(2,1)}, u32[]{:S(2)}) copy-start(bf16[1536,768]{1,0:T(8,128)(2,1)} %param.37) | copy-start | bytes 7077892
  7.2 65.8 %all-gather.6.cloned.1.call-start = ((), (), s32[]{:S(2)}) async-start(), calls=%async_computation.2 | async-start | bytes 1474560 | tf_op jit(solution)/shard_map/byte_attend/all_gather | solution.py:611
  14.2 25.2 %collective-permute-start.1 = (bf16[1024,384]{1,0:T(8,128)(2,1)}, bf16[1024,384]{1,0:T(8,128)(2,1)}, u32[]{:S(2)}, u32[]{:S(2)}) collective-permute-start(bf16[1024,384]{1,0:T(8,128)(2,1)} %slice.158), channel_id=1, source_target_pairs={{0,4},{4,8},{8,12},{12,16},{16,20},{20,24},{24,28},{1,5},{5,9},{9,... | collective-permute-start | bytes 2359304 | tf_op jit(solution)/shard_map/byte_attend/ppermute | solution.py:26
  20.2 19.2 %collective-permute-start = (bf16[512,384]{1,0:T(8,128)(2,1)S(1)}, bf16[512,384]{1,0:T(8,128)(2,1)}, u32[]{:S(2)}, u32[]{:S(2)}) collective-permute-start(bf16[512,384]{1,0:T(8,128)(2,1)S(1)} %slice.157), channel_id=1, source_target_pairs={{0,8},{4,12},{8,16},{12,20},{16,24},{20,28},{1,9},{5,13},{9,17},{1... | collective-permute-start | bytes 1179656 | tf_op jit(solution)/shard_map/byte_attend/ppermute | solution.py:26
  23.6 157.7 %all-gather.8.cloned.1.call-start = ((), (), s32[]{:S(2)}) async-start(), calls=%async_computation.3 | async-start | bytes 3538944 | tf_op jit(solution)/shard_map/cotangent_rows/all_gather | solution.py:630
  26.0 107.4 %copy-start.75 = (s32[1024]{0:T(1024)}, s32[1024]{0:T(1024)S(1)}, u32[]{:S(2)}) copy-start(s32[1024]{0:T(1024)S(1)} %add_subtract_fusion) | copy-start | bytes 12292
  26.6 66.2 %copy-start.49 = (s32[1024]{0:T(1024)}, s32[1024]{0:T(1024)S(1)}, u32[]{:S(2)}) copy-start(s32[1024]{0:T(1024)S(1)} %get-tuple-element.172) | copy-start | bytes 12292
  41.7 17.0 %copy-start.6 = (bf16[2560,192]{1,0:T(8,128)(2,1)}, bf16[2560,192]{1,0:T(8,128)(2,1)S(1)}, u32[]{:S(2)}) copy-start(bf16[2560,192]{1,0:T(8,128)(2,1)S(1)} %get-tuple-element.181.values) | copy-start | bytes 2949124
  41.7 17.0 %copy-start.7 = (bf16[2560,192]{1,0:T(8,128)(2,1)}, bf16[2560,192]{1,0:T(8,128)(2,1)S(1)}, u32[]{:S(2)}) copy-start(bf16[2560,192]{1,0:T(8,128)(2,1)S(1)} %get-tuple-element.182.keys) | copy-start | bytes 2949124
  58.7 18.2 %copy-start.24 = (f32[1,3,1024]{2,1,0:T(4,128)}, f32[1,3,1024]{2,1,0:T(4,128)S(1)}, u32[]{:S(2)}) copy-start(f32[1,3,1024]{2,1,0:T(4,128)S(1)} %get-tuple-element.73.log_total) | copy-start | bytes 36868
  72.4 235.7 %all-gather.10.cloned.1.call-start = ((), (), s32[]{:S(2)}) async-start(), calls=%async_computation.4 | async-start | bytes 3538944 | tf_op jit(solution)/shard_map/patch_dense/all_gather | solution.py:659
  76.9 15.8 %copy-start.28 = (f32[1024,768]{1,0:T(8,128)}, f32[1024,768]{1,0:T(8,128)S(1)}, u32[]{:S(2)}) copy-start(f32[1024,768]{1,0:T(8,128)S(1)} %get-tuple-element.187) | copy-start | bytes 9437188
  142.5 25.1 %copy-start.11 = (bf16[1024,384]{1,0:T(8,128)(2,1)}, bf16[1024,384]{1,0:T(8,128)(2,1)S(1)}, u32[]{:S(2)}) copy-start(bf16[1024,384]{1,0:T(8,128)(2,1)S(1)} %get-tuple-element.178.values) | copy-start | bytes 2359300
  142.5 25.1 %copy-start.13 = (bf16[1024,384]{1,0:T(8,128)(2,1)}, bf16[1024,384]{1,0:T(8,128)(2,1)S(1)}, u32[]{:S(2)}) copy-start(bf16[1024,384]{1,0:T(8,128)(2,1)S(1)} %get-tuple-element.179.keys) | copy-start | bytes 2359300
  142.5 25.1 %copy-start.15 = (bf16[1024,384]{1,0:T(8,128)(2,1)}, bf16[1024,384]{1,0:T(8,128)(2,1)S(1)}, u32[]{:S(2)}) copy-start(bf16[1024,384]{1,0:T(8,128)(2,1)S(1)} %get-tuple-element.180.queries) | copy-start | bytes 2359300
  142.5 25.2 %copy-start.40 = (bf16[384,1536]{1,0:T(8,128)(2,1)S(1)}, bf16[384,1536]{1,0:T(8,128)(2,1)}, u32[]{:S(2)}) copy-start(bf16[384,1536]{1,0:T(8,128)(2,1)} %param.34) | copy-start | bytes 3538948
  241.2 139.4 %all-reduce.11.cloned.1.call-start = ((), (), s32[]{:S(2)}) async-start(), calls=%async_computation.5 | async-start | bytes 3145728 | tf_op jit(solution)/shard_map/result/psum | solution.py:693
  277.6 15.4 %copy-start.71 = (f32[1536]{0:T(1024)S(1)}, f32[1536]{0:T(1024)}, u32[]{:S(2)}) copy-start(f32[1536]{0:T(1024)} %param.32) | copy-start | bytes 18436
  277.6 16.6 %copy-start.43 = (bf16[1024,768]{1,0:T(8,128)(2,1)S(1)}, bf16[1024,768]{1,0:T(8,128)(2,1)}, u32[]{:S(2)}) copy-start(bf16[1024,768]{1,0:T(8,128)(2,1)} %param.23) | copy-start | bytes 4718596
  326.1 155.7 %reduce-scatter.9.cloned.1.call-start = ((), (), s32[]{:S(2)}) async-start(), calls=%async_computation.9 | async-start | bytes 2654208 | tf_op jit(solution)/shard_map/weight_sums/reduce_scatter | solution.py:762
  373.4 173.1 %reduce-scatter.7.cloned.1.call-start = ((), (), s32[]{:S(2)}) async-start(), calls=%async_computation.8 | async-start | bytes 1548288 | tf_op jit(solution)/shard_map/weight_sums/reduce_scatter | solution.py:762
  416.4 31.5 %copy-start.21 = (bf16[1024,192]{1,0:T(8,128)(2,1)}, bf16[1024,192]{1,0:T(8,128)(2,1)S(1)}, u32[]{:S(2)}) copy-start(bf16[1024,192]{1,0:T(8,128)(2,1)S(1)} %get-tuple-element.74) | copy-start | bytes 1179652
  416.7 25.0 %collective-permute-start.2 = (bf16[1024,384]{1,0:T(8,128)(2,1)S(1)}, bf16[1024,384]{1,0:T(8,128)(2,1)S(1)}, u32[]{:S(2)}, u32[]{:S(2)}) collective-permute-start(bf16[1024,384]{1,0:T(8,128)(2,1)S(1)} %fusion.65), channel_id=1, source_target_pairs={{4,0},{8,4},{12,8},{16,12},{20,16},{24,20},{28,24},{5,1},{9,5},{13... | collective-permute-start | bytes 2359304 | tf_op jit(solution)/shard_map/byte_attend_back/ppermute | solution.py:26
  418.4 29.2 %collective-permute-start.3 = (bf16[512,384]{1,0:T(8,128)(2,1)S(1)}, bf16[512,384]{1,0:T(8,128)(2,1)S(1)}, u32[]{:S(2)}, u32[]{:S(2)}) collective-permute-start(bf16[512,384]{1,0:T(8,128)(2,1)S(1)} %pad_maximum_fusion.5), channel_id=1, source_target_pairs={{8,0},{12,4},{16,8},{20,12},{24,16},{28,20},{9,1},{13,5},{17,9},{2... | collective-permute-start | bytes 1179656 | tf_op jit(solution)/shard_map/byte_attend_back/ppermute | solution.py:26
  450.2 22.7 %copy-start.33 = (bf16[1024,768]{1,0:T(8,128)(2,1)S(1)}, bf16[1024,768]{1,0:T(8,128)(2,1)}, u32[]{:S(2)}) copy-start(bf16[1024,768]{1,0:T(8,128)(2,1)} %param.22) | copy-start | bytes 4718596
  450.2 22.7 %copy-start.54 = (f32[1024]{0:T(1024)S(1)}, f32[1024]{0:T(1024)}, u32[]{:S(2)}) copy-start(f32[1024]{0:T(1024)} %copy-done.53) | copy-start | bytes 12292
  450.2 22.7 %copy-start.61 = (f32[768]{0:T(1024)S(1)}, f32[768]{0:T(1024)}, u32[]{:S(2)}) copy-start(f32[768]{0:T(1024)} %param.26) | copy-start | bytes 9220
  450.3 24.2 %copy-start.62 = (bf16[1536]{0:T(1024)(128)(2,1)S(1)}, bf16[1536]{0:T(1024)(128)(2,1)}, u32[]{:S(2)}) copy-start(bf16[1536]{0:T(1024)(128)(2,1)} %get-tuple-element.168) | copy-start | bytes 9220
  450.3 24.2 %copy-start.63 = (bf16[1536]{0:T(1024)(128)(2,1)S(1)}, bf16[1536]{0:T(1024)(128)(2,1)}, u32[]{:S(2)}) copy-start(bf16[1536]{0:T(1024)(128)(2,1)} %get-tuple-element.166) | copy-start | bytes 9220
  450.3 24.2 %copy-start.69 = (bf16[768]{0:T(1024)(128)(2,1)S(1)}, bf16[768]{0:T(1024)(128)(2,1)}, u32[]{:S(2)}) copy-start(bf16[768]{0:T(1024)(128)(2,1)} %get-tuple-element.162) | copy-start | bytes 4612
  481.7 117.7 %all-gather.14.cloned.1.call-start = ((), (), s32[]{:S(2)}) async-start(), calls=%async_computation.7 | async-start | bytes 2654208 | tf_op jit(solution)/shard_map/weight_sums/all_gather | solution.py:763
  482.5 159.9 %all-gather.12.cloned.1.call-start = ((), (), s32[]{:S(2)}) async-start(), calls=%async_computation.6 | async-start | bytes 1548288 | tf_op jit(solution)/shard_map/weight_sums/all_gather | solution.py:763
  (68 other events, 349.8 us)
Sparse Core Ops, SparseCore 0:
  23.7 15.9 all-gather.5
  72.5 72.6 all-gather.7
  241.3 59.0 all-gather.9
  326.2 54.3 all-reduce.10
  384.5 82.0 reduce-scatter.8
  481.8 64.5 reduce-scatter.6
  548.6 50.7 all-gather.13
  601.6 40.6 all-gather.11

commit v3 on v2

--- a/solution.py
+++ b/solution.py
@@ -98,93 +98,67 @@
     )
 
 
-def tensor_sum_body(
-    chunks, part, total, pair_got, mine, across_got, pair_send, pair_recv, far_send, far_recv,
-    out_send, out_recv,
-):
+def tensor_sum_body(chunks, part, total, pair_got, mine, across_got, send_sem, recv_sem):
     place, pair, across = tensor_peers()
     pair_id = {"tensor": pair}
     across_id = {"tensor": across}
     meet((pair_id, across_id))
-    rows = part.shape[0] // 4
+    rows = part.shape[0] // 2
     step = rows // chunks
-    pair_across = (pair + 2) % 4
-
-    def piece(quarter, chunk):
-        return pl.ds(pl.multiple_of(quarter * rows + chunk * step, 16), step)
-
-    copies = []
-    for slot, quarter in enumerate((pair_across, pair)):
-        for chunk in range(chunks):
-            copy = remote(
-                part.at[piece(quarter, chunk)],
-                pair_got.at[slot, pl.ds(chunk * step, step)],
-                pair_send.at[slot, chunk],
-                pair_recv.at[slot, chunk],
-                pair_id,
-            )
-            copy.start()
-            copies.append(copy)
+    core = place % 2
+
+    def piece(half, chunk):
+        return pl.ds(pl.multiple_of(half * rows + chunk * step, 16), step)
+
+    given = []
+    for chunk in range(chunks):
+        copy = remote(
+            part.at[piece(1 - core, chunk)],
+            pair_got.at[pl.ds(chunk * step, step)],
+            send_sem.at[0, chunk],
+            recv_sem.at[0, chunk],
+            pair_id,
+        )
+        copy.start()
+        given.append(copy)
     far = []
     for chunk in range(chunks):
-        copies[chunk].wait_recv()
+        given[chunk].wait_recv()
         here = pl.ds(chunk * step, step)
-        mine[here] = (
-            part[piece(across, chunk)].astype(WIDE_TYPE) + pair_got[0, here].astype(WIDE_TYPE)
-        ).astype(NARROW_TYPE)
+        mine[here] = narrow(wide(part[piece(core, chunk)]) + wide(pair_got[here]))
         copy = remote(
             mine.at[here],
             across_got.at[here],
-            far_send.at[chunk],
-            far_recv.at[chunk],
+            send_sem.at[1, chunk],
+            recv_sem.at[1, chunk],
             across_id,
         )
         copy.start()
         far.append(copy)
-    out_copies = []
+    back = []
     for chunk in range(chunks):
-        copies[chunks + chunk].wait_recv()
         far[chunk].wait_recv()
         here = pl.ds(chunk * step, step)
-        own = piece(place, chunk)
-        total[own] = (
-            part[own].astype(WIDE_TYPE)
-            + pair_got[1, here].astype(WIDE_TYPE)
-            + across_got[here].astype(WIDE_TYPE)
-        ).astype(NARROW_TYPE)
-        for kind, peer in ((0, across_id), (1, pair_id)):
-            copy = remote(
-                total.at[own],
-                total.at[own],
-                out_send.at[kind, chunk],
-                out_recv.at[kind, chunk],
-                peer,
-            )
-            copy.start()
-            out_copies.append(copy)
-    passed = []
-    for chunk in range(chunks):
-        out_copies[2 * chunk].wait_recv()
-        theirs = piece(across, chunk)
+        own = piece(core, chunk)
+        total[own] = narrow(wide(mine[here]) + wide(across_got[here]))
         copy = remote(
-            total.at[theirs],
-            total.at[theirs],
-            out_send.at[2, chunk],
-            out_recv.at[2, chunk],
+            total.at[own],
+            total.at[own],
+            send_sem.at[2, chunk],
+            recv_sem.at[2, chunk],
             pair_id,
         )
         copy.start()
-        passed.append(copy)
-    for chunk in range(chunks):
-        out_copies[2 * chunk + 1].wait_recv()
-        passed[chunk].wait_recv()
-    for copy in copies + far + out_copies + passed:
+        back.append(copy)
+    for copy in back:
+        copy.wait_recv()
+    for copy in given + far + back:
         copy.wait_send()
 
 
 def tensor_sum(part, collective_id, chunks):
     rows, cols = part.shape
-    quarter = rows // 4
+    half = rows // 2
     dma = pltpu.SemaphoreType.DMA
     return pl.pallas_call(
         functools.partial(tensor_sum_body, chunks),
@@ -192,10 +166,9 @@
         out_specs=pl.BlockSpec(memory_space=pltpu.VMEM),
         out_shape=jax.ShapeDtypeStruct((rows, cols), NARROW_TYPE),
         scratch_shapes=[
-            pltpu.VMEM((2, quarter, cols), NARROW_TYPE),
-            pltpu.VMEM((quarter, cols), NARROW_TYPE),
-            pltpu.VMEM((quarter, cols), NARROW_TYPE),
-            dma((2, chunks)), dma((2, chunks)), dma((chunks,)), dma((chunks,)),
+            pltpu.VMEM((half, cols), NARROW_TYPE),
+            pltpu.VMEM((half, cols), NARROW_TYPE),
+            pltpu.VMEM((half, cols), NARROW_TYPE),
             dma((3, chunks)), dma((3, chunks)),
         ],
         compiler_params=pltpu.CompilerParams(
@@ -374,38 +347,52 @@
     return (key_pos >= low_row) & (key_pos <= query_pos)
 
 
+def choose_span(counts, spans, query_rows, block, run):
+    if len(spans) == 1:
+        run(spans[0])
+    else:
+        count = counts[block]
+        for span in spans:
+            pl.when(count == span // query_rows)(functools.partial(run, span))
+
+
 def forward_body(
-    heads, query_rows, span, offset, upright, low, queries, keys, values, mixed, log_total
+    heads, query_rows, spans, offset, upright, counts, low, queries, keys, values, mixed, log_total
 ):
     block = pl.program_id(1)
-    start = jnp.maximum(block * query_rows + query_rows + offset - span, 0)
-    start = pl.multiple_of(start, 128)
-    allowed = allowed_pairs(low[...], start, span, block * query_rows + offset, query_rows)
-    rows = pl.ds(start, span)
-    for head in range(heads):
-        cols = slice(head * HD, (head + 1) * HD)
-        scores = contract(keys[rows, cols], queries[:, cols] * SCORE_SCALE, 1, 1)
-        scores = jnp.where(allowed, scores, NEGATIVE)
-        top = jnp.max(scores, axis=0, keepdims=True)
-        raised = jnp.exp(scores - top)
-        total = jnp.sum(raised, axis=0, keepdims=True)
-        weights = narrow(raised * (1.0 / total))
-        mixed_head = contract(values[rows, cols], weights, 0, 0)
-        if upright:
-            mixed[cols, :] = narrow(mixed_head)
-        else:
-            mixed[:, cols] = narrow(mixed_head.T)
-        log_total[0, head : head + 1, :] = top + jnp.log(total)
+
+    def run(span):
+        start = pl.multiple_of(block * query_rows + query_rows + offset - span, 128)
+        allowed = allowed_pairs(low[...], start, span, block * query_rows + offset, query_rows)
+        rows = pl.ds(start, span)
+        for head in range(heads):
+            cols = slice(head * HD, (head + 1) * HD)
+            scores = contract(keys[rows, cols], queries[:, cols] * SCORE_SCALE, 1, 1)
+            scores = jnp.where(allowed, scores, NEGATIVE)
+            top = jnp.max(scores, axis=0, keepdims=True)
+            raised = jnp.exp(scores - top)
+            total = jnp.sum(raised, axis=0, keepdims=True)
+            mixed_head = contract(values[rows, cols], narrow(raised), 0, 0) * (1.0 / total)
+            if upright:
+                mixed[cols, :] = narrow(mixed_head)
+            else:
+                mixed[:, cols] = narrow(mixed_head.T)
+            log_total[0, head : head + 1, :] = top + jnp.log(total)
+
+    choose_span(counts, spans, query_rows, block, run)
 
 
 def backward_body(
     heads,
     query_rows,
-    span,
+    spans,
     offset,
+    upright,
+    counts,
     low,
     log_total,
     queries,
+    mixed,
     out_grads,
     keys,
     values,
@@ -422,23 +409,29 @@
         key_sum[...] = jnp.zeros_like(key_sum)
         value_sum[...] = jnp.zeros_like(value_sum)
 
-    start = jnp.maximum(block * query_rows + query_rows + offset - span, 0)
-    start = pl.multiple_of(start, 128)
-    allowed = allowed_pairs(low[...], start, span, block * query_rows + offset, query_rows)
-    rows = pl.ds(start, span)
-    for head in range(heads):
-        cols = slice(head * HD, (head + 1) * HD)
-        query = queries[:, cols] * SCORE_SCALE
-        out_grad = out_grads[:, cols]
-        key = keys[rows, cols]
-        scores = contract(key, query, 1, 1)
-        weights = jnp.where(allowed, jnp.exp(scores - log_total[0, head : head + 1, :]), 0.0)
-        weight_grad = contract(values[rows, cols], out_grad, 1, 1)
-        inner = jnp.sum(weights * weight_grad, axis=0, keepdims=True)
-        score_grad = narrow(weights * (weight_grad - inner))
-        query_grads[:, cols] = narrow(contract(key, score_grad, 0, 0).T * SCORE_SCALE)
-        key_sum[rows, cols] += contract(score_grad, query, 1, 0)
-        value_sum[rows, cols] += contract(narrow(weights), out_grad, 1, 0)
+    def run(span):
+        start = pl.multiple_of(block * query_rows + query_rows + offset - span, 128)
+        allowed = allowed_pairs(low[...], start, span, block * query_rows + offset, query_rows)
+        rows = pl.ds(start, span)
+        for head in range(heads):
+            cols = slice(head * HD, (head + 1) * HD)
+            query = queries[:, cols] * SCORE_SCALE
+            out_grad = out_grads[:, cols]
+            if upright:
+                overlap = wide(mixed[cols, :]) * wide(out_grad).T
+            else:
+                overlap = (wide(mixed[:, cols]) * wide(out_grad)).T
+            inner = jnp.sum(overlap, axis=0, keepdims=True)
+            key = keys[rows, cols]
+            scores = contract(key, query, 1, 1)
+            weights = jnp.where(allowed, jnp.exp(scores - log_total[0, head : head + 1, :]), 0.0)
+            weight_grad = contract(values[rows, cols], out_grad, 1, 1)
+            score_grad = narrow(weights * (weight_grad - inner))
+            query_grads[:, cols] = narrow(contract(key, score_grad, 0, 0).T * SCORE_SCALE)
+            key_sum[rows, cols] += contract(score_grad, query, 1, 0)
+            value_sum[rows, cols] += contract(narrow(weights), out_grad, 1, 0)
+
+    choose_span(counts, spans, query_rows, block, run)
 
     @pl.when(block == pl.num_programs(1) - 1)
     def finish():
@@ -446,55 +439,57 @@
         value_grads[...] = narrow(value_sum[...])
 
 
-def attend_sizes(queries, keys, span, query_rows):
+def attend_sizes(queries, keys, spans, query_rows):
     rows, cols = queries.shape
     extent = keys.shape[0]
     group_cols = 128 if cols % 128 == 0 else cols
     groups = cols // group_cols
     heads = group_cols // HD
+    count_spec = pl.BlockSpec(memory_space=pltpu.SMEM)
     low_spec = pl.BlockSpec((1, query_rows), lambda g, b: (0, b))
     row_spec = pl.BlockSpec((query_rows, group_cols), lambda g, b: (b, g))
+    flat_spec = pl.BlockSpec((group_cols, query_rows), lambda g, b: (g, b))
     all_spec = pl.BlockSpec((extent, group_cols), lambda g, b: (0, g))
     log_spec = pl.BlockSpec((1, heads, query_rows), lambda g, b: (g, 0, b))
-    args = (heads, query_rows, span, extent - rows)
+    args = (heads, query_rows, spans, extent - rows)
     log_shape = jax.ShapeDtypeStruct((groups, heads, rows), WIDE_TYPE)
     grid = (groups, rows // query_rows)
-    flops = 2 * rows * span * cols
-    return args, grid, low_spec, row_spec, all_spec, log_spec, log_shape, group_cols, flops
-
-
-def attend_forward(low, queries, keys, values, span, query_rows, upright):
-    args, grid, low_spec, row_spec, all_spec, log_spec, log_shape, unused, flops = attend_sizes(
-        queries, keys, span, query_rows
-    )
-    mixed_spec, mixed_shape = row_spec, queries.shape
-    if upright:
-        group_cols = args[0] * HD
-        mixed_spec = pl.BlockSpec((group_cols, query_rows), lambda g, b: (g, b))
-        mixed_shape = queries.shape[::-1]
+    flops = 2 * rows * spans[-1] * cols
+    specs = (count_spec, low_spec, row_spec, flat_spec, all_spec, log_spec)
+    return args, grid, specs, log_shape, group_cols, flops
+
+
+def attend_forward(counts, low, queries, keys, values, spans, query_rows, upright):
+    args, grid, specs, log_shape, unused, flops = attend_sizes(queries, keys, spans, query_rows)
+    count_spec, low_spec, row_spec, flat_spec, all_spec, log_spec = specs
+    mixed_shape = queries.shape[::-1] if upright else queries.shape
     return pl.pallas_call(
         functools.partial(forward_body, *args, upright),
         grid=grid,
-        in_specs=[low_spec, row_spec, all_spec, all_spec],
-        out_specs=[mixed_spec, log_spec],
+        in_specs=[count_spec, low_spec, row_spec, all_spec, all_spec],
+        out_specs=[flat_spec if upright else row_spec, log_spec],
         out_shape=[jax.ShapeDtypeStruct(mixed_shape, NARROW_TYPE), log_shape],
         compiler_params=pltpu.CompilerParams(vmem_limit_bytes=VMEM_BYTES),
         cost_estimate=pl.CostEstimate(
             flops=16 * flops, transcendentals=flops // 128, bytes_accessed=1 << 20
         ),
         name="attend_forward",
-    )(low, queries, keys, values)
-
-
-def attend_backward(low, log_total, queries, out_grads, keys, values, span, query_rows):
-    args, grid, low_spec, row_spec, all_spec, log_spec, unused, group_cols, flops = attend_sizes(
-        queries, keys, span, query_rows
-    )
+    )(counts, low, queries, keys, values)
+
+
+def attend_backward(
+    counts, low, log_total, queries, mixed, out_grads, keys, values, spans, query_rows, upright
+):
+    args, grid, specs, unused, group_cols, flops = attend_sizes(queries, keys, spans, query_rows)
+    count_spec, low_spec, row_spec, flat_spec, all_spec, log_spec = specs
+    mixed_spec = flat_spec if upright else row_spec
     key_shape = jax.ShapeDtypeStruct(keys.shape, NARROW_TYPE)
     return pl.pallas_call(
-        functools.partial(backward_body, *args),
+        functools.partial(backward_body, *args, upright),
         grid=grid,
-        in_specs=[low_spec, log_spec, row_spec, row_spec, all_spec, all_spec],
+        in_specs=[
+            count_spec, low_spec, log_spec, row_spec, mixed_spec, row_spec, all_spec, all_spec
+        ],
         out_specs=[row_spec, all_spec, all_spec],
         out_shape=[jax.ShapeDtypeStruct(queries.shape, NARROW_TYPE), key_shape, key_shape],
         scratch_shapes=[pltpu.VMEM((keys.shape[0], group_cols), WIDE_TYPE)] * 2,
@@ -503,7 +498,11 @@
             flops=20 * flops, transcendentals=flops // 128, bytes_accessed=1 << 20
         ),
         name="attend_backward",
-    )(low, log_total, queries, out_grads, keys, values)
+    )(counts, low, log_total, queries, mixed, out_grads, keys, values)
+
+
+def together(*values):
+    return lax.optimization_barrier(values)
 
 
 def in_blocks(function, rows, block_rows):
@@ -565,15 +564,16 @@
     rank_low = rank_low[None, :].astype(jnp.int32)
     slot_rows = seq_devices * capacity
 
+    def compact_rows(slots, first_row, block_rows):
+        places = lax.dynamic_slice_in_dim(rank_slot, first_row, block_rows, 0)
+        take_map = narrow(places[:, None] == jnp.arange(slot_rows)[None, :])
+        return narrow(product(take_map, slots))
+
     def compact(slots):
         block_rows = min(1024, total_rows)
-
-        def one_block(first_row):
-            places = lax.dynamic_slice_in_dim(rank_slot, first_row, block_rows, 0)
-            take_map = narrow(places[:, None] == jnp.arange(slot_rows)[None, :])
-            return narrow(product(take_map, slots))
-
-        return in_blocks(one_block, total_rows, block_rows)
+        return in_blocks(
+            lambda first_row: compact_rows(slots, first_row, block_rows), total_rows, block_rows
+        )
 
     def my_slots(table):
         padded = jnp.pad(table, ((0, capacity), (0, 0)))
@@ -597,15 +597,17 @@
             arrived_list.append(from_behind(key_value[tok_rows - need_rows :], "seq", step + 1))
         extended = jnp.concatenate(arrived_list[::-1] + [key_value], axis=0)
         delta_slots = narrow(product(send_map, cotangent))
-        extended, delta_slots = lax.optimization_barrier((extended, delta_slots))
+        extended, first_half = together(extended, delta_slots[:, : width // 2])
+        slot_halves = [lax.all_gather(first_half, "seq", axis=0, tiled=True)]
         keys = extended[:, :head_cols]
         values = extended[:, head_cols:]
         window_low = jnp.maximum(
             jnp.arange(tok_rows, dtype=jnp.int32) + 1, WIN - device * tok_rows
         )[None, :]
-        window_span = WIN + query_rows
+        window_spans = (WIN + query_rows,)
+        window_counts = jnp.zeros((tok_rows // query_rows,), jnp.int32)
         mixed_heads, window_log = attend_forward(
-            window_low, queries, keys, values, window_span, query_rows, True
+            window_counts, window_low, queries, keys, values, window_spans, query_rows, True
         )
         all_mixed = tensor_gather(mixed_heads, 0, 2)
         all_output = lax.all_gather(attend_output, "tensor", axis=0, tiled=True)
@@ -624,11 +626,16 @@
         rows_here = narrow(
             product(send_map, attend_high) + product(send_map, attend_rest) + rows_sum
         )
-        byte_rows = compact(seq_gather(rows_here, 2))
+        gathered_rows, second_half = together(
+            seq_gather(rows_here, 2), delta_slots[:, width // 2 :]
+        )
+        byte_rows = compact(gathered_rows)
 
     with jax.named_scope("cotangent_rows"):
-        delta_grad = compact(lax.all_gather(delta_slots, "seq", axis=0, tiled=True))
-        delta_own = my_block(delta_grad)
+        slot_halves.append(lax.all_gather(second_half, "seq", axis=0, tiled=True))
+        delta_own = jnp.concatenate(
+            [compact_rows(half, device * owned_rows, owned_rows) for half in slot_halves], axis=1
+        )
 
     wide_pad = ((0, 0), (0, big_width - width))
     with jax.named_scope("patch_attend"):
@@ -639,9 +646,22 @@
         patch_keys = patch_projected[:, patch_cols : 2 * patch_cols]
         patch_values = patch_projected[:, 2 * patch_cols :]
         patch_query_rows = min(256, total_rows)
-        patch_span = min(total_rows, item_cap + patch_query_rows)
+        most_blocks = min(total_rows, item_cap + patch_query_rows) // patch_query_rows
+        patch_spans = tuple(patch_query_rows * (blocks + 1) for blocks in range(most_blocks))
+        patch_counts = (
+            jnp.arange(total_rows // patch_query_rows, dtype=jnp.int32)
+            + 1
+            - rank_low[0, ::patch_query_rows] // patch_query_rows
+        )
         mixed_patch, patch_log = attend_forward(
-            rank_low, patch_queries, patch_keys, patch_values, patch_span, patch_query_rows, False
+            patch_counts,
+            rank_low,
+            patch_queries,
+            patch_keys,
+            patch_values,
+            patch_spans,
+            patch_query_rows,
+            False,
         )
         branch_own = wide(tensor_sum(narrow(product(my_block(mixed_patch), patch_output)), 3, 2))
 
@@ -654,12 +674,96 @@
         normed_four_grad = wide(tensor_sum(narrow(times_transposed(dense_pre_grad, dense_up)), 4, 2))
         after_patch_grad, densegain_grad = norm_back(after_patch, dense_gain, normed_four_grad)
         branch_grad_own = narrow(after_patch_grad + wide(jnp.pad(delta_own, wide_pad)))
-        branch_grad = seq_gather(branch_grad_own, 5)
-        branch_grad, normed_later = lax.optimization_barrier((branch_grad, normed_four))
+        branch_grad, normed_later = together(seq_gather(branch_grad_own, 5), normed_four)
         all_normed = lax.all_gather(normed_later, "seq", axis=0, tiled=True)
+
+    with jax.named_scope("patch_attend_back"):
+        patchoutput_grad = transposed_times(mixed_patch, branch_grad)
+        mixed_patch_grad = narrow(times_transposed(branch_grad, patch_output))
+        patch_projected_grad = jnp.concatenate(
+            attend_backward(
+                patch_counts,
+                rank_low,
+                patch_log,
+                patch_queries,
+                mixed_patch,
+                mixed_patch_grad,
+                patch_keys,
+                patch_values,
+                patch_spans,
+                patch_query_rows,
+                False,
+            ),
+            axis=1,
+        )
+        patchinput_grad = transposed_times(normed_three, patch_projected_grad)
+        patchinput_grad = patchinput_grad.reshape(big_width, 3, patch_cols)
+        normed_three_grad = times_transposed(my_slots(patch_projected_grad), patch_matrix)
+        normed_three_grad = wide(tensor_sum(narrow(normed_three_grad), 6, 2))
+        patch_norm_grad, patchgain_grad = norm_back(
+            wide(jnp.pad(rows_here, wide_pad)), patch_gain, normed_three_grad
+        )
+        rows_grad = narrow(wide(my_slots(branch_grad[:, :width])) + patch_norm_grad[:, :width])
+
+    with jax.named_scope("byte_feed_back"):
+        feed_grad = narrow(
+            jnp.where(
+                boundary[:, None] == 1,
+                transposed_times(send_map, rows_grad),
+                wide(cotangent),
+            )
+        )
+        activated_grad = times_transposed(feed_grad, byte_down)
+        gate_grad = narrow(gelu_back(gate_pre, activated_grad))
+        bytedown_grad = transposed_times(activated, feed_grad)
+        byteup_grad = transposed_times(normed_two, gate_grad)
+        feed_pack = narrow(jnp.concatenate([byteup_grad, bytedown_grad], axis=1))
+        normed_two_part = narrow(times_transposed(gate_grad, byte_up))
+        feed_pack, normed_two_part, all_normed = together(feed_pack, normed_two_part, all_normed)
+        feed_part_sum = lax.psum_scatter(feed_pack, "seq", scatter_dimension=0, tiled=True)
+        normed_two_grad = wide(tensor_sum(normed_two_part, 7, 4))
+        feed_norm_grad, bytegain_grad = norm_back(after_attend, byte_gain, normed_two_grad)
+        after_attend_grad = wide(feed_grad) + feed_norm_grad
+
+    with jax.named_scope("byte_attend_back"):
+        attend_branch_grad = narrow(after_attend_grad)
+        attendoutput_grad = product(mixed_heads, attend_branch_grad)
+        mixed_heads_grad = narrow(times_transposed(attend_branch_grad, attend_output))
+        query_grad, key_grad, value_grad = attend_backward(
+            window_counts,
+            window_low,
+            window_log,
+            queries,
+            mixed_heads,
+            mixed_heads_grad,
+            keys,
+            values,
+            window_spans,
+            query_rows,
+            True,
+        )
+        pair_grad = jnp.concatenate([key_grad, value_grad], axis=1)
+        pair_grad, all_normed, delta_halves = together(pair_grad, all_normed, tuple(slot_halves))
+        own_grad = wide(pair_grad[WIN:])
+        begin_row = WIN
+        for step, need_rows in enumerate(need_list):
+            begin_row = begin_row - need_rows
+            returned = from_behind(pair_grad[begin_row : begin_row + need_rows], "seq", -step - 1)
+            own_grad = own_grad.at[tok_rows - need_rows :].add(wide(returned))
+        own_grad, feed_part_sum = together(own_grad, feed_part_sum)
+        projected_grad = jnp.concatenate([query_grad, narrow(own_grad)], axis=1)
+        attendinput_grad = transposed_times(normed, projected_grad)
+        attend_pack = narrow(jnp.concatenate([attendinput_grad, attendoutput_grad.T], axis=1))
+        normed_part = narrow(times_transposed(projected_grad, in_matrix))
+        attend_pack, normed_part = together(attend_pack, normed_part)
+        normed_grad = wide(tensor_sum(normed_part, 8, 4))
+        stream_norm_grad, attendgain_grad = norm_back(stream_value, attend_gain, normed_grad)
+        inflow = narrow(after_attend_grad + stream_norm_grad)
 
     with jax.named_scope("dense_weights"):
         block_rows = min(1024, total_rows)
+
+        delta_grad = jnp.concatenate([compact(half) for half in delta_halves], axis=1)
 
         def dense_block(first_row):
             some_normed = lax.dynamic_slice_in_dim(all_normed, first_row, block_rows, 0)
@@ -690,91 +794,29 @@
         delta_part = product(my_slots(mixed_patch), patch_output[:, :width])
         delta_part = narrow(delta_part + product(my_slots(dense_act), dense_down))
         result_part = wide(feed_part) + transposed_times(send_map, delta_part)
-        result = narrow(after_attend + wide(lax.psum(narrow(result_part), "tensor")))
-
-    with jax.named_scope("patch_attend_back"):
-        patchoutput_grad = transposed_times(mixed_patch, branch_grad)
-        mixed_patch_grad = narrow(times_transposed(branch_grad, patch_output))
-        patch_projected_grad = jnp.concatenate(
-            attend_backward(
-                rank_low,
-                patch_log,
-                patch_queries,
-                mixed_patch_grad,
-                patch_keys,
-                patch_values,
-                patch_span,
-                patch_query_rows,
-            ),
-            axis=1,
-        )
-        patchinput_grad = transposed_times(normed_three, patch_projected_grad)
-        patchinput_grad = patchinput_grad.reshape(big_width, 3, patch_cols)
-        normed_three_grad = times_transposed(my_slots(patch_projected_grad), patch_matrix)
-        normed_three_grad = wide(tensor_sum(narrow(normed_three_grad), 6, 2))
-        patch_norm_grad, patchgain_grad = norm_back(
-            wide(jnp.pad(rows_here, wide_pad)), patch_gain, normed_three_grad
-        )
-        rows_grad = narrow(wide(my_slots(branch_grad[:, :width])) + patch_norm_grad[:, :width])
-
-    with jax.named_scope("byte_feed_back"):
-        feed_grad = narrow(
-            jnp.where(
-                boundary[:, None] == 1,
-                transposed_times(send_map, rows_grad),
-                wide(cotangent),
-            )
-        )
-        activated_grad = times_transposed(feed_grad, byte_down)
-        gate_grad = narrow(gelu_back(gate_pre, activated_grad))
-        bytedown_grad = transposed_times(activated, feed_grad)
-        byteup_grad = transposed_times(normed_two, gate_grad)
-        feed_pack = narrow(jnp.concatenate([byteup_grad, bytedown_grad], axis=1))
-        normed_two_part = narrow(times_transposed(gate_grad, byte_up))
-        feed_pack, normed_two_part = lax.optimization_barrier((feed_pack, normed_two_part))
-        normed_two_grad = wide(tensor_sum(normed_two_part, 7, 2))
-        feed_norm_grad, bytegain_grad = norm_back(after_attend, byte_gain, normed_two_grad)
-        after_attend_grad = wide(feed_grad) + feed_norm_grad
-
-    with jax.named_scope("byte_attend_back"):
-        attend_branch_grad = narrow(after_attend_grad)
-        attendoutput_grad = product(mixed_heads, attend_branch_grad)
-        mixed_heads_grad = narrow(times_transposed(attend_branch_grad, attend_output))
-        query_grad, key_grad, value_grad = attend_backward(
-            window_low, window_log, queries, mixed_heads_grad, keys, values, window_span, query_rows
-        )
-        pair_grad = jnp.concatenate([key_grad, value_grad], axis=1)
-        own_grad = wide(pair_grad[WIN:])
-        begin_row = WIN
-        for step, need_rows in enumerate(need_list):
-            begin_row = begin_row - need_rows
-            returned = from_behind(pair_grad[begin_row : begin_row + need_rows], "seq", -step - 1)
-            own_grad = own_grad.at[tok_rows - need_rows :].add(wide(returned))
-        projected_grad = jnp.concatenate([query_grad, narrow(own_grad)], axis=1)
-        attendinput_grad = transposed_times(normed, projected_grad)
-        normed_grad = wide(tensor_sum(narrow(times_transposed(projected_grad, in_matrix)), 8, 2))
-        stream_norm_grad, attendgain_grad = norm_back(stream_value, attend_gain, normed_grad)
-        inflow = narrow(after_attend_grad + stream_norm_grad)
+        result = narrow(after_attend + wide(tensor_sum(narrow(result_part), 9, 4)))
 
     with jax.named_scope("weight_sums"):
-
-        def seq_sum(pieces):
-            part = lax.psum_scatter(pieces, "seq", scatter_dimension=0, tiled=True)
-            return wide(lax.all_gather(part, "seq", axis=0, tiled=True))
-
-        feed_sum = seq_sum(feed_pack)
+        feed_sum = lax.all_gather(feed_part_sum, "seq", axis=0, tiled=True)
+        attend_part = lax.psum_scatter(attend_pack, "seq", scatter_dimension=0, tiled=True)
+        feed_sum, attend_part = together(feed_sum, attend_part)
+        feed_sum = wide(feed_sum)
         hidden = byte_up.shape[1]
         byteup_grad = feed_sum[:, :hidden]
         bytedown_grad = feed_sum[:, hidden:]
         gains = jnp.concatenate([attendgain_grad, bytegain_grad, patchgain_grad, densegain_grad])
-        gain_cols = gains.shape[0] // width
-        gains = jnp.pad(gains.reshape(gain_cols, width).T, ((0, 0), (0, 128 - gain_cols)))
-        attend_sum = seq_sum(
-            narrow(jnp.concatenate([attendinput_grad, attendoutput_grad.T, gains], axis=1))
-        )
+        gains = gains.reshape(-1, width)
+        gain_rows = gains.shape[0]
+        gains = narrow(jnp.pad(gains, ((0, 16 - gain_rows), (0, 0))))
+        attend_sum = lax.all_gather(
+            jnp.concatenate([attend_part, gains], axis=0), "seq", axis=0, tiled=True
+        )
+        attend_sum = wide(attend_sum).reshape(seq_devices, -1, width)
+        part_rows = attend_part.shape[0]
+        gains = jnp.sum(attend_sum[:, part_rows : part_rows + gain_rows], axis=0).reshape(-1)
+        attend_sum = attend_sum[:, :part_rows].reshape(width, width)
         attendinput_grad = attend_sum[:, : 3 * head_cols].reshape(width, 3, head_cols)
-        attendoutput_grad = attend_sum[:, 3 * head_cols : 4 * head_cols].T
-        gains = attend_sum[:, 4 * head_cols : 4 * head_cols + gain_cols].T.reshape(-1)
+        attendoutput_grad = attend_sum[:, 3 * head_cols :].T
         attendgain_grad = gains[:width]
         bytegain_grad = gains[width : 2 * width]
         patchgain_grad = gains[2 * width : 2 * width + big_width]

time: 665 us -> 591 us (0.89)
  waiting for transfers between devices: 143 us -> 71.7 us
  Pallas kernels: 269 us -> 248 us
  local copies, waits for them, and re-layouts: 63.4 us -> 74.1 us
    reduce_scatter x2 -> x0, waiting for transfers between devices: 37.2 us -> none  [seq_sum(): part = lax.psum_scatter(pieces, 'seq', scatter_dimension=0, tiled=True)]
    all_gather x3 -> x4, waiting for transfers between devices: 71.6 us -> 38.1 us  [the longest x1 17.9 us: on_device(): lax.all_gather(jnp.concatenate([attend_part, gains], axis=0), 'seq', axis...]
    pallas_call x2, Pallas kernels: 51 us -> 38.1 us  [attend_backward(): pl.pallas_call(functools.partial(backward_body, *args, upright), grid=gri...]
    pallas_call x2, Pallas kernels: 42 us -> 31.7 us  [attend_forward(): pl.pallas_call(functools.partial(forward_body, *args, upright), grid=grid...]
    pallas_call x6 -> x7, Pallas kernels: 101 us -> 110 us  [tensor_sum(): pl.pallas_call(functools.partial(tensor_sum_body, chunks), in_specs=[pl.B...]
    psum x1 -> x0, waiting for transfers between devices: 7.14 us -> none  [on_device(): lax.psum(narrow(result_part), 'tensor')]
    pallas_call x2, Pallas kernels: 62.4 us -> 55.4 us  [seq_gather(): pl.pallas_call(functools.partial(seq_gather_body, count), in_specs=[pl.Bl...]
    dot_general x32 -> x35, matrix products: 115 us -> 121 us  [contract(): lax.dot_general(left_side, right_side, (((left_axis,), (right_axis,)), ((...]
  transfers between devices with their start and end apart: 12 -> 12, of which waited for: 6 -> 6; matrix products, arithmetic and copies ran while one was open for 21% -> 26% of each run, Pallas kernels for 36% -> 37%
where the time goes in v3:
time: 591 us; the launch traced here: 583 us
  Pallas kernels  248 us (42%)
  matrix products  121 us (20%)
  local copies, waits for them, and re-layouts  74.1 us (13%)
  waiting for transfers between devices  71.7 us (12%)
  other arithmetic  37 us (6%)
  between operations  17.9 us (3%)
  starting transfers between devices  13 us (2%)
    dot_general x35, matrix products, contract(): lax.dot_general(left_side, right_side, (((left_axis,), (right_axis,)), ((...  121 us
    pallas_call x7, Pallas kernels, tensor_sum(): pl.pallas_call(functools.partial(tensor_sum_body, chunks), in_specs=[pl.B...  110 us
    pallas_call x2, Pallas kernels, seq_gather(): pl.pallas_call(functools.partial(seq_gather_body, count), in_specs=[pl.Bl...  55.4 us
    unnamed x202, local copies, waits for them, and re-layouts  49.6 us
    pallas_call x2, Pallas kernels, attend_backward(): pl.pallas_call(functools.partial(backward_body, *args, upright), grid=gri...  38.1 us
    ppermute x4, waiting for transfers between devices, from_behind(): lax.ppermute(value, axis, [(source, source + steps) for source in range(i...  32.5 us
    pallas_call x2, Pallas kernels, attend_forward(): pl.pallas_call(functools.partial(forward_body, *args, upright), grid=grid...  31.7 us
    all_gather x1, waiting for transfers between devices, on_device(): lax.all_gather(jnp.concatenate([attend_part, gains], axis=0), 'seq', axis...  17.9 us
  transfers between devices with their start and end apart: 12, of which 6 were waited for; matrix products, arithmetic and copies ran while one was open for 26% of the time, Pallas kernels for 37%

profile of v3, /device:TPU:0, one launch (start us, length us, event | category | flops | bytes accessed | tf_op | source)
XLA Modules:
  0.0 583.2 jit_solution(1623170273328473034)
XLA Ops:
  14.2 5.8 collective-permute-start.1
  32.7 6.0 %copy.86 = bf16[1536,3,384]{0,2,1:T(8,128)(2,1)} copy(bf16[1536,3,384]{2,0,1:T(8,128)(2,1)} %param.33) | data formatting | bytes 7077888 | tf_op args[11]
  47.1 14.7 %attend_forward.2 = (bf16[192,1024]{1,0:T(8,128)(2,1)S(1)}, f32[1,3,1024]{2,1,0:T(4,128)S(1)}) custom-call(s32[4]{0:T(128)S(1)} %broadcast_42_counts.2.counts, s32[1,1024]{1,0:T(1,128)S(1)} %add_maximum_fusion.low, bf16[1024,192]{1,0:T(8,128)(2,1)S(1)} %slice.172.queries, bf16[2560,192]{1,0:T(8,128)(2,1)S(1)} %get-tuple-element.206.keys, ...), custom_call_target="tpu_custom_call" | custom-call | flops 11274289152 | bytes 1048576 | tf_op jit(solution)/shard_map/byte_attend/attend_forward/pallas_call | solution.py:466
  61.8 12.6 %tensor_gather.1 = bf16[768,1024]{1,0:T(8,128)(2,1)S(1)} custom-call(bf16[192,1024]{1,0:T(8,128)(2,1)S(1)} %get-tuple-element.76.block.mixed), custom_call_target="tpu_custom_call" | custom-call | tf_op jit(solution)/shard_map/byte_attend/tensor_gather/pallas_call | solution.py:229
  84.9 9.5 %tensor_sum.7 = bf16[256,768]{1,0:T(8,128)(2,1)S(1)} custom-call(bf16[256,768]{1,0:T(8,128)(2,1)S(1)} %convolution_convert_fusion.12.part), custom_call_target="tpu_custom_call" | custom-call | tf_op jit(solution)/shard_map/patch_rows/tensor_sum/pallas_call | solution.py:163
  95.7 35.2 %seq_gather.2 = bf16[2048,768]{1,0:T(8,128)(2,1)S(1)} custom-call(bf16[256,768]{1,0:T(8,128)(2,1)S(1)} %fusion.48.block), custom_call_target="tpu_custom_call" | custom-call | tf_op jit(solution)/shard_map/patch_rows/seq_gather/pallas_call | solution.py:331
  132.6 5.6 fusion.38
  140.3 6.8 %convolution_convert_fusion = bf16[1024,1152]{1,0:T(8,128)(2,1)S(1)} fusion(bf16[1536,1152]{0,1:T(8,128)(2,1)} %bitcast.71, bf16[1024,768]{1,0:T(8,128)(2,1)} %copy-done.49, f32[1536]{0:T(1024)S(1)} %copy-done.76, f32[1024]{0:T(1024)S(1)} %add_rsqrt_fusion), kind=kOutput, calls=%fused_computation.36 | convolution fusion | flops 3631349760 | bytes 7481344 | tf_op jit(solution)/shard_map/patch_attend/dot_general | solution.py:48
  147.3 17.0 %attend_forward.3 = (bf16[1024,384]{1,0:T(8,128)(2,1)S(1)}, f32[3,2,1024]{2,1,0:T(2,128)S(1)}) custom-call(s32[4]{0:T(128)S(1)} %fusion.109.counts, s32[1,1024]{1,0:T(1,128)S(1)} %bitcast.69, bf16[1024,384]{1,0:T(8,128)(2,1)S(1)} %get-tuple-element.204.queries, bf16[1024,384]{1,0:T(8,128)(2,1)S(1)} %get-tuple-element.203.keys, ...), custom_call_target="tpu_custom_call" | custom-call | flops 12884901888 | bytes 1048576 | tf_op jit(solution)/shard_map/patch_attend/attend_forward/pallas_call | solution.py:466
  164.8 9.5 %tensor_sum.8 = bf16[128,1536]{1,0:T(8,128)(2,1)S(1)} custom-call(bf16[128,1536]{1,0:T(8,128)(2,1)S(1)} %convolution_convert_fusion.3.part), custom_call_target="tpu_custom_call" | custom-call | tf_op jit(solution)/shard_map/patch_attend/tensor_sum/pallas_call | solution.py:163
  179.0 5.9 %all-gather.11.cloned.1.call-done = bf16[2048,384]{1,0:T(8,128)(2,1)} async-done(((bf16[256,384]{1,0:T(8,128)(2,1)}), bf16[2048,384]{1,0:T(8,128)(2,1)}) %all-gather.11.cloned.1.call-update) | async-done | bytes 1572880 | tf_op jit(solution)/shard_map/cotangent_rows/all_gather | solution.py:635
  196.3 5.9 %convolution_convert_fusion.2.part = bf16[128,1536]{1,0:T(8,128)(2,1)} fusion(bf16[1536,1536]{1,0:T(8,128)(2,1)} %param.36, f32[128,1536]{1,0:T(8,128)} %fusion.142, bf16[1536,768]{1,0:T(8,128)(2,1)S(1)} %copy-done, bf16[128,384]{1,0:T(8,128)(2,1)} %copy-done.55, bf16[128,384]{1,0:T(8,128)(2,1)} %convolution_convert_fusion.17), kind=kOutput, calls=%fused_computation.67 | convolution fusion | flops 910491648 | bytes 8454144 | tf_op jit(solution)/shard_map/patch_dense/dot_general | solution.py:48
  203.2 9.5 %tensor_sum.9 = bf16[128,1536]{1,0:T(8,128)(2,1)S(1)} custom-call(bf16[128,1536]{1,0:T(8,128)(2,1)S(1)} %copy-done.21), custom_call_target="tpu_custom_call" | custom-call | tf_op jit(solution)/shard_map/patch_dense/tensor_sum/pallas_call | solution.py:163
  216.6 20.3 %seq_gather.3 = bf16[1024,1536]{1,0:T(8,128)(2,1)S(1)} custom-call(bf16[128,1536]{1,0:T(8,128)(2,1)S(1)} %fusion.65.block), custom_call_target="tpu_custom_call" | custom-call | tf_op jit(solution)/shard_map/patch_dense/seq_gather/pallas_call | solution.py:331
  244.9 19.8 %attend_backward.2 = (bf16[1024,384]{1,0:T(8,128)(2,1)S(1)}, bf16[1024,384]{1,0:T(8,128)(2,1)S(1)}, bf16[1024,384]{1,0:T(8,128)(2,1)S(1)}) custom-call(s32[4]{0:T(128)S(1)} %fusion.109.counts, s32[1,1024]{1,0:T(1,128)S(1)} %bitcast.70, f32[3,2,1024]{2,1,0:T(2,128)S(1)} %copy-done.26, bf16[1024,384]{1,0:T(8,128)(2,1)S(1)} %copy-done.18, ...), custom_call_target="tpu_custom_call" | custom-call | flops 16106127360 | bytes 1048576 | tf_op jit(solution)/shard_map/patch_attend_back/attend_backward/pallas_call | solution.py:487
  268.8 14.0 %tensor_sum.10 = bf16[256,1536]{1,0:T(8,128)(2,1)S(1)} custom-call(bf16[256,1536]{1,0:T(8,128)(2,1)S(1)} %convolution_convert_fusion.1.part), custom_call_target="tpu_custom_call" | custom-call | tf_op jit(solution)/shard_map/patch_attend_back/tensor_sum/pallas_call | solution.py:163
  298.1 4.3 copy.97
  303.9 22.5 %tensor_sum.11 = bf16[1024,768]{1,0:T(8,128)(2,1)S(1)} custom-call(bf16[1024,768]{1,0:T(8,128)(2,1)S(1)} %copy-done.6), custom_call_target="tpu_custom_call" | custom-call | tf_op jit(solution)/shard_map/byte_feed_back/tensor_sum/pallas_call | solution.py:163
  335.7 18.3 %attend_backward.3 = (bf16[1024,192]{1,0:T(8,128)(2,1)S(1)}, bf16[2560,192]{1,0:T(8,128)(2,1)S(1)}, bf16[2560,192]{1,0:T(8,128)(2,1)S(1)}) custom-call(s32[4]{0:T(128)S(1)} %broadcast_42_counts.2.counts, s32[1,1024]{1,0:T(1,128)S(1)} %add_maximum_fusion.low, f32[1,3,1024]{2,1,0:T(4,128)S(1)} %copy-done.28, bf16[1024,192]{1,0:T(8,128)(2,1)S(1)} %copy-done.20, ...), custom_call_target="tpu_custom_call" | custom-call | flops 14092861440 | bytes 1048576 | tf_op jit(solution)/shard_map/byte_attend_back/attend_backward/pallas_call | solution.py:487
  358.9 19.1 %collective-permute-done.2 = bf16[1024,384]{1,0:T(8,128)(2,1)S(1)} collective-permute-done((bf16[1024,384]{1,0:T(8,128)(2,1)S(1)}, bf16[1024,384]{1,0:T(8,128)(2,1)S(1)}, u32[]{:S(2)}, u32[]{:S(2)}) %collective-permute-start.2) | collective-permute-done | bytes 786464 | tf_op jit(solution)/shard_map/byte_attend_back/ppermute | solution.py:26
  379.3 13.4 %collective-permute-done.3 = bf16[512,384]{1,0:T(8,128)(2,1)S(1)} collective-permute-done((bf16[512,384]{1,0:T(8,128)(2,1)S(1)}, bf16[512,384]{1,0:T(8,128)(2,1)S(1)}, u32[]{:S(2)}, u32[]{:S(2)}) %collective-permute-start.3) | collective-permute-done | bytes 393248 | tf_op jit(solution)/shard_map/byte_attend_back/ppermute | solution.py:26
  405.8 9.2 %fusion.43 = f32[1536,1152]{0,1:T(8,128)} fusion(bf16[1024,1152]{1,0:T(8,128)(2,1)} %copy-done.42, bf16[1024,768]{1,0:T(8,128)(2,1)} %copy-done.49, f32[1536]{0:T(1024)} %param.32, f32[1024]{0:T(1024)} %copy-done.83), kind=kOutput, calls=%fused_computation.92 | convolution fusion | flops 3630170112 | bytes 11020288 | tf_op jit(solution)/shard_map/patch_attend_back/dot_general | solution.py:48
  414.9 8.1 %copy.93 = f32[1536,3,384]{2,0,1:T(8,128)} copy(f32[1536,3,384]{0,2,1:T(8,128)} %bitcast.77) | data formatting | bytes 14155776
  423.1 4.8 fusion.143
  428.8 10.6 %multiply_convert_fusion = (bf16[1024,1536]{1,0:T(8,128)(2,1)S(1)}, f32[1024,1536]{1,0:T(8,128)}) fusion(bf16[1024,1536]{1,0:T(8,128)(2,1)} %all-gather.13.cloned.1.call-done, bf16[1536,1536]{1,0:T(8,128)(2,1)} %param.36), kind=kOutput, calls=%fused_computation.18 | convolution fusion | flops 4845993984 | bytes 17301504 | tf_op jit(solution)/shard_map/dense_weights/dot_general | solution.py:48
  448.2 22.5 %tensor_sum.12 = bf16[1024,768]{1,0:T(8,128)(2,1)S(1)} custom-call(bf16[1024,768]{1,0:T(8,128)(2,1)S(1)} %copy-done.3), custom_call_target="tpu_custom_call" | custom-call | tf_op jit(solution)/shard_map/result/tensor_sum/pallas_call | solution.py:163
  477.7 4.5 fusion.51
  482.2 22.6 %tensor_sum.13 = bf16[1024,768]{1,0:T(8,128)(2,1)S(1)} custom-call(bf16[1024,768]{1,0:T(8,128)(2,1)S(1)} %copy-done.5), custom_call_target="tpu_custom_call" | custom-call | tf_op jit(solution)/shard_map/byte_attend_back/tensor_sum/pallas_call | solution.py:163
  508.8 14.3 %all-gather.15.cloned.1.call-done = bf16[768,1536]{1,0:T(8,128)(2,1)} async-done(((bf16[96,1536]{1,0:T(8,128)(2,1)}), bf16[768,1536]{1,0:T(8,128)(2,1)}) %all-gather.15.cloned.1.call-update) | async-done | bytes 2359312 | tf_op jit(solution)/shard_map/weight_sums/all_gather | solution.py:800
  524.1 17.0 %fusion.36 = f32[1536,1536]{1,0:T(8,128)} fusion(bf16[1024,1536]{1,0:T(8,128)(2,1)} %all-gather.13.cloned.1.call-done, f32[1024,1536]{1,0:T(8,128)} %get-tuple-element.215, bf16[1536,768]{1,0:T(8,128)(2,1)S(1)} %copy-done, bf16[1024,384]{0,1:T(8,128)(2,1)} %copy-done.95, bf16[1024,384]{0,1:T(8,128)(2,1)} %copy-done.96), kind=kOutput, calls=%fused_computation.64 | convolution fusion | flops 7282360320 | bytes 22806528 | tf_op jit(solution)/shard_map/dense_weights/dot_general | solution.py:48
  541.1 5.1 fusion.33
  548.7 17.9 %all-gather.17.cloned.1.call-done = bf16[896,768]{1,0:T(8,128)(2,1)} async-done(((bf16[112,768]{1,0:T(8,128)(2,1)}), bf16[896,768]{1,0:T(8,128)(2,1)}) %all-gather.17.cloned.1.call-update) | async-done | bytes 1376272 | tf_op jit(solution)/shard_map/weight_sums/all_gather | solution.py:811
  (336 shorter events, 152.9 us)
Async XLA Ops:
  7.2 189.1 %copy-start = (bf16[1536,768]{1,0:T(8,128)(2,1)S(1)}, bf16[1536,768]{1,0:T(8,128)(2,1)}, u32[]{:S(2)}) copy-start(bf16[1536,768]{1,0:T(8,128)(2,1)} %param.37) | copy-start | bytes 7077892
  7.2 68.7 %all-gather.7.cloned.1.call-start = ((), (), s32[]{:S(2)}) async-start(), calls=%async_computation.2 | async-start | bytes 1474560 | tf_op jit(solution)/shard_map/byte_attend/all_gather | solution.py:613
  14.2 27.6 %collective-permute-start.1 = (bf16[1024,384]{1,0:T(8,128)(2,1)}, bf16[1024,384]{1,0:T(8,128)(2,1)}, u32[]{:S(2)}, u32[]{:S(2)}) collective-permute-start(bf16[1024,384]{1,0:T(8,128)(2,1)} %slice.174), channel_id=1, source_target_pairs={{0,4},{4,8},{8,12},{12,16},{16,20},{20,24},{24,28},{1,5},{5,9},{9,... | collective-permute-start | bytes 2359304 | tf_op jit(solution)/shard_map/byte_attend/ppermute | solution.py:26
  20.2 21.6 %collective-permute-start = (bf16[512,384]{1,0:T(8,128)(2,1)S(1)}, bf16[512,384]{1,0:T(8,128)(2,1)}, u32[]{:S(2)}, u32[]{:S(2)}) collective-permute-start(bf16[512,384]{1,0:T(8,128)(2,1)S(1)} %slice.173), channel_id=1, source_target_pairs={{0,8},{4,12},{8,16},{12,20},{16,24},{20,28},{1,9},{5,13},{9,17},{1... | collective-permute-start | bytes 1179656 | tf_op jit(solution)/shard_map/byte_attend/ppermute | solution.py:26
  23.6 152.8 %all-gather.9.cloned.1.call-start = ((), (), s32[]{:S(2)}) async-start(), calls=%async_computation.3 | async-start | bytes 1769472 | tf_op jit(solution)/shard_map/byte_attend/all_gather | solution.py:601
  30.8 16.4 %copy-start.19 = (bf16[1024,192]{1,0:T(8,128)(2,1)}, bf16[1024,192]{1,0:T(8,128)(2,1)S(1)}, u32[]{:S(2)}) copy-start(bf16[1024,192]{1,0:T(8,128)(2,1)S(1)} %slice.172.queries) | copy-start | bytes 1179652
  61.8 18.0 %copy-start.27 = (f32[1,3,1024]{2,1,0:T(4,128)}, f32[1,3,1024]{2,1,0:T(4,128)S(1)}, u32[]{:S(2)}) copy-start(f32[1,3,1024]{2,1,0:T(4,128)S(1)} %get-tuple-element.79.log_total) | copy-start | bytes 36868
  75.6 109.3 %all-gather.11.cloned.1.call-start = ((), (), s32[]{:S(2)}) async-start(), calls=%async_computation.4 | async-start | bytes 1769472 | tf_op jit(solution)/shard_map/cotangent_rows/all_gather | solution.py:635
  95.1 37.5 %copy-start.81 = (s32[1024]{0:T(1024)S(1)}, s32[1024]{0:T(1024)}, u32[]{:S(2)}) copy-start(s32[1024]{0:T(1024)} %copy-done.80) | copy-start | bytes 12292
  139.8 158.3 %all-gather.13.cloned.1.call-start = ((), (), s32[]{:S(2)}) async-start(), calls=%async_computation.5 | async-start | bytes 3538944 | tf_op jit(solution)/shard_map/patch_dense/all_gather | solution.py:678
  147.3 17.1 %copy-start.14 = (bf16[1024,384]{1,0:T(8,128)(2,1)}, bf16[1024,384]{1,0:T(8,128)(2,1)S(1)}, u32[]{:S(2)}) copy-start(bf16[1024,384]{1,0:T(8,128)(2,1)S(1)} %get-tuple-element.202.values) | copy-start | bytes 2359300
  147.3 17.1 %copy-start.15 = (bf16[1024,384]{1,0:T(8,128)(2,1)}, bf16[1024,384]{1,0:T(8,128)(2,1)S(1)}, u32[]{:S(2)}) copy-start(bf16[1024,384]{1,0:T(8,128)(2,1)S(1)} %get-tuple-element.203.keys) | copy-start | bytes 2359300
  147.3 17.1 %copy-start.17 = (bf16[1024,384]{1,0:T(8,128)(2,1)}, bf16[1024,384]{1,0:T(8,128)(2,1)S(1)}, u32[]{:S(2)}) copy-start(bf16[1024,384]{1,0:T(8,128)(2,1)S(1)} %get-tuple-element.204.queries) | copy-start | bytes 2359300
  147.3 17.1 %copy-start.46 = (bf16[384,1536]{1,0:T(8,128)(2,1)S(1)}, bf16[384,1536]{1,0:T(8,128)(2,1)}, u32[]{:S(2)}) copy-start(bf16[384,1536]{1,0:T(8,128)(2,1)} %param.34) | copy-start | bytes 3538948
  212.7 24.2 %copy-start.47 = (bf16[384,1536]{1,0:T(8,128)(2,1)S(1)}, bf16[384,1536]{1,0:T(8,128)(2,1)}, u32[]{:S(2)}) copy-start(bf16[384,1536]{1,0:T(8,128)(2,1)} %param.34) | copy-start | bytes 3538948
  239.6 155.2 %reduce-scatter.7.cloned.1.call-start = ((), (), s32[]{:S(2)}) async-start(), calls=%async_computation.8 | async-start | bytes 2654208
  267.5 15.4 %copy-start.77 = (f32[1536]{0:T(1024)S(1)}, f32[1536]{0:T(1024)}, u32[]{:S(2)}) copy-start(f32[1536]{0:T(1024)} %param.32) | copy-start | bytes 18436
  267.5 16.0 %copy-start.50 = (bf16[1024,768]{1,0:T(8,128)(2,1)S(1)}, bf16[1024,768]{1,0:T(8,128)(2,1)}, u32[]{:S(2)}) copy-start(bf16[1024,768]{1,0:T(8,128)(2,1)} %param.23) | copy-start | bytes 4718596
  302.4 205.3 %reduce-scatter.9.cloned.1.call-start = ((), (), s32[]{:S(2)}) async-start(), calls=%async_computation.9 | async-start | bytes 1327104
  303.9 22.6 %copy-start.31 = (f32[1024,768]{1,0:T(8,128)S(1)}, f32[1024,768]{1,0:T(8,128)}, u32[]{:S(2)}) copy-start(f32[1024,768]{1,0:T(8,128)} %copy-done.29) | copy-start | bytes 9437188
  354.9 23.1 %collective-permute-start.2 = (bf16[1024,384]{1,0:T(8,128)(2,1)S(1)}, bf16[1024,384]{1,0:T(8,128)(2,1)S(1)}, u32[]{:S(2)}, u32[]{:S(2)}) collective-permute-start(bf16[1024,384]{1,0:T(8,128)(2,1)S(1)} %slice.155), channel_id=1, source_target_pairs={{4,0},{8,4},{12,8},{16,12},{20,16},{24,20},{28,24},{5,1},{9,5},{13... | collective-permute-start | bytes 2359304 | tf_op jit(solution)/shard_map/byte_attend_back/ppermute | solution.py:26
  356.4 36.3 %collective-permute-start.3 = (bf16[512,384]{1,0:T(8,128)(2,1)S(1)}, bf16[512,384]{1,0:T(8,128)(2,1)S(1)}, u32[]{:S(2)}, u32[]{:S(2)}) collective-permute-start(bf16[512,384]{1,0:T(8,128)(2,1)S(1)} %slice.157), channel_id=1, source_target_pairs={{8,0},{12,4},{16,8},{20,12},{24,16},{28,20},{9,1},{13,5},{17,9},{2... | collective-permute-start | bytes 1179656 | tf_op jit(solution)/shard_map/byte_attend_back/ppermute | solution.py:26
  379.2 18.9 %copy-start.24 = (bf16[1024,192]{1,0:T(8,128)(2,1)S(1)}, bf16[1024,192]{1,0:T(8,128)(2,1)}, u32[]{:S(2)}) copy-start(bf16[1024,192]{1,0:T(8,128)(2,1)} %copy-done.23) | copy-start | bytes 1179652
  379.2 18.9 %copy-start.62 = (f32[1024]{0:T(1024)S(1)}, f32[1024]{0:T(1024)}, u32[]{:S(2)}) copy-start(f32[1024]{0:T(1024)} %copy-done.61) | copy-start | bytes 12292
  379.2 18.9 %copy-start.67 = (f32[768]{0:T(1024)S(1)}, f32[768]{0:T(1024)}, u32[]{:S(2)}) copy-start(f32[768]{0:T(1024)} %param.26) | copy-start | bytes 9220
  405.5 117.6 %all-gather.15.cloned.1.call-start = ((), (), s32[]{:S(2)}) async-start(), calls=%async_computation.6 | async-start | bytes 2654208 | tf_op jit(solution)/shard_map/weight_sums/all_gather | solution.py:800
  428.8 137.8 %all-gather.17.cloned.1.call-start = ((), (), s32[]{:S(2)}) async-start(), calls=%async_computation.7 | async-start | bytes 1548288 | tf_op jit(solution)/shard_map/weight_sums/all_gather | solution.py:811
  448.2 22.6 %copy-start.32 = (f32[1024,768]{1,0:T(8,128)S(1)}, f32[1024,768]{1,0:T(8,128)}, u32[]{:S(2)}) copy-start(f32[1024,768]{1,0:T(8,128)} %copy-done.29) | copy-start | bytes 9437188
  482.2 23.8 %copy-start.36 = (bf16[1024,768]{1,0:T(8,128)(2,1)S(1)}, bf16[1024,768]{1,0:T(8,128)(2,1)}, u32[]{:S(2)}) copy-start(bf16[1024,768]{1,0:T(8,128)(2,1)} %param.22) | copy-start | bytes 4718596
  482.2 25.2 %copy-start.68 = (bf16[1536]{0:T(1024)(128)(2,1)S(1)}, bf16[1536]{0:T(1024)(128)(2,1)}, u32[]{:S(2)}) copy-start(bf16[1536]{0:T(1024)(128)(2,1)} %get-tuple-element.194) | copy-start | bytes 9220
  482.2 25.2 %copy-start.75 = (bf16[768]{0:T(1024)(128)(2,1)S(1)}, bf16[768]{0:T(1024)(128)(2,1)}, u32[]{:S(2)}) copy-start(bf16[768]{0:T(1024)(128)(2,1)} %get-tuple-element.188) | copy-start | bytes 4612
  524.1 17.0 %copy-start.64 = (f32[1024]{0:T(1024)S(1)}, f32[1024]{0:T(1024)}, u32[]{:S(2)}) copy-start(f32[1024]{0:T(1024)} %copy-done.63) | copy-start | bytes 12292
  (78 other events, 369.7 us)
Sparse Core Ops, SparseCore 0:
  23.8 15.9 all-gather.6
  75.7 54.6 all-gather.8
  139.9 44.9 all-gather.10
  239.7 58.3 all-gather.12
  302.5 72.8 reduce-scatter.6
  405.7 63.8 reduce-scatter.8
  472.3 50.7 all-gather.14
  525.9 40.6 all-gather.16

commit v4 on v3

--- a/solution.py
+++ b/solution.py
@@ -98,11 +98,35 @@
     )
 
 
-def tensor_sum_body(chunks, part, total, pair_got, mine, across_got, send_sem, recv_sem):
+def seq_peers(count):
+    device = lax.axis_index("seq")
+    spot = ring_spot(device, count)
+    ahead = {"seq": ring_at((spot + 1) % count, count)}
+    behind = {"seq": ring_at((spot + count - 1) % count, count)}
+    return device, spot, ahead, behind
+
+
+def ring_at(spot, count):
+    half = spot // (count // 2)
+    return (1 - half) * 2 * spot + half * (2 * (count - 1 - spot) + 1)
+
+
+def ring_spot(device, count):
+    return device // 2 + (device % 2) * (count - 1 - 2 * (device // 2))
+
+
+def run_stages(transfers, pattern):
+    for index in pattern:
+        next(transfers[index], None)
+    for transfer in transfers:
+        for unused in transfer:
+            pass
+
+
+def tensor_sum_stages(chunks, part, total, pair_got, mine, across_got, send_sem, recv_sem):
     place, pair, across = tensor_peers()
     pair_id = {"tensor": pair}
     across_id = {"tensor": across}
-    meet((pair_id, across_id))
     rows = part.shape[0] // 2
     step = rows // chunks
     core = place % 2
@@ -121,6 +145,7 @@
         )
         copy.start()
         given.append(copy)
+    yield
     far = []
     for chunk in range(chunks):
         given[chunk].wait_recv()
@@ -135,6 +160,7 @@
         )
         copy.start()
         far.append(copy)
+    yield
     back = []
     for chunk in range(chunks):
         far[chunk].wait_recv()
@@ -150,39 +176,17 @@
         )
         copy.start()
         back.append(copy)
+        yield
     for copy in back:
         copy.wait_recv()
     for copy in given + far + back:
         copy.wait_send()
 
 
-def tensor_sum(part, collective_id, chunks):
-    rows, cols = part.shape
-    half = rows // 2
-    dma = pltpu.SemaphoreType.DMA
-    return pl.pallas_call(
-        functools.partial(tensor_sum_body, chunks),
-        in_specs=[pl.BlockSpec(memory_space=pltpu.VMEM)],
-        out_specs=pl.BlockSpec(memory_space=pltpu.VMEM),
-        out_shape=jax.ShapeDtypeStruct((rows, cols), NARROW_TYPE),
-        scratch_shapes=[
-            pltpu.VMEM((half, cols), NARROW_TYPE),
-            pltpu.VMEM((half, cols), NARROW_TYPE),
-            pltpu.VMEM((half, cols), NARROW_TYPE),
-            dma((3, chunks)), dma((3, chunks)),
-        ],
-        compiler_params=pltpu.CompilerParams(
-            collective_id=collective_id, has_side_effects=True, vmem_limit_bytes=VMEM_BYTES
-        ),
-        name="tensor_sum",
-    )(part)
-
-
-def tensor_gather_body(chunks, block, out, local_sem, send_sem, recv_sem):
+def tensor_gather_stages(chunks, block, out, local_sem, send_sem, recv_sem):
     place, pair, across = tensor_peers()
     pair_id = {"tensor": pair}
     across_id = {"tensor": across}
-    meet((pair_id, across_id))
     rows = block.shape[0]
     step = rows // chunks
 
@@ -203,6 +207,7 @@
             copies.append(copy)
     local = pltpu.make_async_copy(block, out.at[pl.ds(pl.multiple_of(place * rows, 16), rows)], local_sem)
     local.start()
+    yield
     passed = []
     for chunk in range(chunks):
         copies[chunk].wait_recv()
@@ -215,6 +220,7 @@
         )
         copy.start()
         passed.append(copy)
+        yield
     local.wait()
     for chunk in range(chunks):
         copies[chunks + chunk].wait_recv()
@@ -223,58 +229,32 @@
         copy.wait_send()
 
 
-def tensor_gather(block, collective_id, chunks):
-    rows, cols = block.shape
-    dma = pltpu.SemaphoreType.DMA
-    return pl.pallas_call(
-        functools.partial(tensor_gather_body, chunks),
-        in_specs=[pl.BlockSpec(memory_space=pltpu.VMEM)],
-        out_specs=pl.BlockSpec(memory_space=pltpu.VMEM),
-        out_shape=jax.ShapeDtypeStruct((4*rows, cols), NARROW_TYPE),
-        scratch_shapes=[dma(()), dma((3, chunks)), dma((3, chunks))],
-        compiler_params=pltpu.CompilerParams(
-            collective_id=collective_id, has_side_effects=True, vmem_limit_bytes=VMEM_BYTES
-        ),
-        name="tensor_gather",
-    )(block)
-
-
-def ring_at(spot, count):
-    half = spot // (count // 2)
-    return (1 - half) * 2 * spot + half * (2 * (count - 1 - spot) + 1)
-
-
-def ring_spot(device, count):
-    return device // 2 + (device % 2) * (count - 1 - 2 * (device // 2))
-
-
-def seq_gather_body(count, block, out, local_sem, ring_send, ring_recv, pair_send, pair_recv):
-    device = lax.axis_index("seq")
+def ring_gather_stages(
+    count, shared, block, out, local_sem, ring_send, ring_recv, pair_send, pair_recv
+):
+    device, spot, ahead, behind = seq_peers(count)
     place, pair, across = tensor_peers()
-    spot = ring_spot(device, count)
-    ahead = {"seq": ring_at((spot + 1) % count, count)}
-    behind = {"seq": ring_at((spot + count - 1) % count, count)}
     pair_id = {"tensor": pair}
-    meet((ahead, behind, pair_id))
     rows = block.shape[0]
-    step = rows // 4
-    core = place % 2
+    step = rows // (4 if shared else 2)
+    first = (place % 2) * 2 * step if shared else 0
 
     def piece(owner, sub):
-        return pl.ds(pl.multiple_of(owner * rows + core * 2 * step + sub * step, 16), step)
+        return pl.ds(pl.multiple_of(owner * rows + first + sub * step, 16), step)
 
     hops = count // 2
     sends = []
     moves = {}
 
+    def owner_at(way, distance):
+        if way == 0:
+            return ring_at((spot + count - distance) % count, count)
+        return ring_at((spot + distance) % count, count)
+
     def launch(way, hop, sub):
-        distance = hop - 1
-        if way == 0:
-            owner = ring_at((spot + count - distance) % count, count)
-        else:
-            owner = ring_at((spot + distance) % count, count)
+        owner = owner_at(way, hop - 1)
         if hop == 1:
-            source = block.at[pl.ds(pl.multiple_of(core * 2 * step + sub * step, 16), step)]
+            source = block.at[pl.ds(pl.multiple_of(first + sub * step, 16), step)]
         else:
             source = out.at[piece(owner, sub)]
         copy = remote(
@@ -295,6 +275,7 @@
         block, out.at[pl.ds(pl.multiple_of(device * rows, 16), rows)], local_sem
     )
     local.start()
+    yield
     pairs = []
     for hop in range(1, hops + 1):
         for way, sub in order:
@@ -303,19 +284,18 @@
             moves[way, hop, sub].wait_recv()
             if hop + 1 < hops or (hop + 1 == hops and way == sub):
                 launch(way, hop + 1, sub)
-            if way == 0:
-                owner = ring_at((spot + count - hop) % count, count)
-            else:
-                owner = ring_at((spot + hop) % count, count)
-            copy = remote(
-                out.at[piece(owner, sub)],
-                out.at[piece(owner, sub)],
-                pair_send.at[way, hop - 1, sub],
-                pair_recv.at[way, hop - 1, sub],
-                pair_id,
-            )
-            copy.start()
-            pairs.append(copy)
+            if shared:
+                owner = owner_at(way, hop)
+                copy = remote(
+                    out.at[piece(owner, sub)],
+                    out.at[piece(owner, sub)],
+                    pair_send.at[way, hop - 1, sub],
+                    pair_recv.at[way, hop - 1, sub],
+                    pair_id,
+                )
+                copy.start()
+                pairs.append(copy)
+        yield
     local.wait()
     for copy in pairs:
         copy.wait_recv()
@@ -323,22 +303,167 @@
         copy.wait_send()
 
 
+def ring_sum_stages(count, part, shard, arrived, send_sem, recv_sem):
+    device, spot, ahead, behind = seq_peers(count)
+    rows = part.shape[0] // count
+    half = rows // 2
+    moves = {}
+
+    def piece(distance, way):
+        owner = ring_at((spot + count - distance if way == 0 else spot + distance) % count, count)
+        return pl.ds(pl.multiple_of(owner * rows + way * half, 16), half)
+
+    def launch(way, step, source):
+        copy = remote(
+            source,
+            arrived.at[way, step],
+            send_sem.at[way, step],
+            recv_sem.at[way, step],
+            (ahead, behind)[way],
+        )
+        copy.start()
+        moves[way, step] = copy
+
+    for way in range(2):
+        launch(way, 0, part.at[piece(1, way)])
+    yield
+    for step in range(count - 1):
+        for way in range(2):
+            moves[way, step].wait_recv()
+            summed = wide(part[piece(step + 2, way)]) + wide(arrived[way, step])
+            if step < count - 2:
+                arrived[way, step] = narrow(summed)
+                launch(way, step + 1, arrived.at[way, step])
+            else:
+                shard[pl.ds(way * half, half)] = narrow(summed)
+        yield
+    for copy in moves.values():
+        copy.wait_send()
+
+
+def meet_tensor(count):
+    place, pair, across = tensor_peers()
+    peers = [{"tensor": pair}, {"tensor": across}]
+    if count:
+        peers += seq_peers(count)[2:]
+    meet(peers)
+
+
+def tensor_sum_body(chunks, *refs):
+    meet_tensor(0)
+    run_stages([tensor_sum_stages(chunks, *refs)], ())
+
+
+def seq_gather_body(count, *refs):
+    device, spot, ahead, behind = seq_peers(count)
+    place, pair, across = tensor_peers()
+    meet((ahead, behind, {"tensor": pair}))
+    run_stages([ring_gather_stages(count, True, *refs)], ())
+
+
+def two_gathers_body(count, chunks, block, rows, out, all_rows, *refs):
+    meet_tensor(count)
+    run_stages(
+        [
+            ring_gather_stages(count, True, rows, all_rows, *refs[3:]),
+            tensor_gather_stages(chunks, block, out, *refs[:3]),
+        ],
+        (0, 1, 0, 1, 1, 0),
+    )
+
+
+def two_sums_body(count, chunks, part, pack, total, shard, *refs):
+    meet_tensor(count)
+    run_stages(
+        [
+            tensor_sum_stages(chunks, part, total, *refs[:5]),
+            ring_sum_stages(count, pack, shard, *refs[5:]),
+        ],
+        (0, 1, 0, 1, 1, 0, 1, 0, 1, 1, 0, 1, 0, 1),
+    )
+
+
+def sum_and_gather_body(count, chunks, part, block, total, out, *refs):
+    meet_tensor(count)
+    run_stages(
+        [
+            tensor_sum_stages(chunks, part, total, *refs[:5]),
+            ring_gather_stages(count, False, block, out, *refs[5:], None, None),
+        ],
+        (0, 1, 0, 1, 0, 1, 0, 1, 0, 1, 0),
+    )
+
+
+DMA = pltpu.SemaphoreType.DMA
+
+
+def sum_scratch(part, chunks):
+    rows, cols = part.shape
+    half = pltpu.VMEM((rows // 2, cols), NARROW_TYPE)
+    return [half, half, half, DMA((3, chunks)), DMA((3, chunks))]
+
+
+def ring_sems(count, sets):
+    return [DMA(())] + [DMA((2, count // 2, 2))] * (2 * sets)
+
+
+def exchange(body, name, collective_id, shapes, scratch, args):
+    results = pl.pallas_call(
+        body,
+        in_specs=[pl.BlockSpec(memory_space=pltpu.VMEM)] * len(args),
+        out_specs=[pl.BlockSpec(memory_space=pltpu.VMEM)] * len(shapes),
+        out_shape=[jax.ShapeDtypeStruct(shape, NARROW_TYPE) for shape in shapes],
+        scratch_shapes=scratch,
+        compiler_params=pltpu.CompilerParams(
+            collective_id=collective_id, has_side_effects=True, vmem_limit_bytes=VMEM_BYTES
+        ),
+        name=name,
+    )(*args)
+    return results[0] if len(shapes) == 1 else results
+
+
+def tensor_sum(part, collective_id, chunks):
+    body = functools.partial(tensor_sum_body, chunks)
+    scratch = sum_scratch(part, chunks)
+    return exchange(body, "tensor_sum", collective_id, [part.shape], scratch, [part])
+
+
 def seq_gather(block, collective_id):
     rows, cols = block.shape
     count = lax.axis_size("seq")
-    dma = pltpu.SemaphoreType.DMA
-    sems = dma((2, count // 2, 2))
-    return pl.pallas_call(
-        functools.partial(seq_gather_body, count),
-        in_specs=[pl.BlockSpec(memory_space=pltpu.VMEM)],
-        out_specs=pl.BlockSpec(memory_space=pltpu.VMEM),
-        out_shape=jax.ShapeDtypeStruct((count*rows, cols), NARROW_TYPE),
-        scratch_shapes=[dma(()), sems, sems, sems, sems],
-        compiler_params=pltpu.CompilerParams(
-            collective_id=collective_id, has_side_effects=True, vmem_limit_bytes=VMEM_BYTES
-        ),
-        name="seq_gather",
-    )(block)
+    body = functools.partial(seq_gather_body, count)
+    scratch = ring_sems(count, 2)
+    return exchange(body, "seq_gather", collective_id, [(count * rows, cols)], scratch, [block])
+
+
+def two_gathers(block, rows, collective_id, chunks):
+    count = lax.axis_size("seq")
+    shapes = [(4 * block.shape[0], block.shape[1]), (count * rows.shape[0], rows.shape[1])]
+    scratch = [DMA(()), DMA((3, chunks)), DMA((3, chunks))] + ring_sems(count, 2)
+    body = functools.partial(two_gathers_body, count, chunks)
+    return exchange(body, "two_gathers", collective_id, shapes, scratch, [block, rows])
+
+
+def two_sums(part, pack, collective_id, chunks):
+    count = lax.axis_size("seq")
+    rows, cols = pack.shape
+    moves = count - 1
+    scratch = sum_scratch(part, chunks) + [
+        pltpu.VMEM((2, moves, rows // count // 2, cols), NARROW_TYPE),
+        DMA((2, moves)),
+        DMA((2, moves)),
+    ]
+    body = functools.partial(two_sums_body, count, chunks)
+    shapes = [part.shape, (rows // count, cols)]
+    return exchange(body, "two_sums", collective_id, shapes, scratch, [part, pack])
+
+
+def sum_and_gather(part, block, collective_id, chunks):
+    count = lax.axis_size("seq")
+    shapes = [part.shape, (count * block.shape[0], block.shape[1])]
+    scratch = sum_scratch(part, chunks) + ring_sems(count, 1)
+    body = functools.partial(sum_and_gather_body, count, chunks)
+    return exchange(body, "sum_and_gather", collective_id, shapes, scratch, [part, block])
 
 
 def allowed_pairs(low_row, first_key, span, first_query, query_rows):
@@ -495,7 +620,9 @@
         scratch_shapes=[pltpu.VMEM((keys.shape[0], group_cols), WIDE_TYPE)] * 2,
         compiler_params=pltpu.CompilerParams(vmem_limit_bytes=VMEM_BYTES),
         cost_estimate=pl.CostEstimate(
-            flops=20 * flops, transcendentals=flops // 128, bytes_accessed=1 << 20
+            flops=(1 if upright else 20) * flops,
+            transcendentals=0 if upright else flops // 128,
+            bytes_accessed=1 << 10 if upright else 1 << 20,
         ),
         name="attend_backward",
     )(counts, low, log_total, queries, mixed, out_grads, keys, values)
@@ -597,8 +724,6 @@
             arrived_list.append(from_behind(key_value[tok_rows - need_rows :], "seq", step + 1))
         extended = jnp.concatenate(arrived_list[::-1] + [key_value], axis=0)
         delta_slots = narrow(product(send_map, cotangent))
-        extended, first_half = together(extended, delta_slots[:, : width // 2])
-        slot_halves = [lax.all_gather(first_half, "seq", axis=0, tiled=True)]
         keys = extended[:, :head_cols]
         values = extended[:, head_cols:]
         window_low = jnp.maximum(
@@ -609,7 +734,7 @@
         mixed_heads, window_log = attend_forward(
             window_counts, window_low, queries, keys, values, window_spans, query_rows, True
         )
-        all_mixed = tensor_gather(mixed_heads, 0, 2)
+        all_mixed, all_slots = two_gathers(mixed_heads, delta_slots, 0, 2)
         all_output = lax.all_gather(attend_output, "tensor", axis=0, tiled=True)
         after_attend = stream_value + transposed_times(all_mixed, all_output)
 
@@ -622,20 +747,14 @@
     with jax.named_scope("patch_rows"):
         attend_high = narrow(after_attend)
         attend_rest = narrow(after_attend - wide(attend_high))
-        rows_sum = wide(tensor_sum(narrow(product(send_map, feed_part)), 1, 2))
+        rows_sum = wide(tensor_sum(narrow(product(send_map, feed_part)), 1, 4))
         rows_here = narrow(
             product(send_map, attend_high) + product(send_map, attend_rest) + rows_sum
         )
-        gathered_rows, second_half = together(
-            seq_gather(rows_here, 2), delta_slots[:, width // 2 :]
-        )
-        byte_rows = compact(gathered_rows)
+        byte_rows = compact(seq_gather(rows_here, 2))
 
     with jax.named_scope("cotangent_rows"):
-        slot_halves.append(lax.all_gather(second_half, "seq", axis=0, tiled=True))
-        delta_own = jnp.concatenate(
-            [compact_rows(half, device * owned_rows, owned_rows) for half in slot_halves], axis=1
-        )
+        delta_own = compact_rows(all_slots, device * owned_rows, owned_rows)
 
     wide_pad = ((0, 0), (0, big_width - width))
     with jax.named_scope("patch_attend"):
@@ -663,7 +782,7 @@
             patch_query_rows,
             False,
         )
-        branch_own = wide(tensor_sum(narrow(product(my_block(mixed_patch), patch_output)), 3, 2))
+        branch_own = wide(tensor_sum(narrow(product(my_block(mixed_patch), patch_output)), 3, 4))
 
     with jax.named_scope("patch_dense"):
         own_rows = wide(jnp.pad(my_block(byte_rows), wide_pad))
@@ -671,14 +790,13 @@
         normed_four = narrow(rms_scale(after_patch, dense_gain))
         dense_pre = product(normed_four, dense_up)
         dense_pre_grad = narrow(gelu_back(dense_pre, times_transposed(delta_own, dense_down)))
-        normed_four_grad = wide(tensor_sum(narrow(times_transposed(dense_pre_grad, dense_up)), 4, 2))
+        normed_four_grad = wide(tensor_sum(narrow(times_transposed(dense_pre_grad, dense_up)), 4, 4))
         after_patch_grad, densegain_grad = norm_back(after_patch, dense_gain, normed_four_grad)
         branch_grad_own = narrow(after_patch_grad + wide(jnp.pad(delta_own, wide_pad)))
         branch_grad, normed_later = together(seq_gather(branch_grad_own, 5), normed_four)
         all_normed = lax.all_gather(normed_later, "seq", axis=0, tiled=True)
 
     with jax.named_scope("patch_attend_back"):
-        patchoutput_grad = transposed_times(mixed_patch, branch_grad)
         mixed_patch_grad = narrow(times_transposed(branch_grad, patch_output))
         patch_projected_grad = jnp.concatenate(
             attend_backward(
@@ -696,10 +814,8 @@
             ),
             axis=1,
         )
-        patchinput_grad = transposed_times(normed_three, patch_projected_grad)
-        patchinput_grad = patchinput_grad.reshape(big_width, 3, patch_cols)
         normed_three_grad = times_transposed(my_slots(patch_projected_grad), patch_matrix)
-        normed_three_grad = wide(tensor_sum(narrow(normed_three_grad), 6, 2))
+        normed_three_grad = wide(tensor_sum(narrow(normed_three_grad), 6, 4))
         patch_norm_grad, patchgain_grad = norm_back(
             wide(jnp.pad(rows_here, wide_pad)), patch_gain, normed_three_grad
         )
@@ -743,78 +859,104 @@
             True,
         )
         pair_grad = jnp.concatenate([key_grad, value_grad], axis=1)
-        pair_grad, all_normed, delta_halves = together(pair_grad, all_normed, tuple(slot_halves))
-        own_grad = wide(pair_grad[WIN:])
+        pair_grad, all_normed, later_slots, later_branch, later_projected = together(
+            pair_grad, all_normed, all_slots, branch_grad, patch_projected_grad
+        )
+        patchoutput_grad = transposed_times(mixed_patch, later_branch)
+        patchinput_grad = transposed_times(normed_three, later_projected)
+        patchinput_grad = patchinput_grad.reshape(big_width, 3, patch_cols)
         begin_row = WIN
+        returned_list = []
         for step, need_rows in enumerate(need_list):
             begin_row = begin_row - need_rows
-            returned = from_behind(pair_grad[begin_row : begin_row + need_rows], "seq", -step - 1)
+            returned_list.append(
+                from_behind(pair_grad[begin_row : begin_row + need_rows], "seq", -step - 1)
+            )
+
+    with jax.named_scope("dense_weights"):
+        block_rows = min(1024, total_rows)
+
+        delta_grad = compact(later_slots)
+        delta_grad, patchoutput_grad, patchinput_grad, feed_part_sum = together(
+            delta_grad, patchoutput_grad, patchinput_grad, feed_part_sum
+        )
+
+        def dense_parts(first_row):
+            some_normed = lax.dynamic_slice_in_dim(all_normed, first_row, block_rows, 0)
+            some_delta = lax.dynamic_slice_in_dim(delta_grad, first_row, block_rows, 0)
+            some_pre = product(some_normed, dense_up)
+            some_act = narrow(gelu_tanh(some_pre))
+            some_grad = narrow(gelu_back(some_pre, times_transposed(some_delta, dense_down)))
+            return some_normed, some_delta, some_act, some_grad
+
+        if total_rows == block_rows:
+            some_normed, some_delta, dense_act, dense_grad = dense_parts(0)
+            densedown_grad = transposed_times(dense_act, some_delta)
+            denseup_grad = transposed_times(some_normed, dense_grad)
+        else:
+
+            def dense_step(sums, first_row):
+                some_normed, some_delta, some_act, some_grad = dense_parts(first_row)
+                down_sum = sums[0] + transposed_times(some_act, some_delta)
+                up_sum = sums[1] + transposed_times(some_normed, some_grad)
+                return (down_sum, up_sum), some_act
+
+            starts = jnp.arange(total_rows // block_rows, dtype=jnp.int32) * block_rows
+            initial = (jnp.zeros(dense_down.shape), jnp.zeros(dense_up.shape))
+            (densedown_grad, denseup_grad), dense_act = lax.scan(dense_step, initial, starts)
+            dense_act = dense_act.reshape(total_rows, -1)
+
+        returned_list, dense_act, densedown_grad, denseup_grad = together(
+            returned_list, dense_act, densedown_grad, denseup_grad
+        )
+
+    with jax.named_scope("byte_attend_sum"):
+        own_grad = wide(pair_grad[WIN:])
+        for need_rows, returned in zip(need_list, returned_list):
             own_grad = own_grad.at[tok_rows - need_rows :].add(wide(returned))
-        own_grad, feed_part_sum = together(own_grad, feed_part_sum)
         projected_grad = jnp.concatenate([query_grad, narrow(own_grad)], axis=1)
         attendinput_grad = transposed_times(normed, projected_grad)
         attend_pack = narrow(jnp.concatenate([attendinput_grad, attendoutput_grad.T], axis=1))
         normed_part = narrow(times_transposed(projected_grad, in_matrix))
         attend_pack, normed_part = together(attend_pack, normed_part)
-        normed_grad = wide(tensor_sum(normed_part, 8, 4))
+        pack_rows = width // seq_devices
+        ring_fits = pack_rows % 32 == 0
+        if ring_fits:
+            normed_grad, attend_part = two_sums(normed_part, attend_pack, 8, 4)
+        else:
+            normed_grad = tensor_sum(normed_part, 8, 4)
+            attend_part = lax.psum_scatter(attend_pack, "seq", scatter_dimension=0, tiled=True)
+        normed_grad = wide(normed_grad)
         stream_norm_grad, attendgain_grad = norm_back(stream_value, attend_gain, normed_grad)
         inflow = narrow(after_attend_grad + stream_norm_grad)
-
-    with jax.named_scope("dense_weights"):
-        block_rows = min(1024, total_rows)
-
-        delta_grad = jnp.concatenate([compact(half) for half in delta_halves], axis=1)
-
-        def dense_block(first_row):
-            some_normed = lax.dynamic_slice_in_dim(all_normed, first_row, block_rows, 0)
-            some_delta = lax.dynamic_slice_in_dim(delta_grad, first_row, block_rows, 0)
-            some_pre = product(some_normed, dense_up)
-            some_act = narrow(gelu_tanh(some_pre))
-            some_grad = narrow(gelu_back(some_pre, times_transposed(some_delta, dense_down)))
-            return (
-                some_act,
-                transposed_times(some_act, some_delta),
-                transposed_times(some_normed, some_grad),
-            )
-
-        if total_rows == block_rows:
-            dense_act, densedown_grad, denseup_grad = dense_block(0)
-        else:
-
-            def dense_step(sums, first_row):
-                some_act, down_part, up_part = dense_block(first_row)
-                return (sums[0] + down_part, sums[1] + up_part), some_act
-
-            starts = jnp.arange(total_rows // block_rows, dtype=jnp.int32) * block_rows
-            initial = (jnp.zeros(dense_down.shape), jnp.zeros(dense_up.shape))
-            (densedown_grad, denseup_grad), dense_act = lax.scan(dense_step, initial, starts)
-            dense_act = dense_act.reshape(total_rows, -1)
 
     with jax.named_scope("result"):
         delta_part = product(my_slots(mixed_patch), patch_output[:, :width])
         delta_part = narrow(delta_part + product(my_slots(dense_act), dense_down))
         result_part = wide(feed_part) + transposed_times(send_map, delta_part)
-        result = narrow(after_attend + wide(tensor_sum(narrow(result_part), 9, 4)))
+        gains = jnp.concatenate([attendgain_grad, bytegain_grad, patchgain_grad, densegain_grad])
+        gains = gains.reshape(-1, width)
+        gain_rows = gains.shape[0]
+        gains = narrow(jnp.pad(gains, ((0, 32 - gain_rows), (0, 0))))
+        attend_block = jnp.concatenate([attend_part, gains], axis=0)
+        result_part, feed_sum = together(
+            narrow(result_part), lax.all_gather(feed_part_sum, "seq", axis=0, tiled=True)
+        )
+        if ring_fits:
+            result_sum, attend_sum = sum_and_gather(result_part, attend_block, 9, 4)
+        else:
+            result_sum = tensor_sum(result_part, 9, 4)
+            attend_sum = lax.all_gather(attend_block, "seq", axis=0, tiled=True)
+        result = narrow(after_attend + wide(result_sum))
 
     with jax.named_scope("weight_sums"):
-        feed_sum = lax.all_gather(feed_part_sum, "seq", axis=0, tiled=True)
-        attend_part = lax.psum_scatter(attend_pack, "seq", scatter_dimension=0, tiled=True)
-        feed_sum, attend_part = together(feed_sum, attend_part)
         feed_sum = wide(feed_sum)
         hidden = byte_up.shape[1]
         byteup_grad = feed_sum[:, :hidden]
         bytedown_grad = feed_sum[:, hidden:]
-        gains = jnp.concatenate([attendgain_grad, bytegain_grad, patchgain_grad, densegain_grad])
-        gains = gains.reshape(-1, width)
-        gain_rows = gains.shape[0]
-        gains = narrow(jnp.pad(gains, ((0, 16 - gain_rows), (0, 0))))
-        attend_sum = lax.all_gather(
-            jnp.concatenate([attend_part, gains], axis=0), "seq", axis=0, tiled=True
-        )
         attend_sum = wide(attend_sum).reshape(seq_devices, -1, width)
-        part_rows = attend_part.shape[0]
-        gains = jnp.sum(attend_sum[:, part_rows : part_rows + gain_rows], axis=0).reshape(-1)
-        attend_sum = attend_sum[:, :part_rows].reshape(width, width)
+        gains = jnp.sum(attend_sum[:, pack_rows : pack_rows + gain_rows], axis=0).reshape(-1)
+        attend_sum = attend_sum[:, :pack_rows].reshape(width, width)
         attendinput_grad = attend_sum[:, : 3 * head_cols].reshape(width, 3, head_cols)
         attendoutput_grad = attend_sum[:, 3 * head_cols :].T
         attendgain_grad = gains[:width]

time: 591 us -> 531 us (0.90)
  waiting for transfers between devices: 71.7 us -> 19.1 us
  Pallas kernels: 248 us -> 260 us
  matrix products: 121 us -> 110 us
  other arithmetic: 37 us -> 30.4 us
    all_gather x4 -> x1, waiting for transfers between devices: 38.1 us -> 0.01 us  [on_device(): lax.all_gather(feed_part_sum, 'seq', axis=0, tiled=True)]
    ppermute x4, waiting for transfers between devices: 32.5 us -> 0.01 us  [from_behind(): lax.ppermute(value, axis, [(source, source + steps) for source in range(i...]
    unnamed x10 -> x5, waiting for transfers between devices: 0.15 us -> 19 us
    pallas_call x10, Pallas kernels: 178 us -> 190 us  [exchange(): pl.pallas_call(body, in_specs=[pl.BlockSpec(memory_space=pltpu.VMEM)] * l...]
    dot_general x35 -> x33, matrix products: 121 us -> 110 us  [contract(): lax.dot_general(left_side, right_side, (((left_axis,), (right_axis,)), ((...]
    unnamed x202 -> x224, local copies, waits for them, and re-layouts: 49.6 us -> 49.4 us
  transfers between devices with their start and end apart: 12 -> 8, of which waited for: 6 -> 2; matrix products, arithmetic and copies ran while one was open for 26% -> 23% of each run, Pallas kernels for 37% -> 24%
where the time goes in v4:
time: 531 us; the launch traced here: 524 us
  Pallas kernels  260 us (49%)
  matrix products  110 us (21%)
  local copies, waits for them, and re-layouts  74.7 us (14%)
  other arithmetic  30.4 us (6%)
  waiting for transfers between devices  19.1 us (4%)
  between operations  17.8 us (3%)
  starting transfers between devices  12 us (2%)
    pallas_call x10, Pallas kernels, exchange(): pl.pallas_call(body, in_specs=[pl.BlockSpec(memory_space=pltpu.VMEM)] * l...  190 us
    dot_general x33, matrix products, contract(): lax.dot_general(left_side, right_side, (((left_axis,), (right_axis,)), ((...  110 us
    unnamed x224, local copies, waits for them, and re-layouts  49.4 us
    pallas_call x2, Pallas kernels, attend_backward(): pl.pallas_call(functools.partial(backward_body, *args, upright), grid=gri...  37.7 us
    pallas_call x2, Pallas kernels, attend_forward(): pl.pallas_call(functools.partial(forward_body, *args, upright), grid=grid...  31.9 us
    unnamed x5, waiting for transfers between devices  19 us
    ppermute x4, starting transfers between devices, from_behind(): lax.ppermute(value, axis, [(source, source + steps) for source in range(i...  11.9 us
  transfers between devices with their start and end apart: 8, of which 2 were waited for; matrix products, arithmetic and copies ran while one was open for 23% of the time, Pallas kernels for 24%

profile of v4, /device:TPU:0, one launch (start us, length us, event | category | flops | bytes accessed | tf_op | source)
XLA Modules:
  0.0 524.0 jit_solution(18140326150476474416)
XLA Ops:
  14.2 5.8 %collective-permute-start.1 = (bf16[1024,384]{1,0:T(8,128)(2,1)}, bf16[1024,384]{1,0:T(8,128)(2,1)}, u32[]{:S(2)}, u32[]{:S(2)}) collective-permute-start(bf16[1024,384]{1,0:T(8,128)(2,1)} %slice.166), channel_id=1, source_target_pairs={{0,4},{4,8},{8,12},{12,16},{16,20},{20,24},{24,28},{1,5},{5,9},{9,... | collective-permute-start | bytes 2359304 | tf_op jit(solution)/shard_map/byte_attend/ppermute | solution.py:26
  28.9 6.2 %copy.89 = bf16[1536,3,384]{0,2,1:T(8,128)(2,1)} copy(bf16[1536,3,384]{2,0,1:T(8,128)(2,1)} %param.33) | data formatting | bytes 7077888 | tf_op args[11]
  42.7 14.7 %attend_forward.2 = (bf16[192,1024]{1,0:T(8,128)(2,1)S(1)}, f32[1,3,1024]{2,1,0:T(4,128)S(1)}) custom-call(s32[4]{0:T(128)S(1)} %broadcast_42_counts.2.counts, s32[1,1024]{1,0:T(1,128)S(1)} %add_maximum_fusion.low, bf16[1024,192]{1,0:T(8,128)(2,1)S(1)} %slice.164.queries, bf16[2560,192]{1,0:T(8,128)(2,1)S(1)} %get-tuple-element.226.keys, ...), custom_call_target="tpu_custom_call" | custom-call | flops 11274289152 | bytes 1048576 | tf_op jit(solution)/shard_map/byte_attend/attend_forward/pallas_call | solution.py:591
  57.4 26.8 %two_gathers.1 = (bf16[768,1024]{1,0:T(8,128)(2,1)S(1)}, bf16[2048,768]{1,0:T(8,128)(2,1)S(1)}) custom-call(bf16[192,1024]{1,0:T(8,128)(2,1)S(1)} %get-tuple-element.85.block.mixed, bf16[256,768]{1,0:T(8,128)(2,1)S(1)} %convolution_convert_fusion.13.rows), custom_call_target="tpu_custom_call" | custom-call | tf_op jit(solution)/shard_map/byte_attend/two_gathers/pallas_call | solution.py:411
  88.3 3.9 multiply_reduce_fusion
  98.5 9.5 %tensor_sum.5 = bf16[256,768]{1,0:T(8,128)(2,1)S(1)} custom-call(bf16[256,768]{1,0:T(8,128)(2,1)S(1)} %convolution_convert_fusion.12.refs_0_), custom_call_target="tpu_custom_call" | custom-call | tf_op jit(solution)/shard_map/patch_rows/tensor_sum/pallas_call | solution.py:411
  108.7 21.7 %seq_gather.2 = bf16[2048,768]{1,0:T(8,128)(2,1)S(1)} custom-call(bf16[256,768]{1,0:T(8,128)(2,1)S(1)} %fusion.46.refs_0_), custom_call_target="tpu_custom_call" | custom-call | tf_op jit(solution)/shard_map/patch_rows/seq_gather/pallas_call | solution.py:411
  134.6 4.7 convolution_convert_fusion
  140.0 17.2 %attend_forward.3 = (bf16[1024,384]{1,0:T(8,128)(2,1)S(1)}, f32[3,2,1024]{2,1,0:T(2,128)S(1)}) custom-call(s32[4]{0:T(128)S(1)} %copy-done.35, s32[1,1024]{1,0:T(1,128)S(1)} %bitcast.70, bf16[1024,384]{1,0:T(8,128)(2,1)S(1)} %get-tuple-element.224.queries, bf16[1024,384]{1,0:T(8,128)(2,1)S(1)} %get-tuple-element.223.keys, ...), custom_call_target="tpu_custom_call" | custom-call | flops 12884901888 | bytes 1048576 | tf_op jit(solution)/shard_map/patch_attend/attend_forward/pallas_call | solution.py:591
  157.6 9.5 %tensor_sum.6 = bf16[128,1536]{1,0:T(8,128)(2,1)S(1)} custom-call(bf16[128,1536]{1,0:T(8,128)(2,1)S(1)} %convolution_convert_fusion.3.refs_0_), custom_call_target="tpu_custom_call" | custom-call | tf_op jit(solution)/shard_map/patch_attend/tensor_sum/pallas_call | solution.py:411
  169.2 4.1 fusion.134
  173.4 5.9 %convolution_convert_fusion.2.refs_0_ = bf16[128,1536]{1,0:T(8,128)(2,1)} fusion(bf16[1536,1536]{1,0:T(8,128)(2,1)} %param.36, f32[128,1536]{1,0:T(8,128)} %fusion.134, bf16[128,768]{1,0:T(8,128)(2,1)} %convolution_convert_fusion.16, bf16[1536,768]{1,0:T(8,128)(2,1)S(1)} %copy-done), kind=kOutput, calls=%fused_computation.65 | convolution fusion | flops 910098432 | bytes 8454144 | tf_op jit(solution)/shard_map/patch_dense/dot_general | solution.py:48
  180.2 9.4 %tensor_sum.7 = bf16[128,1536]{1,0:T(8,128)(2,1)S(1)} custom-call(bf16[128,1536]{1,0:T(8,128)(2,1)S(1)} %copy-done.24), custom_call_target="tpu_custom_call" | custom-call | tf_op jit(solution)/shard_map/patch_dense/tensor_sum/pallas_call | solution.py:411
  193.6 20.3 %seq_gather.3 = bf16[1024,1536]{1,0:T(8,128)(2,1)S(1)} custom-call(bf16[128,1536]{1,0:T(8,128)(2,1)S(1)} %fusion.60.refs_0_), custom_call_target="tpu_custom_call" | custom-call | tf_op jit(solution)/shard_map/patch_dense/seq_gather/pallas_call | solution.py:411
  222.9 19.6 %attend_backward.2 = (bf16[1024,384]{1,0:T(8,128)(2,1)S(1)}, bf16[1024,384]{1,0:T(8,128)(2,1)S(1)}, bf16[1024,384]{1,0:T(8,128)(2,1)S(1)}) custom-call(s32[4]{0:T(128)S(1)} %copy-done.36, s32[1,1024]{1,0:T(1,128)S(1)} %bitcast.71, f32[3,2,1024]{2,1,0:T(2,128)S(1)} %copy-done.39, bf16[1024,384]{1,0:T(8,128)(2,1)S(1)} %copy-done.23, ...), custom_call_target="tpu_custom_call" | custom-call | flops 16106127360 | bytes 1048576 | tf_op jit(solution)/shard_map/patch_attend_back/attend_backward/pallas_call | solution.py:612
  245.9 13.8 %tensor_sum.8 = bf16[256,1536]{1,0:T(8,128)(2,1)S(1)} custom-call(bf16[256,1536]{1,0:T(8,128)(2,1)S(1)} %convolution_convert_fusion.1.refs_0_), custom_call_target="tpu_custom_call" | custom-call | tf_op jit(solution)/shard_map/patch_attend_back/tensor_sum/pallas_call | solution.py:411
  264.9 3.9 fusion.28
  278.2 22.5 %tensor_sum.9 = bf16[1024,768]{1,0:T(8,128)(2,1)S(1)} custom-call(bf16[1024,768]{1,0:T(8,128)(2,1)S(1)} %copy-done.15), custom_call_target="tpu_custom_call" | custom-call | tf_op jit(solution)/shard_map/byte_feed_back/tensor_sum/pallas_call | solution.py:411
  303.5 4.3 copy.100
  318.4 18.1 %attend_backward.3 = (bf16[1024,192]{1,0:T(8,128)(2,1)S(1)}, bf16[2560,192]{1,0:T(8,128)(2,1)S(1)}, bf16[2560,192]{1,0:T(8,128)(2,1)S(1)}) custom-call(s32[4]{0:T(128)S(1)} %copy-done.31, s32[1,1024]{1,0:T(1,128)S(1)} %copy-done.26, f32[1,3,1024]{2,1,0:T(4,128)S(1)} %get-tuple-element.88.log_total, bf16[1024,192]{1,0:T(8,128)(2,1)S(1)} %copy-done.12, ...), custom_call_target="tpu_custom_call" | custom-call | flops 704643072 | bytes 1024 | tf_op jit(solution)/shard_map/byte_attend_back/attend_backward/pallas_call | solution.py:612
  344.1 4.9 fusion.135
  349.1 5.2 fusion.37
  354.3 6.5 %fusion.40 = f32[1536,1152]{0,1:T(8,128)} fusion(bf16[1024,1152]{1,0:T(8,128)(2,1)S(1)} %copy-done.55, bf16[1024,768]{1,0:T(8,128)(2,1)S(1)} %copy-done.62, f32[1536]{0:T(1024)S(1)} %copy-done.89, f32[1024]{0:T(1024)S(1)} %copy-done.96), kind=kOutput, calls=%fused_computation.88 | convolution fusion | flops 3630170112 | bytes 11020288 | tf_op jit(solution)/shard_map/byte_attend_back/dot_general | solution.py:48
  360.8 8.1 %multiply_convert_fusion = (bf16[1024,1536]{1,0:T(8,128)(2,1)}, f32[1024,1536]{1,0:T(8,128)}) fusion(bf16[1024,1536]{1,0:T(8,128)(2,1)S(1)} %copy-done.100, bf16[1536,1536]{1,0:T(8,128)(2,1)S(1)} %bitcast.78), kind=kOutput, calls=%fused_computation.17 | convolution fusion | flops 4845993984 | bytes 17301504 | tf_op jit(solution)/shard_map/dense_weights/dot_general | solution.py:48
  369.0 18.9 %reduce-scatter.4.cloned.1.call-done = bf16[96,1536]{1,0:T(8,128)(2,1)} async-done(((bf16[768,1536]{1,0:T(8,128)(2,1)}), bf16[96,1536]{1,0:T(8,128)(2,1)}) %reduce-scatter.4.cloned.1.call-update) | async-done | bytes 294928
  390.0 15.3 %fusion.34 = f32[1536,1536]{1,0:T(8,128)} fusion(bf16[1024,1536]{1,0:T(8,128)(2,1)} %all-gather.6.cloned.1.call-done, f32[1024,1536]{1,0:T(8,128)} %get-tuple-element.233, bf16[1024,768]{1,0:T(8,128)(2,1)} %fusion.37, bf16[1536,768]{1,0:T(8,128)(2,1)S(1)} %copy-done), kind=kOutput, calls=%fused_computation.62 | convolution fusion | flops 7279214592 | bytes 22806528 | tf_op jit(solution)/shard_map/dense_weights/dot_general | solution.py:48
  405.3 7.2 %fusion.136 = f32[1536,768]{1,0:T(8,128)} fusion(bf16[1024,1536]{1,0:T(8,128)(2,1)} %get-tuple-element.107, bf16[1024,768]{1,0:T(8,128)(2,1)} %fusion.37), kind=kOutput, calls=%fused_computation.235 | convolution fusion | flops 2415919104 | bytes 9437184 | tf_op jit(solution)/shard_map/dense_weights/dot_general | solution.py:48
  425.5 34.2 %two_sums.1 = (bf16[1024,768]{1,0:T(8,128)(2,1)S(1)}, bf16[96,768]{1,0:T(8,128)(2,1)S(1)}) custom-call(bf16[1024,768]{1,0:T(8,128)(2,1)S(1)} %convolution_convert_fusion.4.part, bf16[768,768]{1,0:T(8,128)(2,1)S(1)} %pad_maximum_fusion.4.pack), custom_call_target="tpu_custom_call" | custom-call | tf_op jit(solution)/shard_map/byte_attend_sum/two_sums/pallas_call | solution.py:411
  462.4 8.1 %copy.96 = f32[1536,3,384]{2,0,1:T(8,128)} copy(f32[1536,3,384]{0,2,1:T(8,128)} %bitcast.76) | data formatting | bytes 14155776
  470.6 4.1 add_convert_fusion.1.part
  476.2 22.4 %sum_and_gather.1 = (bf16[1024,768]{1,0:T(8,128)(2,1)S(1)}, bf16[1024,768]{1,0:T(8,128)(2,1)S(1)}) custom-call(bf16[1024,768]{1,0:T(8,128)(2,1)S(1)} %copy-done.5, bf16[128,768]{1,0:T(8,128)(2,1)S(1)} %fusion.90.block), custom_call_target="tpu_custom_call" | custom-call | tf_op jit(solution)/shard_map/result/sum_and_gather/pallas_call | solution.py:411
  507.1 4.5 fusion.126
  (343 shorter events, 124.9 us)
Async XLA Ops:
  7.2 166.2 %copy-start = (bf16[1536,768]{1,0:T(8,128)(2,1)S(1)}, bf16[1536,768]{1,0:T(8,128)(2,1)}, u32[]{:S(2)}) copy-start(bf16[1536,768]{1,0:T(8,128)(2,1)} %param.37) | copy-start | bytes 7077892
  7.2 81.1 %all-gather.4.cloned.1.call-start = ((), (), s32[]{:S(2)}) async-start(), calls=%async_computation.1 | async-start | bytes 1474560 | tf_op jit(solution)/shard_map/byte_attend/all_gather | solution.py:738
  9.8 13.9 %copy-start.97 = (s32[2,4]{1,0:T(2,128)S(1)}, s32[2,4]{1,0:T(2,128)}, u32[]{:S(2)}) copy-start(s32[2,4]{1,0:T(2,128)} %param.25) | copy-start | bytes 100
  9.8 14.1 %copy-start.83 = (s32[1024]{0:T(1024)S(1)}, s32[1024]{0:T(1024)}, u32[]{:S(2)}) copy-start(s32[1024]{0:T(1024)} %param.24) | copy-start | bytes 12292
  14.2 26.1 %collective-permute-start.1 = (bf16[1024,384]{1,0:T(8,128)(2,1)}, bf16[1024,384]{1,0:T(8,128)(2,1)}, u32[]{:S(2)}, u32[]{:S(2)}) collective-permute-start(bf16[1024,384]{1,0:T(8,128)(2,1)} %slice.166), channel_id=1, source_target_pairs={{0,4},{4,8},{8,12},{12,16},{16,20},{20,24},{24,28},{1,5},{5,9},{9,... | collective-permute-start | bytes 2359304 | tf_op jit(solution)/shard_map/byte_attend/ppermute | solution.py:26
  20.3 20.0 %collective-permute-start = (bf16[512,384]{1,0:T(8,128)(2,1)S(1)}, bf16[512,384]{1,0:T(8,128)(2,1)}, u32[]{:S(2)}, u32[]{:S(2)}) collective-permute-start(bf16[512,384]{1,0:T(8,128)(2,1)S(1)} %slice.165), channel_id=1, source_target_pairs={{0,8},{4,12},{8,16},{12,20},{16,24},{20,28},{1,9},{5,13},{9,17},{1... | collective-permute-start | bytes 1179656 | tf_op jit(solution)/shard_map/byte_attend/ppermute | solution.py:26
  23.6 253.1 %all-gather.6.cloned.1.call-start = ((), (), s32[]{:S(2)}) async-start(), calls=%async_computation.2 | async-start | bytes 3538944 | tf_op jit(solution)/shard_map/patch_dense/all_gather | solution.py:797
  28.9 13.7 %copy-start.11 = (bf16[1024,192]{1,0:T(8,128)(2,1)}, bf16[1024,192]{1,0:T(8,128)(2,1)S(1)}, u32[]{:S(2)}) copy-start(bf16[1024,192]{1,0:T(8,128)(2,1)S(1)} %slice.164.queries) | copy-start | bytes 1179652
  42.6 14.7 %copy-start.6 = (bf16[2560,192]{1,0:T(8,128)(2,1)}, bf16[2560,192]{1,0:T(8,128)(2,1)S(1)}, u32[]{:S(2)}) copy-start(bf16[2560,192]{1,0:T(8,128)(2,1)S(1)} %get-tuple-element.225.values) | copy-start | bytes 2949124
  42.6 14.7 %copy-start.7 = (bf16[2560,192]{1,0:T(8,128)(2,1)}, bf16[2560,192]{1,0:T(8,128)(2,1)S(1)}, u32[]{:S(2)}) copy-start(bf16[2560,192]{1,0:T(8,128)(2,1)S(1)} %get-tuple-element.226.keys) | copy-start | bytes 2949124
  42.6 14.7 %copy-start.30 = (s32[4]{0:T(128)}, s32[4]{0:T(128)S(1)}, u32[]{:S(2)}) copy-start(s32[4]{0:T(128)S(1)} %broadcast_42_counts.2.counts) | copy-start | bytes 52
  42.7 44.3 %copy-start.99 = (s32[128]{0:T(128)S(1)}, s32[128]{0:T(128)}, u32[]{:S(2)}) copy-start(s32[128]{0:T(128)} %dynamic_slice.26) | copy-start | bytes 1540
  92.1 15.8 %copy-start.40 = (f32[1024,768]{1,0:T(8,128)}, f32[1024,768]{1,0:T(8,128)S(1)}, u32[]{:S(2)}) copy-start(f32[1024,768]{1,0:T(8,128)S(1)} %get-tuple-element.231) | copy-start | bytes 9437188
  108.0 22.3 %copy-start.93 = (s32[1024]{0:T(1024)S(1)}, s32[1024]{0:T(1024)}, u32[]{:S(2)}) copy-start(s32[1024]{0:T(1024)} %copy-done.92) | copy-start | bytes 12292
  134.5 32.8 %copy-start.53 = (bf16[128,768]{1,0:T(8,128)(2,1)}, bf16[128,768]{1,0:T(8,128)(2,1)S(1)}, u32[]{:S(2)}) copy-start(bf16[128,768]{1,0:T(8,128)(2,1)S(1)} %constant_dynamic-slice_fusion) | copy-start | bytes 589828
  139.5 17.7 %copy-start.19 = (bf16[1024,384]{1,0:T(8,128)(2,1)}, bf16[1024,384]{1,0:T(8,128)(2,1)S(1)}, u32[]{:S(2)}) copy-start(bf16[1024,384]{1,0:T(8,128)(2,1)S(1)} %get-tuple-element.222.values) | copy-start | bytes 2359300
  139.5 17.7 %copy-start.20 = (bf16[1024,384]{1,0:T(8,128)(2,1)}, bf16[1024,384]{1,0:T(8,128)(2,1)S(1)}, u32[]{:S(2)}) copy-start(bf16[1024,384]{1,0:T(8,128)(2,1)S(1)} %get-tuple-element.223.keys) | copy-start | bytes 2359300
  139.5 17.6 %copy-start.22 = (bf16[1024,384]{1,0:T(8,128)(2,1)}, bf16[1024,384]{1,0:T(8,128)(2,1)S(1)}, u32[]{:S(2)}) copy-start(bf16[1024,384]{1,0:T(8,128)(2,1)S(1)} %get-tuple-element.224.queries) | copy-start | bytes 2359300
  139.9 17.3 %copy-start.57 = (bf16[384,1536]{1,0:T(8,128)(2,1)S(1)}, bf16[384,1536]{1,0:T(8,128)(2,1)}, u32[]{:S(2)}) copy-start(bf16[384,1536]{1,0:T(8,128)(2,1)} %param.34) | copy-start | bytes 3538948
  139.9 28.4 %copy-start.67 = (f32[1536]{0:T(1024)S(1)}, f32[1536]{0:T(1024)}, u32[]{:S(2)}) copy-start(f32[1536]{0:T(1024)} %param.35) | copy-start | bytes 18436
  189.7 25.9 %copy-start.58 = (bf16[384,1536]{1,0:T(8,128)(2,1)S(1)}, bf16[384,1536]{1,0:T(8,128)(2,1)}, u32[]{:S(2)}) copy-start(bf16[384,1536]{1,0:T(8,128)(2,1)} %param.34) | copy-start | bytes 3538948
  218.3 169.6 %reduce-scatter.4.cloned.1.call-start = ((), (), s32[]{:S(2)}) async-start(), calls=%async_computation.4 | async-start | bytes 2654208
  244.5 15.4 %copy-start.88 = (f32[1536]{0:T(1024)S(1)}, f32[1536]{0:T(1024)}, u32[]{:S(2)}) copy-start(f32[1536]{0:T(1024)} %param.32) | copy-start | bytes 18436
  245.9 15.2 %copy-start.59 = (bf16[384,1536]{1,0:T(8,128)(2,1)S(1)}, bf16[384,1536]{1,0:T(8,128)(2,1)}, u32[]{:S(2)}) copy-start(bf16[384,1536]{1,0:T(8,128)(2,1)} %param.34) | copy-start | bytes 3538948
  278.2 23.7 %copy-start.42 = (f32[1024,768]{1,0:T(8,128)S(1)}, f32[1024,768]{1,0:T(8,128)}, u32[]{:S(2)}) copy-start(f32[1024,768]{1,0:T(8,128)} %copy-done.40) | copy-start | bytes 9437188
  307.8 166.9 %all-gather.8.cloned.1.call-start = ((), (), s32[]{:S(2)}) async-start(), calls=%async_computation.3 | async-start | bytes 2654208 | tf_op jit(solution)/shard_map/result/all_gather | solution.py:943
  339.0 73.5 %collective-permute-start.2 = (bf16[1024,384]{1,0:T(8,128)(2,1)}, bf16[1024,384]{1,0:T(8,128)(2,1)}, u32[]{:S(2)}, u32[]{:S(2)}) collective-permute-start(bf16[1024,384]{1,0:T(8,128)(2,1)} %slice.146), channel_id=1, source_target_pairs={{4,0},{8,4},{12,8},{16,12},{20,16},{24,20},{28,24},{5,1},{9,5},{13... | collective-permute-start | bytes 2359304 | tf_op jit(solution)/shard_map/byte_attend_back/ppermute | solution.py:26
  340.5 72.0 %collective-permute-start.3 = (bf16[512,384]{1,0:T(8,128)(2,1)}, bf16[512,384]{1,0:T(8,128)(2,1)}, u32[]{:S(2)}, u32[]{:S(2)}) collective-permute-start(bf16[512,384]{1,0:T(8,128)(2,1)} %slice.147), channel_id=1, source_target_pairs={{8,0},{12,4},{16,8},{20,12},{24,16},{28,20},{9,1},{13,5},{17,9},{2... | collective-permute-start | bytes 1179656 | tf_op jit(solution)/shard_map/byte_attend_back/ppermute | solution.py:26
  425.5 35.4 %copy-start.50 = (bf16[1024,768]{1,0:T(8,128)(2,1)S(1)}, bf16[1024,768]{1,0:T(8,128)(2,1)}, u32[]{:S(2)}) copy-start(bf16[1024,768]{1,0:T(8,128)(2,1)} %param.22) | copy-start | bytes 4718596
  425.5 36.8 %copy-start.81 = (bf16[1536]{0:T(1024)(128)(2,1)S(1)}, bf16[1536]{0:T(1024)(128)(2,1)}, u32[]{:S(2)}) copy-start(bf16[1536]{0:T(1024)(128)(2,1)} %get-tuple-element.214) | copy-start | bytes 9220
  425.5 36.8 %copy-start.82 = (bf16[1536]{0:T(1024)(128)(2,1)S(1)}, bf16[1536]{0:T(1024)(128)(2,1)}, u32[]{:S(2)}) copy-start(bf16[1536]{0:T(1024)(128)(2,1)} %get-tuple-element.212) | copy-start | bytes 9220
  425.5 36.8 %copy-start.86 = (bf16[768]{0:T(1024)(128)(2,1)S(1)}, bf16[768]{0:T(1024)(128)(2,1)}, u32[]{:S(2)}) copy-start(bf16[768]{0:T(1024)(128)(2,1)} %get-tuple-element.208) | copy-start | bytes 4612
  (86 other events, 314.5 us)
Sparse Core Ops, SparseCore 0:
  23.8 15.9 all-gather.3
  218.4 58.3 all-gather.5
  307.9 79.9 reduce-scatter.3
  390.5 53.3 all-gather.7

commit v5 on v4

--- a/solution.py
+++ b/solution.py
@@ -626,6 +626,33 @@
         ),
         name="attend_backward",
     )(counts, low, log_total, queries, mixed, out_grads, keys, values)
+
+
+def stacked_body(parts, left, right, out):
+    stacked = contract(left[...], right[...], 0, 0)
+    cols = stacked.shape[1] // parts
+    for part in range(parts):
+        out[part] = stacked[:, part * cols : (part + 1) * cols]
+
+
+def stacked_product(left, right, parts):
+    rows, left_cols = left.shape
+    right_cols = right.shape[1]
+    block_cols = 256
+    if rows > 1024:
+        return transposed_times(left, right).reshape(left_cols, parts, right_cols // parts)
+    return pl.pallas_call(
+        functools.partial(stacked_body, parts),
+        grid=(left_cols // block_cols,),
+        in_specs=[
+            pl.BlockSpec((rows, block_cols), lambda g: (0, g)),
+            pl.BlockSpec((rows, right_cols), lambda g: (0, 0)),
+        ],
+        out_specs=pl.BlockSpec((parts, block_cols, right_cols // parts), lambda g: (0, g, 0)),
+        out_shape=jax.ShapeDtypeStruct((parts, left_cols, right_cols // parts), WIDE_TYPE),
+        compiler_params=pltpu.CompilerParams(vmem_limit_bytes=VMEM_BYTES),
+        name="stacked_product",
+    )(left, right).transpose(1, 0, 2)
 
 
 def together(*values):
@@ -833,7 +860,7 @@
         gate_grad = narrow(gelu_back(gate_pre, activated_grad))
         bytedown_grad = transposed_times(activated, feed_grad)
         byteup_grad = transposed_times(normed_two, gate_grad)
-        feed_pack = narrow(jnp.concatenate([byteup_grad, bytedown_grad], axis=1))
+        feed_pack = narrow(jnp.concatenate([byteup_grad, bytedown_grad], axis=0))
         normed_two_part = narrow(times_transposed(gate_grad, byte_up))
         feed_pack, normed_two_part, all_normed = together(feed_pack, normed_two_part, all_normed)
         feed_part_sum = lax.psum_scatter(feed_pack, "seq", scatter_dimension=0, tiled=True)
@@ -845,6 +872,8 @@
         attend_branch_grad = narrow(after_attend_grad)
         attendoutput_grad = product(mixed_heads, attend_branch_grad)
         mixed_heads_grad = narrow(times_transposed(attend_branch_grad, attend_output))
+        mixed_heads_grad, later_projected = together(mixed_heads_grad, patch_projected_grad)
+        patchinput_grad = stacked_product(normed_three, later_projected, 3)
         query_grad, key_grad, value_grad = attend_backward(
             window_counts,
             window_low,
@@ -859,12 +888,11 @@
             True,
         )
         pair_grad = jnp.concatenate([key_grad, value_grad], axis=1)
-        pair_grad, all_normed, later_slots, later_branch, later_projected = together(
-            pair_grad, all_normed, all_slots, branch_grad, patch_projected_grad
+        pair_grad, patchinput_grad = together(pair_grad, patchinput_grad)
+        query_grad, all_normed, later_slots, later_branch, feed_part_sum = together(
+            query_grad, all_normed, all_slots, branch_grad, feed_part_sum
         )
         patchoutput_grad = transposed_times(mixed_patch, later_branch)
-        patchinput_grad = transposed_times(normed_three, later_projected)
-        patchinput_grad = patchinput_grad.reshape(big_width, 3, patch_cols)
         begin_row = WIN
         returned_list = []
         for step, need_rows in enumerate(need_list):
@@ -877,9 +905,6 @@
         block_rows = min(1024, total_rows)
 
         delta_grad = compact(later_slots)
-        delta_grad, patchoutput_grad, patchinput_grad, feed_part_sum = together(
-            delta_grad, patchoutput_grad, patchinput_grad, feed_part_sum
-        )
 
         def dense_parts(first_row):
             some_normed = lax.dynamic_slice_in_dim(all_normed, first_row, block_rows, 0)
@@ -906,8 +931,8 @@
             (densedown_grad, denseup_grad), dense_act = lax.scan(dense_step, initial, starts)
             dense_act = dense_act.reshape(total_rows, -1)
 
-        returned_list, dense_act, densedown_grad, denseup_grad = together(
-            returned_list, dense_act, densedown_grad, denseup_grad
+        returned_list, dense_act, densedown_grad, denseup_grad, patchoutput_grad = together(
+            returned_list, dense_act, densedown_grad, denseup_grad, patchoutput_grad
         )
 
     with jax.named_scope("byte_attend_sum"):
@@ -915,8 +940,9 @@
         for need_rows, returned in zip(need_list, returned_list):
             own_grad = own_grad.at[tok_rows - need_rows :].add(wide(returned))
         projected_grad = jnp.concatenate([query_grad, narrow(own_grad)], axis=1)
-        attendinput_grad = transposed_times(normed, projected_grad)
-        attend_pack = narrow(jnp.concatenate([attendinput_grad, attendoutput_grad.T], axis=1))
+        attend_pack = narrow(
+            jnp.concatenate([transposed_times(projected_grad, normed), attendoutput_grad], axis=0)
+        )
         normed_part = narrow(times_transposed(projected_grad, in_matrix))
         attend_pack, normed_part = together(attend_pack, normed_part)
         pack_rows = width // seq_devices
@@ -951,14 +977,14 @@
 
     with jax.named_scope("weight_sums"):
         feed_sum = wide(feed_sum)
-        hidden = byte_up.shape[1]
-        byteup_grad = feed_sum[:, :hidden]
-        bytedown_grad = feed_sum[:, hidden:]
+        byteup_grad = feed_sum[:width]
+        bytedown_grad = feed_sum[width:]
         attend_sum = wide(attend_sum).reshape(seq_devices, -1, width)
         gains = jnp.sum(attend_sum[:, pack_rows : pack_rows + gain_rows], axis=0).reshape(-1)
         attend_sum = attend_sum[:, :pack_rows].reshape(width, width)
-        attendinput_grad = attend_sum[:, : 3 * head_cols].reshape(width, 3, head_cols)
-        attendoutput_grad = attend_sum[:, 3 * head_cols :].T
+        attendinput_grad = attend_sum[: 3 * head_cols].reshape(3, head_cols, width)
+        attendinput_grad = attendinput_grad.transpose(2, 0, 1)
+        attendoutput_grad = attend_sum[3 * head_cols :]
         attendgain_grad = gains[:width]
         bytegain_grad = gains[width : 2 * width]
         patchgain_grad = gains[2 * width : 2 * width + big_width]

time: 531 us -> 494 us (0.930)
  local copies, waits for them, and re-layouts: 74.7 us -> 47.9 us
  waiting for transfers between devices: 19.1 us -> 5.92 us
  Pallas kernels: 260 us -> 271 us
  matrix products: 110 us -> 104 us
    unnamed x5 -> x4, waiting for transfers between devices: 19 us -> 0.07 us
    unnamed x224 -> x213, local copies, waits for them, and re-layouts: 49.4 us -> 31.5 us
    pallas_call x0 -> x1, Pallas kernels: none -> 6.92 us  [stacked_product(): pl.pallas_call(functools.partial(stacked_body, parts), grid=(left_cols //...]
    dot_general x33 -> x32, matrix products: 110 us -> 104 us  [contract(): lax.dot_general(left_side, right_side, (((left_axis,), (right_axis,)), ((...]
    reduce_scatter x0 -> x1, waiting for transfers between devices: none -> 5.84 us  [on_device(): lax.psum_scatter(feed_pack, 'seq', scatter_dimension=0, tiled=True)]
  transfers between devices with their start and end apart: 8 -> 8, of which waited for: 2 -> 1; matrix products, arithmetic and copies ran while one was open for 23% -> 21% of each run, Pallas kernels for 24% -> 33%
where the time goes in v5:
time: 494 us; the launch traced here: 487 us
  Pallas kernels  271 us (55%)
  matrix products  104 us (21%)
  local copies, waits for them, and re-layouts  47.9 us (10%)
  other arithmetic  28.6 us (6%)
  between operations  17.7 us (4%)
  starting transfers between devices  11.9 us (2%)
  waiting for transfers between devices  5.92 us (1%)
    pallas_call x10, Pallas kernels, exchange(): pl.pallas_call(body, in_specs=[pl.BlockSpec(memory_space=pltpu.VMEM)] * l...  194 us
    dot_general x32, matrix products, contract(): lax.dot_general(left_side, right_side, (((left_axis,), (right_axis,)), ((...  104 us
    pallas_call x2, Pallas kernels, attend_backward(): pl.pallas_call(functools.partial(backward_body, *args, upright), grid=gri...  37.9 us
    pallas_call x2, Pallas kernels, attend_forward(): pl.pallas_call(functools.partial(forward_body, *args, upright), grid=grid...  32.1 us
    unnamed x213, local copies, waits for them, and re-layouts  31.5 us
    ppermute x4, starting transfers between devices, from_behind(): lax.ppermute(value, axis, [(source, source + steps) for source in range(i...  11.7 us
  transfers between devices with their start and end apart: 8, of which 1 were waited for; matrix products, arithmetic and copies ran while one was open for 21% of the time, Pallas kernels for 33%

profile of v5, /device:TPU:0, one launch (start us, length us, event | category | flops | bytes accessed | tf_op | source)
XLA Modules:
  0.0 487.0 jit_solution(9436141404597691041)
XLA Ops:
  14.2 5.8 %collective-permute-start.1 = (bf16[1024,384]{1,0:T(8,128)(2,1)}, bf16[1024,384]{1,0:T(8,128)(2,1)}, u32[]{:S(2)}, u32[]{:S(2)}) collective-permute-start(bf16[1024,384]{1,0:T(8,128)(2,1)} %slice.170), channel_id=1, source_target_pairs={{0,4},{4,8},{8,12},{12,16},{16,20},{20,24},{24,28},{1,5},{5,9},{9,... | collective-permute-start | bytes 2359304 | tf_op jit(solution)/shard_map/byte_attend/ppermute | solution.py:26
  28.9 6.2 %copy.42 = bf16[1536,3,384]{0,2,1:T(8,128)(2,1)} copy(bf16[1536,3,384]{2,0,1:T(8,128)(2,1)} %param.33) | data formatting | bytes 7077888 | tf_op args[11]
  42.7 14.8 %attend_forward.2 = (bf16[192,1024]{1,0:T(8,128)(2,1)S(1)}, f32[1,3,1024]{2,1,0:T(4,128)S(1)}) custom-call(s32[4]{0:T(128)S(1)} %broadcast_42_counts.2.counts, s32[1,1024]{1,0:T(1,128)S(1)} %add_maximum_fusion.low, bf16[1024,192]{1,0:T(8,128)(2,1)S(1)} %slice.168.queries, bf16[2560,192]{1,0:T(8,128)(2,1)S(1)} %get-tuple-element.144.keys, ...), custom_call_target="tpu_custom_call" | custom-call | flops 11274289152 | bytes 1048576 | tf_op jit(solution)/shard_map/byte_attend/attend_forward/pallas_call | solution.py:591
  57.6 26.8 %two_gathers.1 = (bf16[768,1024]{1,0:T(8,128)(2,1)S(1)}, bf16[2048,768]{1,0:T(8,128)(2,1)S(1)}) custom-call(bf16[192,1024]{1,0:T(8,128)(2,1)S(1)} %get-tuple-element.86.block.mixed, bf16[256,768]{1,0:T(8,128)(2,1)S(1)} %convolution_convert_fusion.14.rows), custom_call_target="tpu_custom_call" | custom-call | tf_op jit(solution)/shard_map/byte_attend/two_gathers/pallas_call | solution.py:411
  88.5 3.9 multiply_reduce_fusion
  98.8 9.5 %tensor_sum.5 = bf16[256,768]{1,0:T(8,128)(2,1)S(1)} custom-call(bf16[256,768]{1,0:T(8,128)(2,1)S(1)} %convolution_convert_fusion.13.refs_0_), custom_call_target="tpu_custom_call" | custom-call | tf_op jit(solution)/shard_map/patch_rows/tensor_sum/pallas_call | solution.py:411
  108.9 21.7 %seq_gather.2 = bf16[2048,768]{1,0:T(8,128)(2,1)S(1)} custom-call(bf16[256,768]{1,0:T(8,128)(2,1)S(1)} %fusion.43.refs_0_), custom_call_target="tpu_custom_call" | custom-call | tf_op jit(solution)/shard_map/patch_rows/seq_gather/pallas_call | solution.py:411
  130.7 3.7 fusion.36
  134.8 4.7 convolution_convert_fusion
  140.2 17.2 %attend_forward.3 = (bf16[1024,384]{1,0:T(8,128)(2,1)S(1)}, f32[3,2,1024]{2,1,0:T(2,128)S(1)}) custom-call(s32[4]{0:T(128)S(1)} %copy-done.37, s32[1,1024]{1,0:T(1,128)S(1)} %bitcast.68, bf16[1024,384]{1,0:T(8,128)(2,1)S(1)} %get-tuple-element.142.queries, bf16[1024,384]{1,0:T(8,128)(2,1)S(1)} %get-tuple-element.141.keys, ...), custom_call_target="tpu_custom_call" | custom-call | flops 12884901888 | bytes 1048576 | tf_op jit(solution)/shard_map/patch_attend/attend_forward/pallas_call | solution.py:591
  158.5 9.5 %tensor_sum.6 = bf16[128,1536]{1,0:T(8,128)(2,1)S(1)} custom-call(bf16[128,1536]{1,0:T(8,128)(2,1)S(1)} %convolution_convert_fusion.3.refs_0_), custom_call_target="tpu_custom_call" | custom-call | tf_op jit(solution)/shard_map/patch_attend/tensor_sum/pallas_call | solution.py:411
  170.2 4.1 fusion.130
  174.3 5.9 %convolution_convert_fusion.2.refs_0_ = bf16[128,1536]{1,0:T(8,128)(2,1)} fusion(bf16[1536,1536]{1,0:T(8,128)(2,1)} %param.36, f32[128,1536]{1,0:T(8,128)} %fusion.130, bf16[128,768]{1,0:T(8,128)(2,1)} %convolution_convert_fusion.16, bf16[1536,768]{1,0:T(8,128)(2,1)S(1)} %copy-done), kind=kOutput, calls=%fused_computation.65 | convolution fusion | flops 910098432 | bytes 8454144 | tf_op jit(solution)/shard_map/patch_dense/dot_general | solution.py:48
  181.2 9.4 %tensor_sum.7 = bf16[128,1536]{1,0:T(8,128)(2,1)S(1)} custom-call(bf16[128,1536]{1,0:T(8,128)(2,1)S(1)} %copy-done.26), custom_call_target="tpu_custom_call" | custom-call | tf_op jit(solution)/shard_map/patch_dense/tensor_sum/pallas_call | solution.py:411
  194.6 20.3 %seq_gather.3 = bf16[1024,1536]{1,0:T(8,128)(2,1)S(1)} custom-call(bf16[128,1536]{1,0:T(8,128)(2,1)S(1)} %fusion.57.refs_0_), custom_call_target="tpu_custom_call" | custom-call | tf_op jit(solution)/shard_map/patch_dense/seq_gather/pallas_call | solution.py:411
  222.8 19.6 %attend_backward.2 = (bf16[1024,384]{1,0:T(8,128)(2,1)S(1)}, bf16[1024,384]{1,0:T(8,128)(2,1)S(1)}, bf16[1024,384]{1,0:T(8,128)(2,1)S(1)}) custom-call(s32[4]{0:T(128)S(1)} %copy-done.38, s32[1,1024]{1,0:T(1,128)S(1)} %bitcast.69, f32[3,2,1024]{2,1,0:T(2,128)S(1)} %copy-done.41, bf16[1024,384]{1,0:T(8,128)(2,1)S(1)} %copy-done.25, ...), custom_call_target="tpu_custom_call" | custom-call | flops 16106127360 | bytes 1048576 | tf_op jit(solution)/shard_map/patch_attend_back/attend_backward/pallas_call | solution.py:612
  247.1 13.8 %tensor_sum.8 = bf16[256,1536]{1,0:T(8,128)(2,1)S(1)} custom-call(bf16[256,1536]{1,0:T(8,128)(2,1)S(1)} %convolution_convert_fusion.1.refs_0_), custom_call_target="tpu_custom_call" | custom-call | tf_op jit(solution)/shard_map/patch_attend_back/tensor_sum/pallas_call | solution.py:411
  264.8 3.9 fusion.28
  273.8 4.4 convolution_convert_fusion.5.refs_0_
  283.0 22.6 %tensor_sum.9 = bf16[1024,768]{1,0:T(8,128)(2,1)S(1)} custom-call(bf16[1024,768]{1,0:T(8,128)(2,1)S(1)} %copy-done.17), custom_call_target="tpu_custom_call" | custom-call | tf_op jit(solution)/shard_map/byte_feed_back/tensor_sum/pallas_call | solution.py:411
  311.6 6.9 %stacked_product.1 = f32[3,1536,384]{2,1,0:T(8,128)} custom-call(bf16[1024,1536]{1,0:T(8,128)(2,1)S(1)} %fusion.4.left, bf16[1024,1152]{1,0:T(8,128)(2,1)S(1)} %copy-done.2), custom_call_target="tpu_custom_call" | custom-call | tf_op jit(solution)/shard_map/byte_attend_back/stacked_product/pallas_call | solution.py:644
  318.5 18.3 %attend_backward.3 = (bf16[1024,192]{1,0:T(8,128)(2,1)S(1)}, bf16[2560,192]{1,0:T(8,128)(2,1)S(1)}, bf16[2560,192]{1,0:T(8,128)(2,1)S(1)}) custom-call(s32[4]{0:T(128)S(1)} %copy-done.33, s32[1,1024]{1,0:T(1,128)S(1)} %copy-done.28, f32[1,3,1024]{2,1,0:T(4,128)S(1)} %get-tuple-element.89.log_total, bf16[1024,192]{1,0:T(8,128)(2,1)S(1)} %copy-done.14, ...), custom_call_target="tpu_custom_call" | custom-call | flops 704643072 | bytes 1024 | tf_op jit(solution)/shard_map/byte_attend_back/attend_backward/pallas_call | solution.py:612
  343.2 5.8 %reduce-scatter.2.cloned.1.call-done = bf16[192,768]{1,0:T(8,128)(2,1)} async-done(((bf16[1536,768]{1,0:T(8,128)(2,1)}), bf16[192,768]{1,0:T(8,128)(2,1)}) %reduce-scatter.2.cloned.1.call-update) | async-done | bytes 294928 | tf_op jit(solution)/shard_map/byte_feed_back/reduce_scatter | solution.py:866
  349.1 11.4 %multiply_convert_fusion = (bf16[1024,1536]{1,0:T(8,128)(2,1)}, f32[1024,1536]{1,0:T(8,128)}) fusion(bf16[1024,1536]{1,0:T(8,128)(2,1)} %all-gather.6.cloned.1.call-done, bf16[1536,1536]{1,0:T(8,128)(2,1)} %param.36), kind=kOutput, calls=%fused_computation.17 | convolution fusion | flops 4845993984 | bytes 17301504 | tf_op jit(solution)/shard_map/dense_weights/dot_general | solution.py:48
  360.5 4.9 %fusion.37 = bf16[1024,768]{1,0:T(8,128)(2,1)} fusion(bf16[2048,768]{1,0:T(8,128)(2,1)S(1)} %copy-done.12, s32[1024]{0:T(1024)S(1)} %copy-done.94), kind=kOutput, calls=%fused_computation.74 | convolution fusion | flops 3224109056 | bytes 4722688 | tf_op jit(solution)/shard_map/dense_weights/dot_general | solution.py:48
  365.4 15.3 %fusion.34 = f32[1536,1536]{1,0:T(8,128)} fusion(bf16[1024,1536]{1,0:T(8,128)(2,1)} %all-gather.6.cloned.1.call-done, f32[1024,1536]{1,0:T(8,128)} %get-tuple-element.151, bf16[1024,768]{1,0:T(8,128)(2,1)} %fusion.37, bf16[1536,768]{1,0:T(8,128)(2,1)S(1)} %copy-done), kind=kOutput, calls=%fused_computation.62 | convolution fusion | flops 7279214592 | bytes 22806528 | tf_op jit(solution)/shard_map/dense_weights/dot_general | solution.py:48
  380.7 7.4 %fusion.131 = f32[1536,768]{1,0:T(8,128)} fusion(bf16[1024,1536]{1,0:T(8,128)(2,1)} %get-tuple-element.109, bf16[1024,768]{1,0:T(8,128)(2,1)} %fusion.37), kind=kOutput, calls=%fused_computation.230 | convolution fusion | flops 2415919104 | bytes 9437184 | tf_op jit(solution)/shard_map/dense_weights/dot_general | solution.py:48
  397.0 37.9 %two_sums.1 = (bf16[1024,768]{1,0:T(8,128)(2,1)S(1)}, bf16[96,768]{1,0:T(8,128)(2,1)S(1)}) custom-call(bf16[1024,768]{1,0:T(8,128)(2,1)S(1)} %convolution_convert_fusion.4.part, bf16[768,768]{1,0:T(8,128)(2,1)S(1)} %pad_maximum_fusion.4.pack), custom_call_target="tpu_custom_call" | custom-call | tf_op jit(solution)/shard_map/byte_attend_sum/two_sums/pallas_call | solution.py:411
  437.8 4.1 add_convert_fusion.1.part
  443.3 22.4 %sum_and_gather.1 = (bf16[1024,768]{1,0:T(8,128)(2,1)S(1)}, bf16[1024,768]{1,0:T(8,128)(2,1)S(1)}) custom-call(bf16[1024,768]{1,0:T(8,128)(2,1)S(1)} %copy-done.7, bf16[128,768]{1,0:T(8,128)(2,1)S(1)} %fusion.87.block), custom_call_target="tpu_custom_call" | custom-call | tf_op jit(solution)/shard_map/result/sum_and_gather/pallas_call | solution.py:411
  470.2 4.5 fusion.122
  476.3 3.7 fusion.31
  (325 shorter events, 98.9 us)
Async XLA Ops:
  7.2 167.1 %copy-start = (bf16[1536,768]{1,0:T(8,128)(2,1)S(1)}, bf16[1536,768]{1,0:T(8,128)(2,1)}, u32[]{:S(2)}) copy-start(bf16[1536,768]{1,0:T(8,128)(2,1)} %param.37) | copy-start | bytes 7077892
  7.2 81.3 %all-gather.4.cloned.1.call-start = ((), (), s32[]{:S(2)}) async-start(), calls=%async_computation.1 | async-start | bytes 1474560 | tf_op jit(solution)/shard_map/byte_attend/all_gather | solution.py:765
  14.2 26.1 %collective-permute-start.1 = (bf16[1024,384]{1,0:T(8,128)(2,1)}, bf16[1024,384]{1,0:T(8,128)(2,1)}, u32[]{:S(2)}, u32[]{:S(2)}) collective-permute-start(bf16[1024,384]{1,0:T(8,128)(2,1)} %slice.170), channel_id=1, source_target_pairs={{0,4},{4,8},{8,12},{12,16},{16,20},{20,24},{24,28},{1,5},{5,9},{9,... | collective-permute-start | bytes 2359304 | tf_op jit(solution)/shard_map/byte_attend/ppermute | solution.py:26
  20.3 20.1 %collective-permute-start = (bf16[512,384]{1,0:T(8,128)(2,1)S(1)}, bf16[512,384]{1,0:T(8,128)(2,1)}, u32[]{:S(2)}, u32[]{:S(2)}) collective-permute-start(bf16[512,384]{1,0:T(8,128)(2,1)S(1)} %slice.169), channel_id=1, source_target_pairs={{0,8},{4,12},{8,16},{12,20},{16,24},{20,28},{1,9},{5,13},{9,17},{1... | collective-permute-start | bytes 1179656 | tf_op jit(solution)/shard_map/byte_attend/ppermute | solution.py:26
  23.6 254.6 %all-gather.6.cloned.1.call-start = ((), (), s32[]{:S(2)}) async-start(), calls=%async_computation.2 | async-start | bytes 3538944 | tf_op jit(solution)/shard_map/patch_dense/all_gather | solution.py:824
  42.7 44.5 %copy-start.97 = (s32[128]{0:T(128)S(1)}, s32[128]{0:T(128)}, u32[]{:S(2)}) copy-start(s32[128]{0:T(128)} %dynamic_slice.26) | copy-start | bytes 1540
  92.4 15.9 %copy-start.42 = (f32[1024,768]{1,0:T(8,128)}, f32[1024,768]{1,0:T(8,128)S(1)}, u32[]{:S(2)}) copy-start(f32[1024,768]{1,0:T(8,128)S(1)} %get-tuple-element.149) | copy-start | bytes 9437188
  108.3 22.4 %copy-start.93 = (s32[1024]{0:T(1024)S(1)}, s32[1024]{0:T(1024)}, u32[]{:S(2)}) copy-start(s32[1024]{0:T(1024)} %copy-done.92) | copy-start | bytes 12292
  134.8 33.9 %copy-start.56 = (bf16[128,768]{1,0:T(8,128)(2,1)}, bf16[128,768]{1,0:T(8,128)(2,1)S(1)}, u32[]{:S(2)}) copy-start(bf16[128,768]{1,0:T(8,128)(2,1)S(1)} %constant_dynamic-slice_fusion) | copy-start | bytes 589828
  139.8 17.7 %copy-start.21 = (bf16[1024,384]{1,0:T(8,128)(2,1)}, bf16[1024,384]{1,0:T(8,128)(2,1)S(1)}, u32[]{:S(2)}) copy-start(bf16[1024,384]{1,0:T(8,128)(2,1)S(1)} %get-tuple-element.140.values) | copy-start | bytes 2359300
  139.8 17.7 %copy-start.22 = (bf16[1024,384]{1,0:T(8,128)(2,1)}, bf16[1024,384]{1,0:T(8,128)(2,1)S(1)}, u32[]{:S(2)}) copy-start(bf16[1024,384]{1,0:T(8,128)(2,1)S(1)} %get-tuple-element.141.keys) | copy-start | bytes 2359300
  139.8 17.6 %copy-start.24 = (bf16[1024,384]{1,0:T(8,128)(2,1)}, bf16[1024,384]{1,0:T(8,128)(2,1)S(1)}, u32[]{:S(2)}) copy-start(bf16[1024,384]{1,0:T(8,128)(2,1)S(1)} %get-tuple-element.142.queries) | copy-start | bytes 2359300
  140.2 17.9 %copy-start.58 = (bf16[384,1536]{1,0:T(8,128)(2,1)S(1)}, bf16[384,1536]{1,0:T(8,128)(2,1)}, u32[]{:S(2)}) copy-start(bf16[384,1536]{1,0:T(8,128)(2,1)} %param.34) | copy-start | bytes 3538948
  140.2 29.0 %copy-start.65 = (f32[1536]{0:T(1024)S(1)}, f32[1536]{0:T(1024)}, u32[]{:S(2)}) copy-start(f32[1536]{0:T(1024)} %param.35) | copy-start | bytes 18436
  190.6 24.2 %copy-start.59 = (bf16[384,1536]{1,0:T(8,128)(2,1)S(1)}, bf16[384,1536]{1,0:T(8,128)(2,1)}, u32[]{:S(2)}) copy-start(bf16[384,1536]{1,0:T(8,128)(2,1)} %param.34) | copy-start | bytes 3538948
  217.6 131.5 %reduce-scatter.2.cloned.1.call-start = ((), (), s32[]{:S(2)}) async-start(), calls=%async_computation.3 | async-start | bytes 2654208 | tf_op jit(solution)/shard_map/byte_feed_back/reduce_scatter | solution.py:866
  244.4 16.7 %copy-start.78 = (f32[1536]{0:T(1024)S(1)}, f32[1536]{0:T(1024)}, u32[]{:S(2)}) copy-start(f32[1536]{0:T(1024)} %param.32) | copy-start | bytes 18436
  247.1 15.4 %copy-start.61 = (bf16[1024,768]{1,0:T(8,128)(2,1)S(1)}, bf16[1024,768]{1,0:T(8,128)(2,1)}, u32[]{:S(2)}) copy-start(bf16[1024,768]{1,0:T(8,128)(2,1)} %param.23) | copy-start | bytes 4718596
  247.1 15.4 %copy-start.68 = (s32[1024]{0:T(1024)S(1)}, s32[1024]{0:T(1024)}, u32[]{:S(2)}) copy-start(s32[1024]{0:T(1024)} %copy-done.66) | copy-start | bytes 12292
  247.1 15.4 %copy-start.91 = (pred[1024]{0:T(1024)(128)(4,1)S(1)}, pred[1024]{0:T(1024)(128)(4,1)}, u32[]{:S(2)}) copy-start(pred[1024]{0:T(1024)(128)(4,1)} %get-tuple-element.137) | copy-start | bytes 3076
  278.2 163.7 %all-gather.8.cloned.1.call-start = ((), (), s32[]{:S(2)}) async-start(), calls=%async_computation.4 | async-start | bytes 2654208 | tf_op jit(solution)/shard_map/result/all_gather | solution.py:969
  280.9 24.8 %copy-start.44 = (f32[1024,768]{1,0:T(8,128)S(1)}, f32[1024,768]{1,0:T(8,128)}, u32[]{:S(2)}) copy-start(f32[1024,768]{1,0:T(8,128)} %copy-done.42) | copy-start | bytes 9437188
  280.9 24.8 %copy-start.72 = (f32[1024]{0:T(1024)S(1)}, f32[1024]{0:T(1024)}, u32[]{:S(2)}) copy-start(f32[1024]{0:T(1024)} %copy-done.70) | copy-start | bytes 12292
  280.9 24.8 %copy-start.81 = (f32[768]{0:T(1024)S(1)}, f32[768]{0:T(1024)}, u32[]{:S(2)}) copy-start(f32[768]{0:T(1024)} %param.29) | copy-start | bytes 9220
  339.4 51.5 %collective-permute-start.2 = (bf16[1024,384]{1,0:T(8,128)(2,1)}, bf16[1024,384]{1,0:T(8,128)(2,1)}, u32[]{:S(2)}, u32[]{:S(2)}) collective-permute-start(bf16[1024,384]{1,0:T(8,128)(2,1)} %slice.150), channel_id=1, source_target_pairs={{4,0},{8,4},{12,8},{16,12},{20,16},{24,20},{28,24},{5,1},{9,5},{13... | collective-permute-start | bytes 2359304 | tf_op jit(solution)/shard_map/byte_attend_back/ppermute | solution.py:26
  340.7 50.2 %collective-permute-start.3 = (bf16[512,384]{1,0:T(8,128)(2,1)}, bf16[512,384]{1,0:T(8,128)(2,1)}, u32[]{:S(2)}, u32[]{:S(2)}) collective-permute-start(bf16[512,384]{1,0:T(8,128)(2,1)} %slice.151), channel_id=1, source_target_pairs={{8,0},{12,4},{16,8},{20,12},{24,16},{28,20},{9,1},{13,5},{17,9},{2... | collective-permute-start | bytes 1179656 | tf_op jit(solution)/shard_map/byte_attend_back/ppermute | solution.py:26
  396.9 40.7 %copy-start.83 = (bf16[1536]{0:T(1024)(128)(2,1)S(1)}, bf16[1536]{0:T(1024)(128)(2,1)}, u32[]{:S(2)}) copy-start(bf16[1536]{0:T(1024)(128)(2,1)} %get-tuple-element.132) | copy-start | bytes 9220
  397.0 40.7 %copy-start.84 = (bf16[1536]{0:T(1024)(128)(2,1)S(1)}, bf16[1536]{0:T(1024)(128)(2,1)}, u32[]{:S(2)}) copy-start(bf16[1536]{0:T(1024)(128)(2,1)} %get-tuple-element.130) | copy-start | bytes 9220
  397.0 40.7 %copy-start.89 = (bf16[768]{0:T(1024)(128)(2,1)S(1)}, bf16[768]{0:T(1024)(128)(2,1)}, u32[]{:S(2)}) copy-start(bf16[768]{0:T(1024)(128)(2,1)} %get-tuple-element.126) | copy-start | bytes 4612
  397.0 40.7 %copy-start.76 = (f32[1024]{0:T(1024)S(1)}, f32[1024]{0:T(1024)}, u32[]{:S(2)}) copy-start(f32[1024]{0:T(1024)} %copy-done.75) | copy-start | bytes 12292
  397.0 40.8 %copy-start.57 = (f32[256,768]{1,0:T(8,128)S(1)}, f32[256,768]{1,0:T(8,128)}, u32[]{:S(2)}) copy-start(f32[256,768]{1,0:T(8,128)} %fusion.65) | copy-start | bytes 2359300
  397.0 40.8 %copy-start.69 = (s32[1024]{0:T(1024)S(1)}, s32[1024]{0:T(1024)}, u32[]{:S(2)}) copy-start(s32[1024]{0:T(1024)} %copy-done.66) | copy-start | bytes 12292
  (82 other events, 366.1 us)
Sparse Core Ops, SparseCore 0:
  23.7 15.9 all-gather.3
  217.7 58.3 all-gather.5
  280.1 68.8 reduce-scatter.1
  365.5 55.2 all-gather.7

commit v6 on v5

--- a/solution.py
+++ b/solution.py
@@ -379,7 +379,7 @@
             tensor_sum_stages(chunks, part, total, *refs[:5]),
             ring_sum_stages(count, pack, shard, *refs[5:]),
         ],
-        (0, 1, 0, 1, 1, 0, 1, 0, 1, 1, 0, 1, 0, 1),
+        (0, 1, 0, 1, 0, 1, 0, 0, 1, 0, 1, 0, 0, 1, 0, 1, 0, 0),
     )
 
 
@@ -390,7 +390,7 @@
             tensor_sum_stages(chunks, part, total, *refs[:5]),
             ring_gather_stages(count, False, block, out, *refs[5:], None, None),
         ],
-        (0, 1, 0, 1, 0, 1, 0, 1, 0, 1, 0),
+        (0, 1, 0, 0, 1, 0, 0, 1, 0, 0, 1, 0, 0, 1, 0),
     )
 
 
@@ -740,9 +740,8 @@
         stream_value = wide(stream)
         normed = narrow(rms_scale(stream_value, attend_gain))
         in_matrix = attend_input.reshape(width, 3 * head_cols)
-        projected = narrow(product(normed, in_matrix))
-        queries = projected[:, :head_cols]
-        key_value = projected[:, head_cols:]
+        key_value = narrow(product(normed, in_matrix[:, head_cols:]))
+        queries = narrow(product(normed, in_matrix[:, :head_cols]))
         need_list = []
         while sum(need_list) < WIN:
             need_list.append(min(tok_rows, WIN - sum(need_list)))
@@ -864,7 +863,7 @@
         normed_two_part = narrow(times_transposed(gate_grad, byte_up))
         feed_pack, normed_two_part, all_normed = together(feed_pack, normed_two_part, all_normed)
         feed_part_sum = lax.psum_scatter(feed_pack, "seq", scatter_dimension=0, tiled=True)
-        normed_two_grad = wide(tensor_sum(normed_two_part, 7, 4))
+        normed_two_grad = wide(tensor_sum(normed_two_part, 7, 8))
         feed_norm_grad, bytegain_grad = norm_back(after_attend, byte_gain, normed_two_grad)
         after_attend_grad = wide(feed_grad) + feed_norm_grad
 
@@ -948,7 +947,7 @@
         pack_rows = width // seq_devices
         ring_fits = pack_rows % 32 == 0
         if ring_fits:
-            normed_grad, attend_part = two_sums(normed_part, attend_pack, 8, 4)
+            normed_grad, attend_part = two_sums(normed_part, attend_pack, 8, 8)
         else:
             normed_grad = tensor_sum(normed_part, 8, 4)
             attend_part = lax.psum_scatter(attend_pack, "seq", scatter_dimension=0, tiled=True)
@@ -969,7 +968,7 @@
             narrow(result_part), lax.all_gather(feed_part_sum, "seq", axis=0, tiled=True)
         )
         if ring_fits:
-            result_sum, attend_sum = sum_and_gather(result_part, attend_block, 9, 4)
+            result_sum, attend_sum = sum_and_gather(result_part, attend_block, 9, 8)
         else:
             result_sum = tensor_sum(result_part, 9, 4)
             attend_sum = lax.all_gather(attend_block, "seq", axis=0, tiled=True)

time: 494 us -> 492 us (level)
    dot_general x32 -> x33, matrix products: 104 us -> 106 us  [contract(): lax.dot_general(left_side, right_side, (((left_axis,), (right_axis,)), ((...]
where the time goes in v6:
time: 492 us; the launch traced here: 485 us
  Pallas kernels  270 us (55%)
  matrix products  106 us (22%)
  local copies, waits for them, and re-layouts  45 us (9%)
  other arithmetic  28.5 us (6%)
  between operations  17.6 us (4%)
  starting transfers between devices  11.9 us (2%)
  waiting for transfers between devices  6.03 us (1%)
    pallas_call x10, Pallas kernels, exchange(): pl.pallas_call(body, in_specs=[pl.BlockSpec(memory_space=pltpu.VMEM)] * l...  193 us
    dot_general x33, matrix products, contract(): lax.dot_general(left_side, right_side, (((left_axis,), (right_axis,)), ((...  106 us
    pallas_call x2, Pallas kernels, attend_backward(): pl.pallas_call(functools.partial(backward_body, *args, upright), grid=gri...  37.9 us
    pallas_call x2, Pallas kernels, attend_forward(): pl.pallas_call(functools.partial(forward_body, *args, upright), grid=grid...  32.1 us
    unnamed x213, local copies, waits for them, and re-layouts  30.4 us
    ppermute x4, starting transfers between devices, from_behind(): lax.ppermute(value, axis, [(source, source + steps) for source in range(i...  11.7 us
  transfers between devices with their start and end apart: 8, of which 1 were waited for; matrix products, arithmetic and copies ran while one was open for 21% of the time, Pallas kernels for 33%

profile of v6, /device:TPU:0, one launch (start us, length us, event | category | flops | bytes accessed | tf_op | source)
XLA Modules:
  0.0 484.6 jit_solution(15107392622978418082)
XLA Ops:
  11.8 5.8 %collective-permute-start.1 = (bf16[1024,384]{1,0:T(8,128)(2,1)S(1)}, bf16[1024,384]{1,0:T(8,128)(2,1)}, u32[]{:S(2)}, u32[]{:S(2)}) collective-permute-start(bf16[1024,384]{1,0:T(8,128)(2,1)S(1)} %convolution_convert_fusion.10), channel_id=1, source_target_pairs={{0,4},{4,8},{8,12},{12,16},{16,20},{20,24},{24,28},{1,5},{5,9},{9,... | collective-permute-start | bytes 2359304 | tf_op jit(solution)/shard_map/byte_attend/ppermute | solution.py:26
  23.5 6.1 %copy.42 = bf16[1536,3,384]{0,2,1:T(8,128)(2,1)} copy(bf16[1536,3,384]{2,0,1:T(8,128)(2,1)} %param.33) | data formatting | bytes 7077888 | tf_op args[11]
  41.3 14.9 %attend_forward.2 = (bf16[192,1024]{1,0:T(8,128)(2,1)S(1)}, f32[1,3,1024]{2,1,0:T(4,128)S(1)}) custom-call(s32[4]{0:T(128)S(1)} %broadcast_42_counts.2.counts, s32[1,1024]{1,0:T(1,128)S(1)} %add_maximum_fusion.low, bf16[1024,192]{1,0:T(8,128)(2,1)S(1)} %convolution_convert_fusion.13.queries, bf16[2560,192]{1,0:T(8,128)(2,1)S(1)} %get-tuple-element.144.keys, ...), custom_call_target="tpu_custom_call" | custom-call | flops 11274289152 | bytes 1048576 | tf_op jit(solution)/shard_map/byte_attend/attend_forward/pallas_call | solution.py:591
  56.2 25.4 %two_gathers.1 = (bf16[768,1024]{1,0:T(8,128)(2,1)S(1)}, bf16[2048,768]{1,0:T(8,128)(2,1)S(1)}) custom-call(bf16[192,1024]{1,0:T(8,128)(2,1)S(1)} %get-tuple-element.86.block.mixed, bf16[256,768]{1,0:T(8,128)(2,1)S(1)} %convolution_convert_fusion.15.rows), custom_call_target="tpu_custom_call" | custom-call | tf_op jit(solution)/shard_map/byte_attend/two_gathers/pallas_call | solution.py:411
  85.7 3.9 multiply_reduce_fusion
  96.0 9.5 %tensor_sum.5 = bf16[256,768]{1,0:T(8,128)(2,1)S(1)} custom-call(bf16[256,768]{1,0:T(8,128)(2,1)S(1)} %convolution_convert_fusion.14.refs_0_), custom_call_target="tpu_custom_call" | custom-call | tf_op jit(solution)/shard_map/patch_rows/tensor_sum/pallas_call | solution.py:411
  106.1 21.7 %seq_gather.2 = bf16[2048,768]{1,0:T(8,128)(2,1)S(1)} custom-call(bf16[256,768]{1,0:T(8,128)(2,1)S(1)} %fusion.43.refs_0_), custom_call_target="tpu_custom_call" | custom-call | tf_op jit(solution)/shard_map/patch_rows/seq_gather/pallas_call | solution.py:411
  127.8 3.7 fusion.36
  132.0 4.7 convolution_convert_fusion
  137.4 17.2 %attend_forward.3 = (bf16[1024,384]{1,0:T(8,128)(2,1)S(1)}, f32[3,2,1024]{2,1,0:T(2,128)S(1)}) custom-call(s32[4]{0:T(128)S(1)} %copy-done.37, s32[1,1024]{1,0:T(1,128)S(1)} %bitcast.67, bf16[1024,384]{1,0:T(8,128)(2,1)S(1)} %get-tuple-element.142.queries, bf16[1024,384]{1,0:T(8,128)(2,1)S(1)} %get-tuple-element.141.keys, ...), custom_call_target="tpu_custom_call" | custom-call | flops 12884901888 | bytes 1048576 | tf_op jit(solution)/shard_map/patch_attend/attend_forward/pallas_call | solution.py:591
  155.6 9.5 %tensor_sum.6 = bf16[128,1536]{1,0:T(8,128)(2,1)S(1)} custom-call(bf16[128,1536]{1,0:T(8,128)(2,1)S(1)} %convolution_convert_fusion.3.refs_0_), custom_call_target="tpu_custom_call" | custom-call | tf_op jit(solution)/shard_map/patch_attend/tensor_sum/pallas_call | solution.py:411
  167.3 4.1 fusion.133
  171.5 5.9 %convolution_convert_fusion.2.refs_0_ = bf16[128,1536]{1,0:T(8,128)(2,1)} fusion(bf16[1536,1536]{1,0:T(8,128)(2,1)} %param.36, f32[128,1536]{1,0:T(8,128)} %fusion.133, bf16[128,768]{1,0:T(8,128)(2,1)} %convolution_convert_fusion.17, bf16[1536,768]{1,0:T(8,128)(2,1)S(1)} %copy-done), kind=kOutput, calls=%fused_computation.65 | convolution fusion | flops 910098432 | bytes 8454144 | tf_op jit(solution)/shard_map/patch_dense/dot_general | solution.py:48
  178.3 9.4 %tensor_sum.7 = bf16[128,1536]{1,0:T(8,128)(2,1)S(1)} custom-call(bf16[128,1536]{1,0:T(8,128)(2,1)S(1)} %copy-done.26), custom_call_target="tpu_custom_call" | custom-call | tf_op jit(solution)/shard_map/patch_dense/tensor_sum/pallas_call | solution.py:411
  191.7 20.3 %seq_gather.3 = bf16[1024,1536]{1,0:T(8,128)(2,1)S(1)} custom-call(bf16[128,1536]{1,0:T(8,128)(2,1)S(1)} %fusion.57.refs_0_), custom_call_target="tpu_custom_call" | custom-call | tf_op jit(solution)/shard_map/patch_dense/seq_gather/pallas_call | solution.py:411
  220.0 19.6 %attend_backward.2 = (bf16[1024,384]{1,0:T(8,128)(2,1)S(1)}, bf16[1024,384]{1,0:T(8,128)(2,1)S(1)}, bf16[1024,384]{1,0:T(8,128)(2,1)S(1)}) custom-call(s32[4]{0:T(128)S(1)} %copy-done.38, s32[1,1024]{1,0:T(1,128)S(1)} %bitcast.68, f32[3,2,1024]{2,1,0:T(2,128)S(1)} %copy-done.41, bf16[1024,384]{1,0:T(8,128)(2,1)S(1)} %copy-done.23, ...), custom_call_target="tpu_custom_call" | custom-call | flops 16106127360 | bytes 1048576 | tf_op jit(solution)/shard_map/patch_attend_back/attend_backward/pallas_call | solution.py:612
  244.3 13.8 %tensor_sum.8 = bf16[256,1536]{1,0:T(8,128)(2,1)S(1)} custom-call(bf16[256,1536]{1,0:T(8,128)(2,1)S(1)} %convolution_convert_fusion.1.refs_0_), custom_call_target="tpu_custom_call" | custom-call | tf_op jit(solution)/shard_map/patch_attend_back/tensor_sum/pallas_call | solution.py:411
  262.0 3.7 fusion.28
  270.8 4.4 convolution_convert_fusion.5.refs_0_
  280.0 22.5 %tensor_sum.9 = bf16[1024,768]{1,0:T(8,128)(2,1)S(1)} custom-call(bf16[1024,768]{1,0:T(8,128)(2,1)S(1)} %copy-done.15), custom_call_target="tpu_custom_call" | custom-call | tf_op jit(solution)/shard_map/byte_feed_back/tensor_sum/pallas_call | solution.py:411
  308.5 7.2 %stacked_product.1 = f32[3,1536,384]{2,1,0:T(8,128)} custom-call(bf16[1024,1536]{1,0:T(8,128)(2,1)S(1)} %fusion.4.left, bf16[1024,1152]{1,0:T(8,128)(2,1)S(1)} %copy-done.2), custom_call_target="tpu_custom_call" | custom-call | tf_op jit(solution)/shard_map/byte_attend_back/stacked_product/pallas_call | solution.py:644
  315.6 18.3 %attend_backward.3 = (bf16[1024,192]{1,0:T(8,128)(2,1)S(1)}, bf16[2560,192]{1,0:T(8,128)(2,1)S(1)}, bf16[2560,192]{1,0:T(8,128)(2,1)S(1)}) custom-call(s32[4]{0:T(128)S(1)} %copy-done.33, s32[1,1024]{1,0:T(1,128)S(1)} %copy-done.28, f32[1,3,1024]{2,1,0:T(4,128)S(1)} %get-tuple-element.89.log_total, bf16[1024,192]{1,0:T(8,128)(2,1)S(1)} %copy-done.25, ...), custom_call_target="tpu_custom_call" | custom-call | flops 704643072 | bytes 1024 | tf_op jit(solution)/shard_map/byte_attend_back/attend_backward/pallas_call | solution.py:612
  340.3 6.0 %reduce-scatter.2.cloned.1.call-done = bf16[192,768]{1,0:T(8,128)(2,1)} async-done(((bf16[1536,768]{1,0:T(8,128)(2,1)}), bf16[192,768]{1,0:T(8,128)(2,1)}) %reduce-scatter.2.cloned.1.call-update) | async-done | bytes 294928 | tf_op jit(solution)/shard_map/byte_feed_back/reduce_scatter | solution.py:865
  346.3 11.4 %multiply_convert_fusion = (bf16[1024,1536]{1,0:T(8,128)(2,1)}, f32[1024,1536]{1,0:T(8,128)}) fusion(bf16[1024,1536]{1,0:T(8,128)(2,1)} %all-gather.6.cloned.1.call-done, bf16[1536,1536]{1,0:T(8,128)(2,1)} %param.36), kind=kOutput, calls=%fused_computation.17 | convolution fusion | flops 4845993984 | bytes 17301504 | tf_op jit(solution)/shard_map/dense_weights/dot_general | solution.py:48
  357.6 4.9 %fusion.37 = bf16[1024,768]{1,0:T(8,128)(2,1)} fusion(bf16[2048,768]{1,0:T(8,128)(2,1)S(1)} %copy-done.12, s32[1024]{0:T(1024)S(1)} %copy-done.94), kind=kOutput, calls=%fused_computation.74 | convolution fusion | flops 3224109056 | bytes 4722688 | tf_op jit(solution)/shard_map/dense_weights/dot_general | solution.py:48
  362.6 15.2 %fusion.34 = f32[1536,1536]{1,0:T(8,128)} fusion(bf16[1024,1536]{1,0:T(8,128)(2,1)} %all-gather.6.cloned.1.call-done, f32[1024,1536]{1,0:T(8,128)} %get-tuple-element.151, bf16[1024,768]{1,0:T(8,128)(2,1)} %fusion.37, bf16[1536,768]{1,0:T(8,128)(2,1)S(1)} %copy-done), kind=kOutput, calls=%fused_computation.62 | convolution fusion | flops 7279214592 | bytes 22806528 | tf_op jit(solution)/shard_map/dense_weights/dot_general | solution.py:48
  377.8 7.4 %fusion.134 = f32[1536,768]{1,0:T(8,128)} fusion(bf16[1024,1536]{1,0:T(8,128)(2,1)} %get-tuple-element.109, bf16[1024,768]{1,0:T(8,128)(2,1)} %fusion.37), kind=kOutput, calls=%fused_computation.233 | convolution fusion | flops 2415919104 | bytes 9437184 | tf_op jit(solution)/shard_map/dense_weights/dot_general | solution.py:48
  394.1 38.1 %two_sums.1 = (bf16[1024,768]{1,0:T(8,128)(2,1)S(1)}, bf16[96,768]{1,0:T(8,128)(2,1)S(1)}) custom-call(bf16[1024,768]{1,0:T(8,128)(2,1)S(1)} %convolution_convert_fusion.4.part, bf16[768,768]{1,0:T(8,128)(2,1)S(1)} %pad_maximum_fusion.4.pack), custom_call_target="tpu_custom_call" | custom-call | tf_op jit(solution)/shard_map/byte_attend_sum/two_sums/pallas_call | solution.py:411
  435.1 4.1 add_convert_fusion.1.part
  440.6 22.8 %sum_and_gather.1 = (bf16[1024,768]{1,0:T(8,128)(2,1)S(1)}, bf16[1024,768]{1,0:T(8,128)(2,1)S(1)}) custom-call(bf16[1024,768]{1,0:T(8,128)(2,1)S(1)} %copy-done.7, bf16[128,768]{1,0:T(8,128)(2,1)S(1)} %fusion.87.block), custom_call_target="tpu_custom_call" | custom-call | tf_op jit(solution)/shard_map/result/sum_and_gather/pallas_call | solution.py:411
  467.9 4.5 fusion.125
  474.1 3.7 fusion.31
  (324 shorter events, 97.6 us)
Async XLA Ops:
  7.2 164.3 %copy-start = (bf16[1536,768]{1,0:T(8,128)(2,1)S(1)}, bf16[1536,768]{1,0:T(8,128)(2,1)}, u32[]{:S(2)}) copy-start(bf16[1536,768]{1,0:T(8,128)(2,1)} %param.37) | copy-start | bytes 7077892
  7.2 78.5 %all-gather.4.cloned.1.call-start = ((), (), s32[]{:S(2)}) async-start(), calls=%async_computation.1 | async-start | bytes 1474560 | tf_op jit(solution)/shard_map/byte_attend/all_gather | solution.py:764
  9.2 27.7 %copy-start.72 = (f32[1024]{0:T(1024)}, f32[1024]{0:T(1024)S(1)}, u32[]{:S(2)}) copy-start(f32[1024]{0:T(1024)S(1)} %fusion.90) | copy-start | bytes 12292
  11.8 27.2 %collective-permute-start.1 = (bf16[1024,384]{1,0:T(8,128)(2,1)S(1)}, bf16[1024,384]{1,0:T(8,128)(2,1)}, u32[]{:S(2)}, u32[]{:S(2)}) collective-permute-start(bf16[1024,384]{1,0:T(8,128)(2,1)S(1)} %convolution_convert_fusion.10), channel_id=1, source_target_pairs={{0,4},{4,8},{8,12},{12,16},{16,20},{20,24},{24,28},{1,5},{5,9},{9,... | collective-permute-start | bytes 2359304 | tf_op jit(solution)/shard_map/byte_attend/ppermute | solution.py:26
  18.4 20.5 %collective-permute-start = (bf16[512,384]{1,0:T(8,128)(2,1)}, bf16[512,384]{1,0:T(8,128)(2,1)}, u32[]{:S(2)}, u32[]{:S(2)}) collective-permute-start(bf16[512,384]{1,0:T(8,128)(2,1)} %slice.169), channel_id=1, source_target_pairs={{0,8},{4,12},{8,16},{12,20},{16,24},{20,28},{1,9},{5,13},{9,17},{1... | collective-permute-start | bytes 1179656 | tf_op jit(solution)/shard_map/byte_attend/ppermute | solution.py:26
  21.8 253.4 %all-gather.6.cloned.1.call-start = ((), (), s32[]{:S(2)}) async-start(), calls=%async_computation.2 | async-start | bytes 3538944 | tf_op jit(solution)/shard_map/patch_dense/all_gather | solution.py:823
  41.3 43.1 %copy-start.97 = (s32[128]{0:T(128)S(1)}, s32[128]{0:T(128)}, u32[]{:S(2)}) copy-start(s32[128]{0:T(128)} %dynamic_slice.26) | copy-start | bytes 1540
  89.6 15.9 %copy-start.42 = (f32[1024,768]{1,0:T(8,128)}, f32[1024,768]{1,0:T(8,128)S(1)}, u32[]{:S(2)}) copy-start(f32[1024,768]{1,0:T(8,128)S(1)} %get-tuple-element.149) | copy-start | bytes 9437188
  105.5 22.4 %copy-start.93 = (s32[1024]{0:T(1024)S(1)}, s32[1024]{0:T(1024)}, u32[]{:S(2)}) copy-start(s32[1024]{0:T(1024)} %copy-done.92) | copy-start | bytes 12292
  132.0 33.8 %copy-start.56 = (bf16[128,768]{1,0:T(8,128)(2,1)}, bf16[128,768]{1,0:T(8,128)(2,1)S(1)}, u32[]{:S(2)}) copy-start(bf16[128,768]{1,0:T(8,128)(2,1)S(1)} %constant_dynamic-slice_fusion) | copy-start | bytes 589828
  137.0 17.6 %copy-start.19 = (bf16[1024,384]{1,0:T(8,128)(2,1)}, bf16[1024,384]{1,0:T(8,128)(2,1)S(1)}, u32[]{:S(2)}) copy-start(bf16[1024,384]{1,0:T(8,128)(2,1)S(1)} %get-tuple-element.140.values) | copy-start | bytes 2359300
  137.0 17.6 %copy-start.20 = (bf16[1024,384]{1,0:T(8,128)(2,1)}, bf16[1024,384]{1,0:T(8,128)(2,1)S(1)}, u32[]{:S(2)}) copy-start(bf16[1024,384]{1,0:T(8,128)(2,1)S(1)} %get-tuple-element.141.keys) | copy-start | bytes 2359300
  137.0 17.6 %copy-start.22 = (bf16[1024,384]{1,0:T(8,128)(2,1)}, bf16[1024,384]{1,0:T(8,128)(2,1)S(1)}, u32[]{:S(2)}) copy-start(bf16[1024,384]{1,0:T(8,128)(2,1)S(1)} %get-tuple-element.142.queries) | copy-start | bytes 2359300
  137.4 17.8 %copy-start.58 = (bf16[384,1536]{1,0:T(8,128)(2,1)S(1)}, bf16[384,1536]{1,0:T(8,128)(2,1)}, u32[]{:S(2)}) copy-start(bf16[384,1536]{1,0:T(8,128)(2,1)} %param.34) | copy-start | bytes 3538948
  137.4 29.0 %copy-start.64 = (f32[1536]{0:T(1024)S(1)}, f32[1536]{0:T(1024)}, u32[]{:S(2)}) copy-start(f32[1536]{0:T(1024)} %param.35) | copy-start | bytes 18436
  187.8 24.2 %copy-start.59 = (bf16[384,1536]{1,0:T(8,128)(2,1)S(1)}, bf16[384,1536]{1,0:T(8,128)(2,1)}, u32[]{:S(2)}) copy-start(bf16[384,1536]{1,0:T(8,128)(2,1)} %param.34) | copy-start | bytes 3538948
  214.7 131.5 %reduce-scatter.2.cloned.1.call-start = ((), (), s32[]{:S(2)}) async-start(), calls=%async_computation.3 | async-start | bytes 2654208 | tf_op jit(solution)/shard_map/byte_feed_back/reduce_scatter | solution.py:865
  241.6 16.7 %copy-start.77 = (f32[1536]{0:T(1024)S(1)}, f32[1536]{0:T(1024)}, u32[]{:S(2)}) copy-start(f32[1536]{0:T(1024)} %param.32) | copy-start | bytes 18436
  244.3 15.4 %copy-start.67 = (s32[1024]{0:T(1024)S(1)}, s32[1024]{0:T(1024)}, u32[]{:S(2)}) copy-start(s32[1024]{0:T(1024)} %copy-done.65) | copy-start | bytes 12292
  244.3 15.4 %copy-start.91 = (pred[1024]{0:T(1024)(128)(4,1)S(1)}, pred[1024]{0:T(1024)(128)(4,1)}, u32[]{:S(2)}) copy-start(pred[1024]{0:T(1024)(128)(4,1)} %get-tuple-element.137) | copy-start | bytes 3076
  275.2 164.0 %all-gather.8.cloned.1.call-start = ((), (), s32[]{:S(2)}) async-start(), calls=%async_computation.4 | async-start | bytes 2654208 | tf_op jit(solution)/shard_map/result/all_gather | solution.py:968
  277.8 24.7 %copy-start.44 = (f32[1024,768]{1,0:T(8,128)S(1)}, f32[1024,768]{1,0:T(8,128)}, u32[]{:S(2)}) copy-start(f32[1024,768]{1,0:T(8,128)} %copy-done.42) | copy-start | bytes 9437188
  277.8 24.7 %copy-start.71 = (f32[1024]{0:T(1024)S(1)}, f32[1024]{0:T(1024)}, u32[]{:S(2)}) copy-start(f32[1024]{0:T(1024)} %copy-done.69) | copy-start | bytes 12292
  277.8 24.7 %copy-start.80 = (f32[768]{0:T(1024)S(1)}, f32[768]{0:T(1024)}, u32[]{:S(2)}) copy-start(f32[768]{0:T(1024)} %param.29) | copy-start | bytes 9220
  336.5 51.5 %collective-permute-start.2 = (bf16[1024,384]{1,0:T(8,128)(2,1)}, bf16[1024,384]{1,0:T(8,128)(2,1)}, u32[]{:S(2)}, u32[]{:S(2)}) collective-permute-start(bf16[1024,384]{1,0:T(8,128)(2,1)} %slice.149), channel_id=1, source_target_pairs={{4,0},{8,4},{12,8},{16,12},{20,16},{24,20},{28,24},{5,1},{9,5},{13... | collective-permute-start | bytes 2359304 | tf_op jit(solution)/shard_map/byte_attend_back/ppermute | solution.py:26
  337.8 50.2 %collective-permute-start.3 = (bf16[512,384]{1,0:T(8,128)(2,1)}, bf16[512,384]{1,0:T(8,128)(2,1)}, u32[]{:S(2)}, u32[]{:S(2)}) collective-permute-start(bf16[512,384]{1,0:T(8,128)(2,1)} %slice.150), channel_id=1, source_target_pairs={{8,0},{12,4},{16,8},{20,12},{24,16},{28,20},{9,1},{13,5},{17,9},{2... | collective-permute-start | bytes 1179656 | tf_op jit(solution)/shard_map/byte_attend_back/ppermute | solution.py:26
  394.1 40.8 %copy-start.83 = (bf16[1536]{0:T(1024)(128)(2,1)S(1)}, bf16[1536]{0:T(1024)(128)(2,1)}, u32[]{:S(2)}) copy-start(bf16[1536]{0:T(1024)(128)(2,1)} %get-tuple-element.132) | copy-start | bytes 9220
  394.1 40.8 %copy-start.84 = (bf16[1536]{0:T(1024)(128)(2,1)S(1)}, bf16[1536]{0:T(1024)(128)(2,1)}, u32[]{:S(2)}) copy-start(bf16[1536]{0:T(1024)(128)(2,1)} %get-tuple-element.130) | copy-start | bytes 9220
  394.1 40.8 %copy-start.89 = (bf16[768]{0:T(1024)(128)(2,1)S(1)}, bf16[768]{0:T(1024)(128)(2,1)}, u32[]{:S(2)}) copy-start(bf16[768]{0:T(1024)(128)(2,1)} %get-tuple-element.126) | copy-start | bytes 4612
  394.1 40.9 %copy-start.75 = (f32[1024]{0:T(1024)S(1)}, f32[1024]{0:T(1024)}, u32[]{:S(2)}) copy-start(f32[1024]{0:T(1024)} %copy-done.74) | copy-start | bytes 12292
  394.1 40.9 %copy-start.57 = (f32[256,768]{1,0:T(8,128)S(1)}, f32[256,768]{1,0:T(8,128)}, u32[]{:S(2)}) copy-start(f32[256,768]{1,0:T(8,128)} %fusion.66) | copy-start | bytes 2359300
  394.1 40.9 %copy-start.68 = (s32[1024]{0:T(1024)S(1)}, s32[1024]{0:T(1024)}, u32[]{:S(2)}) copy-start(s32[1024]{0:T(1024)} %copy-done.65) | copy-start | bytes 12292
  (82 other events, 384.1 us)
Sparse Core Ops, SparseCore 0:
  21.9 15.9 all-gather.3
  214.8 58.3 all-gather.5
  277.3 68.9 reduce-scatter.1
  362.7 55.2 all-gather.7
